TPU v7x, 32 devices: a whole 2x2x4 slice. The times are simulated.
32 devices in a mesh: seq: 4 (over z), fsdp: 4 (over y, core), replica: 2 (over x).
Axes of the slice: x: 2, y: 2, z: 4, core: 2. Of those that a mesh axis runs over, the one named last changes fastest.
Arguments:
- tokens: bfloat16 [8, 512, 1600], P(('fsdp', 'replica'), 'seq'), may hold values from -6 to 6
- cotangent: bfloat16 [8, 512, 1600], P(('fsdp', 'replica'), 'seq'), may hold values from -6 to 6
- segments: int32 [8, 512], P(('fsdp', 'replica'), 'seq'), may hold values from 0 to 3, never falling along the last dimension, each value on 1 to 256 neighbouring positions
- norm1_gain: bfloat16 [2, 1600], P(None, ('seq', 'fsdp')), may hold values from 0.099609375 to 1.8984375
- norm1_shift: bfloat16 [2, 1600], P(None, ('seq', 'fsdp')), may hold values from -3 to 3
- w_qkv: bfloat16 [2, 1600, 4800], P(None, ('seq', 'fsdp')), may hold values from -0.15625 to 0.15625
- b_query: bfloat16 [2, 1600], P(None, ('seq', 'fsdp')), may hold values from -3 to 3
- b_value: bfloat16 [2, 1600], P(None, ('seq', 'fsdp')), may hold values from -3 to 3
- w_out: bfloat16 [2, 1600, 1600], P(None, ('seq', 'fsdp')), may hold values from -1.25 to 1.25
- b_out: bfloat16 [2, 1600], P(None, ('seq', 'fsdp')), may hold values from -3 to 3
- norm2_gain: bfloat16 [2, 1600], P(None, ('seq', 'fsdp')), may hold values from 0.099609375 to 1.8984375
- norm2_shift: bfloat16 [2, 1600], P(None, ('seq', 'fsdp')), may hold values from -3 to 3
- w_up: bfloat16 [2, 1600, 6400], P(None, ('seq', 'fsdp')), may hold values from -0.15625 to 0.15625
- b_up: bfloat16 [2, 6400], P(None, ('seq', 'fsdp')), may hold values from -3 to 3
- w_down: bfloat16 [2, 6400, 1600], P(None, ('seq', 'fsdp')), may hold values from -0.109375 to 0.109375
- b_down: bfloat16 [2, 1600], P(None, ('seq', 'fsdp')), may hold values from -3 to 3
Outputs:
- output: float32 [8, 512, 1600], P(('fsdp', 'replica'), 'seq')
- grad_tokens: float32 [8, 512, 1600], P(('fsdp', 'replica'), 'seq')
- grad_norm1_gain: float32 [2, 1600], P(None, ('seq', 'fsdp'))
- grad_norm1_shift: float32 [2, 1600], P(None, ('seq', 'fsdp'))
- grad_w_qkv: float32 [2, 1600, 4800], P(None, ('seq', 'fsdp'))
- grad_b_query: float32 [2, 1600], P(None, ('seq', 'fsdp'))
- grad_b_value: float32 [2, 1600], P(None, ('seq', 'fsdp'))
- grad_w_out: float32 [2, 1600, 1600], P(None, ('seq', 'fsdp'))
- grad_b_out: float32 [2, 1600], P(None, ('seq', 'fsdp'))
- grad_norm2_gain: float32 [2, 1600], P(None, ('seq', 'fsdp'))
- grad_norm2_shift: float32 [2, 1600], P(None, ('seq', 'fsdp'))
- grad_w_up: float32 [2, 1600, 6400], P(None, ('seq', 'fsdp'))
- grad_b_up: float32 [2, 6400], P(None, ('seq', 'fsdp'))
- grad_w_down: float32 [2, 6400, 1600], P(None, ('seq', 'fsdp'))
- grad_b_down: float32 [2, 1600], P(None, ('seq', 'fsdp'))
Inputs may be any that keep to these rules, and one draw needn't show every extreme that they name: `segments`: segment numbers never fall along a sequence; each document has at most 256 tokens.
All inputs are finite; a program needn't handle non-finite values.
Results may differ from a plain program's by a relative error of at most 0.019.
Values may be sent and summed in bfloat16 or wider, within the bound.
No kernel may reach another device: no remote copies, remote signals or barrier semaphores. Data moves between devices by JAX's collectives and lax.ppermute only.
A program may use at most 448 MiB of HBM per device.

v0:
```python
import math

import jax
import jax.numpy as jnp
from jax import lax
from jax.sharding import PartitionSpec as P

HEADS = 25
HD = 64


def layer_norm(hidden, gain, shift):
    mean = jnp.mean(hidden, axis=-1, keepdims=True)
    centred = hidden - mean
    spread = jnp.mean(centred * centred, axis=-1, keepdims=True)
    return centred * lax.rsqrt(spread + 1e-05) * gain + shift


def gelu_tanh(value):
    return (
        0.5
        * value
        * (1.0 + jnp.tanh(0.7978845608028654 * (value + 0.044715 * value * value * value)))
    )


def fetch_forward(
    norm1_gain,
    norm1_shift,
    w_qkv,
    b_query,
    b_value,
    w_out,
    b_out,
    norm2_gain,
    norm2_shift,
    w_up,
    b_up,
    w_down,
    b_down,
):
    return (
        lax.all_gather(norm1_gain, ("seq", "fsdp"), axis=0, tiled=True),
        lax.all_gather(norm1_shift, ("seq", "fsdp"), axis=0, tiled=True),
        lax.all_gather(w_qkv, ("seq", "fsdp"), axis=0, tiled=True),
        lax.all_gather(b_query, ("seq", "fsdp"), axis=0, tiled=True),
        lax.all_gather(b_value, ("seq", "fsdp"), axis=0, tiled=True),
        lax.all_gather(w_out, ("seq", "fsdp"), axis=0, tiled=True),
        lax.all_gather(b_out, ("seq", "fsdp"), axis=0, tiled=True),
        lax.all_gather(norm2_gain, ("seq", "fsdp"), axis=0, tiled=True),
        lax.all_gather(norm2_shift, ("seq", "fsdp"), axis=0, tiled=True),
        lax.all_gather(w_up, ("seq", "fsdp"), axis=0, tiled=True),
        lax.all_gather(b_up, ("seq", "fsdp"), axis=0, tiled=True),
        lax.all_gather(w_down, ("seq", "fsdp"), axis=0, tiled=True),
        lax.all_gather(b_down, ("seq", "fsdp"), axis=0, tiled=True),
    )


def fetch_backward(
    norm1_gain,
    norm1_shift,
    w_qkv,
    b_query,
    b_value,
    w_out,
    b_out,
    norm2_gain,
    norm2_shift,
    w_up,
    b_up,
    w_down,
    b_down,
):
    return (
        lax.all_gather(norm1_gain, ("seq", "fsdp"), axis=0, tiled=True),
        lax.all_gather(norm1_shift, ("seq", "fsdp"), axis=0, tiled=True),
        lax.all_gather(w_qkv, ("seq", "fsdp"), axis=0, tiled=True),
        lax.all_gather(b_query, ("seq", "fsdp"), axis=0, tiled=True),
        lax.all_gather(b_value, ("seq", "fsdp"), axis=0, tiled=True),
        lax.all_gather(w_out, ("seq", "fsdp"), axis=0, tiled=True),
        lax.all_gather(b_out, ("seq", "fsdp"), axis=0, tiled=True),
        lax.all_gather(norm2_gain, ("seq", "fsdp"), axis=0, tiled=True),
        lax.all_gather(norm2_shift, ("seq", "fsdp"), axis=0, tiled=True),
        lax.all_gather(w_up, ("seq", "fsdp"), axis=0, tiled=True),
        lax.all_gather(b_up, ("seq", "fsdp"), axis=0, tiled=True),
        lax.all_gather(w_down, ("seq", "fsdp"), axis=0, tiled=True),
        lax.all_gather(b_down, ("seq", "fsdp"), axis=0, tiled=True),
    )


def masked_scores(query_heads, key_heads, allowed, scale):
    raw = (
        jnp.einsum("qhd,khd->hqk", query_heads, key_heads, preferred_element_type=jnp.float32)
        * scale
    )
    return jnp.where(allowed[None], raw, -1e30)


def forward_layer(hidden, segment, weights, scale):
    (
        norm1_gain,
        norm1_shift,
        w_qkv,
        b_query,
        b_value,
        w_out,
        b_out,
        norm2_gain,
        norm2_shift,
        w_up,
        b_up,
        w_down,
        b_down,
    ) = weights
    length = hidden.shape[0]
    width = hidden.shape[1]
    normed = layer_norm(
        hidden, norm1_gain.astype(jnp.float32), norm1_shift.astype(jnp.float32)
    ).astype(jnp.bfloat16)
    packed = jnp.dot(normed, w_qkv, preferred_element_type=jnp.float32)
    queries = (packed[:, :width] + b_query.astype(jnp.float32)).astype(jnp.bfloat16)
    keys = packed[:, width : 2 * width].astype(jnp.bfloat16)
    values = (packed[:, 2 * width :] + b_value.astype(jnp.float32)).astype(jnp.bfloat16)
    all_keys, all_values, key_segment = (
        lax.all_gather(keys, "seq", axis=0, tiled=True),
        lax.all_gather(values, "seq", axis=0, tiled=True),
        lax.all_gather(segment, "seq", axis=0, tiled=True),
    )
    total = all_keys.shape[0]
    query_pos = lax.axis_index("seq") * length + jnp.arange(length, dtype=jnp.int32)
    key_pos = jnp.arange(total, dtype=jnp.int32)
    allowed = (segment[:, None] == key_segment[None, :]) & (key_pos[None, :] <= query_pos[:, None])
    query_heads = queries.reshape(length, HEADS, HD)
    key_heads = all_keys.reshape(total, HEADS, HD)
    value_heads = all_values.reshape(total, HEADS, HD)
    scores = masked_scores(query_heads, key_heads, allowed, scale)
    top = jnp.max(scores, axis=-1, keepdims=True)
    expo = jnp.exp(scores - top)
    denom = jnp.sum(expo, axis=-1, keepdims=True)
    log_total = top + jnp.log(denom)
    probs = (expo / denom).astype(jnp.bfloat16)
    mixed = jnp.einsum("hqk,khd->qhd", probs, value_heads, preferred_element_type=jnp.float32)
    mixed = mixed.reshape(length, width).astype(jnp.bfloat16)
    middle = hidden + (
        jnp.dot(mixed, w_out, preferred_element_type=jnp.float32) + b_out.astype(jnp.float32)
    )
    normed_two = layer_norm(
        middle, norm2_gain.astype(jnp.float32), norm2_shift.astype(jnp.float32)
    ).astype(jnp.bfloat16)
    lifted = jnp.dot(normed_two, w_up, preferred_element_type=jnp.float32) + b_up.astype(
        jnp.float32
    )
    activated = gelu_tanh(lifted).astype(jnp.bfloat16)
    result = middle + (
        jnp.dot(activated, w_down, preferred_element_type=jnp.float32) + b_down.astype(jnp.float32)
    )
    saved = (
        hidden,
        normed,
        query_heads,
        key_heads,
        value_heads,
        allowed,
        log_total,
        mixed,
        middle,
        normed_two,
        lifted,
        activated,
    )
    return (result, saved)


def backward_layer(grad_out, saved, weights, scale):
    (
        hidden,
        normed,
        query_heads,
        key_heads,
        value_heads,
        allowed,
        log_total,
        mixed,
        middle,
        normed_two,
        lifted,
        activated,
    ) = saved
    (
        norm1_gain,
        norm1_shift,
        w_qkv,
        b_query,
        b_value,
        w_out,
        b_out,
        norm2_gain,
        norm2_shift,
        w_up,
        b_up,
        w_down,
        b_down,
    ) = weights
    length = hidden.shape[0]
    width = hidden.shape[1]
    total = key_heads.shape[0]
    grad_lowered = grad_out.astype(jnp.bfloat16)
    grad_activated = jnp.dot(grad_lowered, w_down.T, preferred_element_type=jnp.float32)
    gelu_pull = jax.vjp(gelu_tanh, lifted)[1]
    grad_lifted = gelu_pull(grad_activated)[0].astype(jnp.bfloat16)
    grad_normed_two = jnp.dot(grad_lifted, w_up.T, preferred_element_type=jnp.float32)
    norm_pull_two = jax.vjp(
        layer_norm, middle, norm2_gain.astype(jnp.float32), norm2_shift.astype(jnp.float32)
    )[1]
    grad_middle_norm, grad_norm2_gain, grad_norm2_shift = norm_pull_two(grad_normed_two)
    grad_w_down = jnp.dot(activated.T, grad_lowered, preferred_element_type=jnp.float32)
    grad_b_down = jnp.sum(grad_lowered.astype(jnp.float32), axis=0)
    grad_w_up = jnp.dot(normed_two.T, grad_lifted, preferred_element_type=jnp.float32)
    grad_b_up = jnp.sum(grad_lifted.astype(jnp.float32), axis=0)
    mlp_shards = (
        lax.psum_scatter(
            grad_norm2_gain.astype(jnp.bfloat16), ("seq", "fsdp"), scatter_dimension=0, tiled=True
        ).astype(jnp.float32),
        lax.psum_scatter(
            grad_norm2_shift.astype(jnp.bfloat16), ("seq", "fsdp"), scatter_dimension=0, tiled=True
        ).astype(jnp.float32),
        lax.psum_scatter(
            grad_w_up.astype(jnp.bfloat16), ("seq", "fsdp"), scatter_dimension=0, tiled=True
        ).astype(jnp.float32),
        lax.psum_scatter(
            grad_b_up.astype(jnp.bfloat16), ("seq", "fsdp"), scatter_dimension=0, tiled=True
        ).astype(jnp.float32),
        lax.psum_scatter(
            grad_w_down.astype(jnp.bfloat16), ("seq", "fsdp"), scatter_dimension=0, tiled=True
        ).astype(jnp.float32),
        lax.psum_scatter(
            grad_b_down.astype(jnp.bfloat16), ("seq", "fsdp"), scatter_dimension=0, tiled=True
        ).astype(jnp.float32),
    )
    grad_middle = grad_out + grad_middle_norm
    grad_attended = grad_middle.astype(jnp.bfloat16)
    grad_mixed = jnp.dot(grad_attended, w_out.T, preferred_element_type=jnp.float32).astype(
        jnp.bfloat16
    )
    grad_mixed = grad_mixed.reshape(length, HEADS, HD)
    scores = masked_scores(query_heads, key_heads, allowed, scale)
    probs = jnp.exp(scores - log_total)
    grad_probs = jnp.einsum(
        "qhd,khd->hqk", grad_mixed, value_heads, preferred_element_type=jnp.float32
    )
    grad_value_heads = jnp.einsum(
        "hqk,qhd->khd", probs.astype(jnp.bfloat16), grad_mixed, preferred_element_type=jnp.float32
    )
    row_dot = jnp.sum(grad_probs * probs, axis=-1, keepdims=True)
    grad_scores = (probs * (grad_probs - row_dot)).astype(jnp.bfloat16)
    grad_query = (
        jnp.einsum("hqk,khd->qhd", grad_scores, key_heads, preferred_element_type=jnp.float32)
        * scale
    )
    grad_key_heads = (
        jnp.einsum("hqk,qhd->khd", grad_scores, query_heads, preferred_element_type=jnp.float32)
        * scale
    )
    grad_keys, grad_values = (
        lax.psum_scatter(
            grad_key_heads.reshape(total, width).astype(jnp.bfloat16),
            "seq",
            scatter_dimension=0,
            tiled=True,
        ).astype(jnp.float32),
        lax.psum_scatter(
            grad_value_heads.reshape(total, width).astype(jnp.bfloat16),
            "seq",
            scatter_dimension=0,
            tiled=True,
        ).astype(jnp.float32),
    )
    grad_queries = grad_query.reshape(length, width).astype(jnp.bfloat16)
    grad_keys_low = grad_keys.astype(jnp.bfloat16)
    grad_values_low = grad_values.astype(jnp.bfloat16)
    grad_packed = jnp.concatenate([grad_queries, grad_keys_low, grad_values_low], axis=1)
    grad_normed = jnp.dot(grad_packed, w_qkv.T, preferred_element_type=jnp.float32)
    norm_pull_one = jax.vjp(
        layer_norm, hidden, norm1_gain.astype(jnp.float32), norm1_shift.astype(jnp.float32)
    )[1]
    grad_hidden_norm, grad_norm1_gain, grad_norm1_shift = norm_pull_one(grad_normed)
    grad_w_out = jnp.dot(mixed.T, grad_attended, preferred_element_type=jnp.float32)
    grad_b_out = jnp.sum(grad_attended.astype(jnp.float32), axis=0)
    grad_w_qkv = jnp.dot(normed.T, grad_packed, preferred_element_type=jnp.float32)
    grad_b_query = jnp.sum(grad_queries.astype(jnp.float32), axis=0)
    grad_b_value = jnp.sum(grad_values_low.astype(jnp.float32), axis=0)
    attn_shards = (
        lax.psum_scatter(
            grad_norm1_gain.astype(jnp.bfloat16), ("seq", "fsdp"), scatter_dimension=0, tiled=True
        ).astype(jnp.float32),
        lax.psum_scatter(
            grad_norm1_shift.astype(jnp.bfloat16), ("seq", "fsdp"), scatter_dimension=0, tiled=True
        ).astype(jnp.float32),
        lax.psum_scatter(
            grad_w_qkv.astype(jnp.bfloat16), ("seq", "fsdp"), scatter_dimension=0, tiled=True
        ).astype(jnp.float32),
        lax.psum_scatter(
            grad_b_query.astype(jnp.bfloat16), ("seq", "fsdp"), scatter_dimension=0, tiled=True
        ).astype(jnp.float32),
        lax.psum_scatter(
            grad_b_value.astype(jnp.bfloat16), ("seq", "fsdp"), scatter_dimension=0, tiled=True
        ).astype(jnp.float32),
        lax.psum_scatter(
            grad_w_out.astype(jnp.bfloat16), ("seq", "fsdp"), scatter_dimension=0, tiled=True
        ).astype(jnp.float32),
        lax.psum_scatter(
            grad_b_out.astype(jnp.bfloat16), ("seq", "fsdp"), scatter_dimension=0, tiled=True
        ).astype(jnp.float32),
    )
    return (grad_middle + grad_hidden_norm, tuple(attn_shards) + tuple(mlp_shards))


def shards(
    tokens,
    cotangent,
    segments,
    norm1_gain,
    norm1_shift,
    w_qkv,
    b_query,
    b_value,
    w_out,
    b_out,
    norm2_gain,
    norm2_shift,
    w_up,
    b_up,
    w_down,
    b_down,
):
    stacks = (
        norm1_gain,
        norm1_shift,
        w_qkv,
        b_query,
        b_value,
        w_out,
        b_out,
        norm2_gain,
        norm2_shift,
        w_up,
        b_up,
        w_down,
        b_down,
    )
    layers = w_qkv.shape[0]
    scale = 1.0 / math.sqrt(HD)
    hidden = tokens[0].astype(jnp.float32)
    segment = segments[0].astype(jnp.bfloat16)
    saved_all = []
    for layer in range(layers):
        weights = fetch_forward(*tuple((stack[layer] for stack in stacks)))
        hidden, saved = forward_layer(hidden, segment, weights, scale)
        saved_all.append(saved)
    grad_hidden = cotangent[0].astype(jnp.float32)
    shard_lists = [None] * layers
    for layer in reversed(range(layers)):
        weights = fetch_backward(*tuple((stack[layer] for stack in stacks)))
        grad_hidden, shard_lists[layer] = backward_layer(
            grad_hidden, saved_all[layer], weights, scale
        )
    stacked = [
        jnp.stack([shard_lists[layer][index] for layer in range(layers)]) for index in range(13)
    ]
    matrix_parts = (
        lax.psum_scatter(
            stacked[2].astype(jnp.bfloat16), "replica", scatter_dimension=2, tiled=True
        ).astype(jnp.float32),
        lax.psum_scatter(
            stacked[5].astype(jnp.bfloat16), "replica", scatter_dimension=2, tiled=True
        ).astype(jnp.float32),
        lax.psum_scatter(
            stacked[9].astype(jnp.bfloat16), "replica", scatter_dimension=2, tiled=True
        ).astype(jnp.float32),
        lax.psum_scatter(
            stacked[11].astype(jnp.bfloat16), "replica", scatter_dimension=2, tiled=True
        ).astype(jnp.float32),
    )
    matrices = (
        lax.all_gather(matrix_parts[0].astype(jnp.bfloat16), "replica", axis=2, tiled=True).astype(
            jnp.float32
        ),
        lax.all_gather(matrix_parts[1].astype(jnp.bfloat16), "replica", axis=2, tiled=True).astype(
            jnp.float32
        ),
        lax.all_gather(matrix_parts[2].astype(jnp.bfloat16), "replica", axis=2, tiled=True).astype(
            jnp.float32
        ),
        lax.all_gather(matrix_parts[3].astype(jnp.bfloat16), "replica", axis=2, tiled=True).astype(
            jnp.float32
        ),
    )
    smalls = lax.psum(
        (
            stacked[0],
            stacked[1],
            stacked[3],
            stacked[4],
            stacked[6],
            stacked[7],
            stacked[8],
            stacked[10],
            stacked[12],
        ),
        "replica",
    )
    return (
        hidden[None],
        grad_hidden[None],
        smalls[0],
        smalls[1],
        matrices[0],
        smalls[2],
        smalls[3],
        matrices[1],
        smalls[4],
        smalls[5],
        smalls[6],
        matrices[2],
        smalls[7],
        matrices[3],
        smalls[8],
    )


def solution(mesh):
    in_specs = (
        P(("fsdp", "replica"), "seq", None),
        P(("fsdp", "replica"), "seq", None),
        P(("fsdp", "replica"), "seq"),
        P(None, ("seq", "fsdp")),
        P(None, ("seq", "fsdp")),
        P(None, ("seq", "fsdp"), None),
        P(None, ("seq", "fsdp")),
        P(None, ("seq", "fsdp")),
        P(None, ("seq", "fsdp"), None),
        P(None, ("seq", "fsdp")),
        P(None, ("seq", "fsdp")),
        P(None, ("seq", "fsdp")),
        P(None, ("seq", "fsdp"), None),
        P(None, ("seq", "fsdp")),
        P(None, ("seq", "fsdp"), None),
        P(None, ("seq", "fsdp")),
    )
    out_specs = (
        P(("fsdp", "replica"), "seq", None),
        P(("fsdp", "replica"), "seq", None),
        P(None, ("seq", "fsdp")),
        P(None, ("seq", "fsdp")),
        P(None, ("seq", "fsdp"), None),
        P(None, ("seq", "fsdp")),
        P(None, ("seq", "fsdp")),
        P(None, ("seq", "fsdp"), None),
        P(None, ("seq", "fsdp")),
        P(None, ("seq", "fsdp")),
        P(None, ("seq", "fsdp")),
        P(None, ("seq", "fsdp"), None),
        P(None, ("seq", "fsdp")),
        P(None, ("seq", "fsdp"), None),
        P(None, ("seq", "fsdp")),
    )
    return jax.shard_map(shards, mesh=mesh, in_specs=in_specs, out_specs=out_specs, check_vma=False)
```

profile of v0, /device:TPU:0, one launch (start us, length us, event | category | flops | bytes accessed | tf_op | source)
XLA Modules:
  0.0 3199.4 jit_solution(13057229421913861689)
XLA Ops:
  29.2 89.8 %all-reduce.58.cloned.1.call-done = (bf16[6400]{0:T(1024)(128)(2,1)}, bf16[1600]{0:T(1024)(128)(2,1)}, bf16[1600]{0:T(1024)(128)(2,1)}, bf16[1600]{0:T(1024)(128...) async-done(((bf16[6400]{0:T(1024)(128)(2,1)}, ...) | async-done | bytes 73616
  120.3 157.0 %all-gather.57.cloned.1.call-done = bf16[1,1600,4800]{2,0,1:T(2,128)(2,1)} async-done(((bf16[1,100,4800]{2,0,1:T(2,128)(2,1)}), bf16[1,1600,4800]{2,0,1:T(2,128)(2,1)}) %all-gather.57.cloned.1.call-update) | async-done | bytes 15360016 | tf_op jit(solution)/shard_map/all_gather | solution.py:45
  341.2 31.1 all-gather.43.cloned.1.call-done
  377.5 84.3 %all-gather.59.cloned.1.call-done = bf16[1,1600,1600]{2,0,1:T(2,128)(2,1)} async-done(((bf16[1,100,1600]{2,0,1:T(2,128)(2,1)}), bf16[1,1600,1600]{2,0,1:T(2,128)(2,1)}) %all-gather.59.cloned.1.call-update) | async-done | bytes 5120016 | tf_op jit(solution)/shard_map/all_gather | solution.py:48
  468.3 196.7 %all-gather.61.cloned.1.call-done = bf16[1,1600,6400]{2,0,1:T(2,128)(2,1)} async-done(((bf16[1,100,6400]{2,0,1:T(2,128)(2,1)}), bf16[1,1600,6400]{2,0,1:T(2,128)(2,1)}) %all-gather.61.cloned.1.call-update) | async-done | bytes 20480016 | tf_op jit(solution)/shard_map/all_gather | solution.py:52
  685.9 90.9 %all-gather.63.cloned.1.call-done = bf16[1,6400,1600]{2,1,0:T(8,128)(2,1)} async-done(((bf16[1,400,1600]{2,1,0:T(8,128)(2,1)}), bf16[1,6400,1600]{2,1,0:T(8,128)(2,1)}) %all-gather.63.cloned.1.call-update) | async-done | bytes 20480016 | tf_op jit(solution)/shard_map/all_gather | solution.py:54
  791.2 144.5 %all-gather.65.cloned.1.call-done = bf16[1,1600,4800]{2,0,1:T(2,128)(2,1)} async-done(((bf16[1,100,4800]{2,0,1:T(2,128)(2,1)}), bf16[1,1600,4800]{2,0,1:T(2,128)(2,1)}) %all-gather.65.cloned.1.call-update) | async-done | bytes 15360016 | tf_op jit(solution)/shard_map/all_gather | solution.py:45
  958.2 33.2 %all-gather.49.cloned.1.call-done = bf16[512,1600]{0,1:T(8,128)(2,1)} async-done(((bf16[128,1600]{0,1:T(8,128)(2,1)}), bf16[512,1600]{0,1:T(8,128)(2,1)}) %all-gather.49.cloned.1.call-update) | async-done | bytes 1638416 | tf_op jit(solution)/shard_map/all_gather | solution.py:125
  998.5 31.2 all-gather.47.cloned.1.call-done
  1034.9 84.4 %all-gather.67.cloned.1.call-done = bf16[1,1600,1600]{2,0,1:T(2,128)(2,1)} async-done(((bf16[1,100,1600]{2,0,1:T(2,128)(2,1)}), bf16[1,1600,1600]{2,0,1:T(2,128)(2,1)}) %all-gather.67.cloned.1.call-update) | async-done | bytes 5120016 | tf_op jit(solution)/shard_map/all_gather | solution.py:48
  1125.9 196.6 %all-gather.69.cloned.1.call-done = bf16[1,1600,6400]{2,0,1:T(2,128)(2,1)} async-done(((bf16[1,100,6400]{2,0,1:T(2,128)(2,1)}), bf16[1,1600,6400]{2,0,1:T(2,128)(2,1)}) %all-gather.69.cloned.1.call-update) | async-done | bytes 20480016 | tf_op jit(solution)/shard_map/all_gather | solution.py:52
  1322.5 21.0 fusion.33
  1343.5 91.5 %all-gather.71.cloned.1.call-done = bf16[1,6400,1600]{2,1,0:T(8,128)(2,1)} async-done(((bf16[1,400,1600]{2,1,0:T(8,128)(2,1)}), bf16[1,6400,1600]{2,1,0:T(8,128)(2,1)}) %all-gather.71.cloned.1.call-update) | async-done | bytes 20480016 | tf_op jit(solution)/shard_map/all_gather | solution.py:54
  1517.7 37.3 %reduce-scatter.43.cloned.1.call-done = bf16[128,1600]{1,0:T(8,128)(2,1)} async-done(((bf16[512,1600]{1,0:T(8,128)(2,1)}), bf16[128,1600]{1,0:T(8,128)(2,1)}) %reduce-scatter.43.cloned.1.call-update) | async-done | bytes 409616
  1589.5 21.9 multiply_reduce_fusion.3
  1688.1 533.9 %fusion.165 = (bf16[104,6400]{1,0:T(8,128)(2,1)}, bf16[104,6400]{1,0:T(8,128)(2,1)}) fusion(bf16[1600,6400]{1,0:T(8,128)(2,1)} %convolution_convert_fusion.2, bf16[1600,6400]{1,0:T(8,128)(2,1)} %convolution_convert_fusion.3), kind=kCustom, calls=%all-reduce-scatter.7 | all-reduce-scatter fusion | flops 21299200 | bytes 43622912
  2226.6 38.7 %collective-permute-start.6 = (bf16[60,6400]{1,0:T(8,128)(2,1)}, bf16[60,6400]{1,0:T(8,128)(2,1)}, u32[]{:S(2)}, u32[]{:S(2)}) collective-permute-start(bf16[60,6400]{1,0:T(8,128)(2,1)} %slice.152), channel_id=1, source_target_pairs={{0,2},{2,4},{4,6},{6,8},{8,10},{10,12},{12,14},{14,16},{16,18},{18... | collective-permute-start | bytes 2304008
  2337.3 430.5 %fusion.164 = (bf16[104,4800]{1,0:T(8,128)(2,1)S(1)}, bf16[104,4800]{1,0:T(8,128)(2,1)S(1)}, bf16[112,1600]{1,0:T(8,128)(2,1)}, bf16[112,1600]{1,0:T(8,128)(2,1)}) fusion(bf16[1600,4800]{1,0:T(8,128)(2,1)} %convolution_convert_fusion.4, bf16[1600,4800]{1,0:T(8,128)(2,1)} %convolution_convert_fusion.5, bf16[1600,1600]{1,0:T(8,128)(2,1)} %convolution_convert_fusion.6, ...), kind=kCustom, calls=%all-reduce-scatter.6 | all-reduce-scatter fusion | flops 21708800 | bytes 43674112
  2767.9 36.0 %collective-permute-start = (bf16[60,4800]{1,0:T(8,128)(2,1)S(1)}, bf16[60,4800]{1,0:T(8,128)(2,1)S(1)}, u32[]{:S(2)}, u32[]{:S(2)}) collective-permute-start(bf16[60,4800]{1,0:T(8,128)(2,1)S(1)} %slice.148), channel_id=1, source_target_pairs={{0,2},{2,4},{4,6},{6,8},{8,10},{10,12},{12,14},{14,16},{16,18},{18... | collective-permute-start | bytes 1728008
  2926.6 55.5 %all-reduce.56.cloned.1.call-done = (bf16[1600]{0:T(1024)(128)(2,1)}, bf16[1600]{0:T(1024)(128)(2,1)}, bf16[1600]{0:T(1024)(128)(2,1)}, bf16[1600]{0:T(1024)(128...) async-done(((bf16[1600]{0:T(1024)(128)(2,1)}, ...) | async-done | bytes 80016
  2987.4 36.7 %reduce-scatter.57.cloned.1.call-done = bf16[800,800]{1,0:T(8,128)(2,1)} async-done(((bf16[1600,800]{1,0:T(8,128)(2,1)}), bf16[800,800]{1,0:T(8,128)(2,1)}) %reduce-scatter.57.cloned.1.call-update) | async-done | bytes 1280016
  3057.8 21.3 all_gather.150
  3100.9 33.1 %all-gather.51.cloned.1.call-done = bf16[2,100,4800]{1,0,2:T(2,128)(2,1)} async-done(((bf16[2,100,2400]{1,0,2:T(2,128)(2,1)}), bf16[2,100,4800]{1,0,2:T(2,128)(2,1)}) %all-gather.51.cloned.1.call-update) | async-done | bytes 1920016 | tf_op jit(solution)/shard_map/all_gather | solution.py:385
  3143.4 39.0 %all-gather.55.cloned.1.call-done = bf16[2,400,1600]{1,0,2:T(2,128)(2,1)} async-done(((bf16[2,400,800]{1,0,2:T(2,128)(2,1)}), bf16[2,400,1600]{1,0,2:T(2,128)(2,1)}) %all-gather.55.cloned.1.call-update) | async-done | bytes 2560016 | tf_op jit(solution)/shard_map/all_gather | solution.py:394
  (546 shorter events, 643.1 us)
Async XLA Ops:
  7.2 111.8 %all-reduce.58.cloned.1.call-start = ((), (), s32[]{:S(2)}) async-start(), calls=%async_computation.36 | async-start | bytes 180224
  22.0 255.3 %all-gather.57.cloned.1.call-start = ((), (), s32[]{:S(2)}) async-start(), calls=%async_computation.19 | async-start | bytes 33075200 | tf_op jit(solution)/shard_map/all_gather | solution.py:45
  28.6 305.3 %all-gather.45.cloned.1.call-start = ((), (), s32[]{:S(2)}) async-start(), calls=%async_computation.11 | async-start | bytes 2048000 | tf_op jit(solution)/shard_map/all_gather | solution.py:125
  298.3 163.4 %all-gather.59.cloned.1.call-start = ((), (), s32[]{:S(2)}) async-start(), calls=%async_computation.20 | async-start | bytes 11315200 | tf_op jit(solution)/shard_map/all_gather | solution.py:48
  302.1 362.8 %all-gather.61.cloned.1.call-start = ((), (), s32[]{:S(2)}) async-start(), calls=%async_computation.21 | async-start | bytes 43520000 | tf_op jit(solution)/shard_map/all_gather | solution.py:52
  307.3 469.6 %all-gather.63.cloned.1.call-start = ((), (), s32[]{:S(2)}) async-start(), calls=%async_computation.22 | async-start | bytes 22630400 | tf_op jit(solution)/shard_map/all_gather | solution.py:54
  310.8 624.9 %all-gather.65.cloned.1.call-start = ((), (), s32[]{:S(2)}) async-start(), calls=%async_computation.23 | async-start | bytes 33075200 | tf_op jit(solution)/shard_map/all_gather | solution.py:45
  311.5 679.8 %all-gather.49.cloned.1.call-start = ((), (), s32[]{:S(2)}) async-start(), calls=%async_computation.13 | async-start | bytes 2048000 | tf_op jit(solution)/shard_map/all_gather | solution.py:125
  955.8 163.5 %all-gather.67.cloned.1.call-start = ((), (), s32[]{:S(2)}) async-start(), calls=%async_computation.24 | async-start | bytes 11315200 | tf_op jit(solution)/shard_map/all_gather | solution.py:48
  956.5 366.0 %all-gather.69.cloned.1.call-start = ((), (), s32[]{:S(2)}) async-start(), calls=%async_computation.25 | async-start | bytes 43520000 | tf_op jit(solution)/shard_map/all_gather | solution.py:52
  957.1 477.9 %all-gather.71.cloned.1.call-start = ((), (), s32[]{:S(2)}) async-start(), calls=%async_computation.26 | async-start | bytes 22630400 | tf_op jit(solution)/shard_map/all_gather | solution.py:54
  957.8 558.6 %reduce-scatter.45.cloned.1.call-start = ((), (), s32[]{:S(2)}) async-start(), calls=%async_computation.28 | async-start | bytes 2129920
  1493.7 831.9 %reduce-scatter.49.cloned.1.call-start = ((), (), s32[]{:S(2)}) async-start(), calls=%async_computation.30 | async-start | bytes 2129920
  1622.7 704.2 %reduce-scatter.47.cloned.1.call-start = ((), (), s32[]{:S(2)}) async-start(), calls=%async_computation.29 | async-start | bytes 2129920
  1637.6 1225.9 %reduce-scatter.41.cloned.1.call-start = ((), (), s32[]{:S(2)}) async-start(), calls=%async_computation.17 | async-start | bytes 22630400 | tf_op jit(solution)/shard_map/reduce_scatter | solution.py:233
  1649.4 1214.1 %reduce-scatter.39.cloned.1.call-start = ((), (), s32[]{:S(2)}) async-start(), calls=%async_computation.16 | async-start | bytes 22630400 | tf_op jit(solution)/shard_map/reduce_scatter | solution.py:233
  1661.3 1247.8 %reduce-scatter.55.cloned.1.call-start = ((), (), s32[]{:S(2)}) async-start(), calls=%async_computation.33 | async-start | bytes 4915200
  2325.5 594.5 %reduce-scatter.51.cloned.1.call-start = ((), (), s32[]{:S(2)}) async-start(), calls=%async_computation.31 | async-start | bytes 3686400
  2841.7 140.4 %all-reduce.56.cloned.1.call-start = ((), (), s32[]{:S(2)}) async-start(), calls=%async_computation.35 | async-start | bytes 196608
  2863.4 160.7 %reduce-scatter.57.cloned.1.call-start = ((), (), s32[]{:S(2)}) async-start(), calls=%async_computation.34 | async-start | bytes 4300800
  2879.2 177.3 %reduce-scatter.53.cloned.1.call-start = ((), (), s32[]{:S(2)}) async-start(), calls=%async_computation.32 | async-start | bytes 1228800
  2908.9 186.0 %all-gather.53.cloned.1.call-start = ((), (), s32[]{:S(2)}) async-start(), calls=%async_computation.15 | async-start | bytes 3993600 | tf_op jit(solution)/shard_map/all_gather | solution.py:391
  2919.9 214.2 %all-gather.51.cloned.1.call-start = ((), (), s32[]{:S(2)}) async-start(), calls=%async_computation.14 | async-start | bytes 3686400 | tf_op jit(solution)/shard_map/all_gather | solution.py:385
  2924.0 258.4 %all-gather.55.cloned.1.call-start = ((), (), s32[]{:S(2)}) async-start(), calls=%async_computation.18 | async-start | bytes 4915200 | tf_op jit(solution)/shard_map/all_gather | solution.py:394
  (134 other events, 6390.6 us)
Sparse Core Ops, SparseCore 0:
  22.1 96.7 all-reduce.57
  121.1 156.1 all-gather.56
  295.1 38.7 all-gather.44
  335.3 36.9 all-gather.42
  374.9 86.7 all-gather.58
  463.7 201.1 all-gather.60
  666.5 110.2 all-gather.62
  779.0 156.5 all-gather.64
  952.6 38.7 all-gather.48
  992.8 36.9 all-gather.46
  1032.5 86.7 all-gather.66
  1121.3 201.1 all-gather.68
  1324.7 110.2 all-gather.70
  1479.0 37.4 reduce-scatter.44
  1518.6 36.3 reduce-scatter.42
  1701.7 336.3 reduce-scatter.40
  2042.2 280.8 reduce-scatter.38
  2325.8 45.0 reduce-scatter.54
  2841.9 36.9 reduce-scatter.50
  2885.5 96.5 all-reduce.55
  2985.0 39.0 reduce-scatter.56
  3046.6 48.2 all-gather.52
  3096.8 37.1 all-gather.50
  3136.0 46.3 all-gather.54
  (3 shorter events, 90.8 us)
where the time goes:
time: 3220 us; the launch traced here: 3200 us
  waiting for transfers between devices  1480 us (46%)
  blocking collectives  1000 us (31%)
  matrix products  334 us (10%)
  local copies, waits for them, and re-layouts  218 us (7%)
  starting transfers between devices  102 us (3%)
  other arithmetic  38.5 us (1%)
    unnamed x2, blocking collectives  964 us
    all_gather x2, waiting for transfers between devices, fetch_forward(): lax.all_gather(w_up, ('seq', 'fsdp'), axis=0, tiled=True)  393 us
    all_gather x2, waiting for transfers between devices, fetch_forward(): lax.all_gather(w_qkv, ('seq', 'fsdp'), axis=0, tiled=True)  301 us
    unnamed x45, waiting for transfers between devices  244 us
    unnamed x330, local copies, waits for them, and re-layouts  187 us
    all_gather x2, waiting for transfers between devices, fetch_forward(): lax.all_gather(w_down, ('seq', 'fsdp'), axis=0, tiled=True)  182 us
    all_gather x2, waiting for transfers between devices, fetch_forward(): lax.all_gather(w_out, ('seq', 'fsdp'), axis=0, tiled=True)  169 us
    unnamed x18, starting transfers between devices  101 us
  transfers between devices with their start and end apart: 35, of which 22 were waited for; matrix products, arithmetic and copies ran while one was open for 43% of the time, Pallas kernels for 0%

commit v1 on v0

v1 whole, which is shorter than its diff:
```python
import functools
import math

import jax
import jax.numpy as jnp
from jax import lax
from jax.sharding import PartitionSpec as P

HEADS = 25
HD = 64
BF = jnp.bfloat16
F32 = jnp.float32
ALL = ("seq", "fsdp", "replica")
GROUP = ("fsdp", "replica")
OWNERS = ("seq", "fsdp")


def dot(a, b, ca, cb):
    return lax.dot_general(a, b, (((ca,), (cb,)), ((), ())), preferred_element_type=F32)


def norm_parts(v):
    mean = jnp.mean(v, axis=-1, keepdims=True)
    centred = v - mean
    spread = jnp.mean(centred * centred, axis=-1, keepdims=True)
    inv = lax.rsqrt(spread + 1e-05)
    return centred * inv, inv


def norm_pull(grad, unit, inv, gain):
    scaled = grad * gain
    first = jnp.mean(scaled, axis=-1, keepdims=True)
    second = jnp.mean(scaled * unit, axis=-1, keepdims=True)
    return inv * (scaled - first - unit * second)


def gelu_tanh(value):
    return (
        0.5
        * value
        * (1.0 + jnp.tanh(0.7978845608028654 * (value + 0.044715 * value * value * value)))
    )


def gelu_slope(value):
    inner = 0.7978845608028654 * (value + 0.044715 * value * value * value)
    tanh = jnp.tanh(inner)
    slope = 0.7978845608028654 * (1.0 + 3.0 * 0.044715 * value * value)
    return 0.5 * (1.0 + tanh) + 0.5 * value * (1.0 - tanh * tanh) * slope


class Plan:
    def __init__(self, mesh):
        self.nz = mesh.shape["seq"]
        self.nf = mesh.shape["fsdp"]
        self.nr = mesh.shape["replica"]
        self.group = self.nf * self.nr
        self.cube = self.nf == 4 and self.nr == 2
        self.heads = 2 * -(-HEADS // (2 * self.group))

    def rank_of(self, f, r):
        half = self.group // 2
        if self.nf % 2:
            return f * self.nr + r
        return (f % 2) * half + (f // 2) * self.nr + r

    def rank(self):
        return self.rank_of(lax.axis_index("fsdp"), lax.axis_index("replica"))

    def order(self):
        members = [(self.rank_of(f, r), f * self.nr + r) for f in range(self.nf) for r in range(self.nr)]
        return [member for _, member in sorted(members)]

    def regroup(self, v):
        place = {}
        for f in range(self.nf):
            for r in range(self.nr):
                place[self.rank_of(f, r)] = f * self.nr + r
        pairs = []
        for z in range(self.nz):
            for g in range(self.group):
                slot = (g // self.nz) * self.nz + z
                pairs.append((z * self.group + place[g], (g % self.nz) * self.group + place[slot]))
        return lax.ppermute(v, ALL, pairs)

    def swap_core(self, v):
        return lax.ppermute(v, "fsdp", [(f, f ^ 1) for f in range(self.nf)])

    def swap_y(self, v):
        return lax.ppermute(v, "fsdp", [(f, f ^ 2) for f in range(self.nf)])

    def swap_x(self, v):
        return lax.ppermute(v, "replica", [(r, r ^ 1) for r in range(self.nr)])

    def swap_xy(self, v):
        pairs = [
            (f * self.nr + r, (f ^ 2) * self.nr + (r ^ 1))
            for f in range(self.nf)
            for r in range(self.nr)
        ]
        return lax.ppermute(v, GROUP, pairs)

    def bits(self):
        f = lax.axis_index("fsdp")
        return f % 2, f // 2, lax.axis_index("replica")

    def gather_rows(self, v):
        if not self.cube:
            full = lax.all_gather(v, GROUP, axis=0, tiled=False)
            return full[jnp.array(self.order())].reshape(-1, v.shape[1])
        half = v.shape[0] // 2
        if v.shape[0] % 32:
            from_x = self.swap_x(v)
            four = jnp.concatenate([v, from_x, self.swap_y(jnp.concatenate([v, from_x]))])
        else:
            from_x = self.swap_x(v)
            from_y = self.swap_y(v)
            corner_a = self.swap_y(from_x[:half])
            corner_b = self.swap_x(from_y[half:])
            four = jnp.concatenate([v, from_x, from_y, corner_a, corner_b])
        return jnp.concatenate([four, self.swap_core(four)])

    def scatter_rows(self, v):
        rows = v.shape[0] // self.group
        if not self.cube:
            blocks = v.astype(BF).reshape(self.group, rows, -1)
            back = [0] * self.group
            for rank, member in enumerate(self.order()):
                back[member] = rank
            blocks = blocks[jnp.array(back)].reshape(v.shape)
            return lax.psum_scatter(blocks, GROUP, scatter_dimension=0, tiled=True).astype(F32)
        half = rows // 2
        mine, other = v[: 4 * rows], v[4 * rows :]
        four = mine + self.swap_core(other.astype(BF)).astype(F32)
        own, to_x, to_y, corner = (four[i * rows : (i + 1) * rows] for i in range(4))
        corner = corner.astype(BF)
        add_x = self.swap_y(corner[:half]).astype(F32)
        add_y = self.swap_x(corner[half:]).astype(F32)
        to_x = jnp.concatenate([to_x[:half] + add_x, to_x[half:]]).astype(BF)
        to_y = jnp.concatenate([to_y[:half], to_y[half:] + add_y]).astype(BF)
        return own + self.swap_x(to_x).astype(F32) + self.swap_y(to_y).astype(F32)

    def working_to_rank(self, v, axis):
        if not self.cube:
            return v
        core, y, x = self.bits()
        shape = v.shape
        v = v.reshape(shape[:axis] + (2, 2, 2) + shape[axis + 1 :])
        v = jnp.where(core == 1, jnp.flip(v, axis), v)
        v = jnp.where(y == 1, jnp.flip(v, axis + 1), v)
        v = jnp.where(x == 1, jnp.flip(v, axis + 2), v)
        return v.reshape(shape)

    def exchange(self, v):
        if not self.cube:
            back = [0] * self.group
            for rank, member in enumerate(self.order()):
                back[member] = rank
            v = lax.all_to_all(v[jnp.array(back)], GROUP, split_axis=0, concat_axis=0, tiled=True)
            return v[jnp.array(self.order())]
        near = v[:4]
        far = self.swap_core(v[4:])
        both = jnp.stack([near, far])
        own = both[:, 0]
        from_x = self.swap_x(both[:, 1])
        from_y = self.swap_y(both[:, 2])
        from_xy = self.swap_xy(both[:, 3])
        return jnp.stack([own, from_x, from_y, from_xy], axis=1).reshape(v.shape)

    def exchange_fsdp(self, v):
        if not self.cube:
            return lax.all_to_all(v, "fsdp", split_axis=0, concat_axis=0, tiled=True)
        core, y, _ = self.bits()
        shape = v.shape

        def flips(u):
            u = u.reshape((2, 2) + shape[1:])
            u = jnp.where(y == 1, jnp.flip(u, 0), u)
            u = jnp.where(core == 1, jnp.flip(u, 1), u)
            return u

        v = flips(v)
        other = self.swap_core(v[:, 1])
        both = jnp.stack([v[:, 0], other], axis=1)
        far = self.swap_y(both[1])
        return flips(jnp.stack([both[0], far])).reshape(shape)

    def gather_replica(self, v, axis):
        if self.nr != 2:
            return lax.all_gather(v, "replica", axis=axis, tiled=True)
        x = lax.axis_index("replica")
        other = self.swap_x(v)
        return jnp.concatenate(
            [jnp.where(x == 0, v, other), jnp.where(x == 0, other, v)], axis=axis
        )


def gather_seq(v):
    return lax.all_gather(v, "seq", axis=0, tiled=True)


def scatter_seq(v):
    return lax.psum_scatter(v, "seq", scatter_dimension=0, tiled=True)


def heads_of(v, plan, total):
    return v.reshape(-1, total, plan.heads, HD)


def attend(packed, codes, plan, total, scale):
    width = plan.heads * HD
    q, k, v = (heads_of(packed[:, i * width : (i + 1) * width], plan, total) for i in range(3))
    code = codes.reshape(-1, total)
    low = (code // 65536) * 65536
    allowed = (code[:, None, :] <= code[:, :, None]) & (code[:, None, :] >= low[:, :, None])
    scores = jnp.einsum("sqhd,skhd->shqk", q, k, preferred_element_type=F32) * scale
    scores = jnp.where(allowed[:, None], scores, -1e30)
    top = jnp.max(scores, axis=-1, keepdims=True)
    expo = jnp.exp(scores - top)
    denom = jnp.sum(expo, axis=-1, keepdims=True)
    lse = top + jnp.log(denom)
    probs = (expo / denom).astype(BF)
    mixed = jnp.einsum("shqk,skhd->sqhd", probs, v, preferred_element_type=F32)
    return mixed.reshape(-1, width).astype(BF), lse


def attend_back(packed, codes, lse, g_mixed, plan, total, scale):
    width = plan.heads * HD
    q, k, v = (heads_of(packed[:, i * width : (i + 1) * width], plan, total) for i in range(3))
    gm = heads_of(g_mixed, plan, total)
    code = codes.reshape(-1, total)
    low = (code // 65536) * 65536
    allowed = (code[:, None, :] <= code[:, :, None]) & (code[:, None, :] >= low[:, :, None])
    scores = jnp.einsum("sqhd,skhd->shqk", q, k, preferred_element_type=F32) * scale
    probs = jnp.exp(jnp.where(allowed[:, None], scores, -1e30) - lse)
    g_probs = jnp.einsum("sqhd,skhd->shqk", gm, v, preferred_element_type=F32)
    g_v = jnp.einsum("shqk,sqhd->skhd", probs.astype(BF), gm, preferred_element_type=F32)
    row = jnp.sum(g_probs * probs, axis=-1, keepdims=True)
    g_s = (probs * (g_probs - row)).astype(BF)
    g_q = jnp.einsum("shqk,skhd->sqhd", g_s, k, preferred_element_type=F32) * scale
    g_k = jnp.einsum("shqk,sqhd->skhd", g_s, q, preferred_element_type=F32) * scale
    return jnp.concatenate([u.reshape(-1, width).astype(BF) for u in (g_q, g_k, g_v)], axis=1)


def shards(
    plan,
    tokens,
    cotangent,
    segments,
    norm1_gain,
    norm1_shift,
    w_qkv,
    b_query,
    b_value,
    w_out,
    b_out,
    norm2_gain,
    norm2_shift,
    w_up,
    b_up,
    w_down,
    b_down,
):
    nz, nf, nr, group = plan.nz, plan.nf, plan.nr, plan.group
    layers, own_rows, triple = w_qkv.shape
    width = triple // 3
    own_hidden = w_down.shape[1]
    piece = own_hidden // nr
    length = tokens.shape[1]
    total = length * nz
    hpr = plan.heads
    span = hpr * HD
    scale = 1.0 / math.sqrt(HD)
    fsdp = lax.axis_index("fsdp")
    replica = lax.axis_index("replica")
    seq = lax.axis_index("seq")
    rank = plan.rank()

    def head_columns(v):
        rows = v.shape[0]
        v = v.reshape(rows, 3, width)
        v = jnp.pad(v, ((0, 0), (0, 0), (0, group * span - width)))
        v = v.reshape(rows, 3, group, span)
        ranks = jnp.array([[plan.rank_of(f, r) for f in range(nf)] for r in range(nr)])
        v = jnp.take(v, ranks[replica], axis=2)
        return v.transpose(2, 0, 1, 3).reshape(nf, rows, 3 * span)

    def fetch(layer):
        qkv = plan.exchange_fsdp(head_columns(w_qkv[layer]))
        qkv = gather_seq(qkv.reshape(nf * own_rows, 3 * span))
        half = width // nr
        out = lax.dynamic_slice_in_dim(w_out[layer], replica * half, half, 1)
        out = gather_seq(out)
        up = w_up[layer].reshape(own_rows, nz, nf, nr, piece)
        up = lax.dynamic_index_in_dim(up, replica, 3, keepdims=False)
        up = up.transpose(2, 0, 1, 3).reshape(nf, own_rows, nz * piece)
        up = gather_seq(plan.exchange_fsdp(up).reshape(nf * own_rows, nz * piece))
        down = lax.dynamic_slice_in_dim(w_down[layer], replica * piece, piece, 0)
        down = gather_seq(down)
        out = plan.gather_replica(out, 1)
        out = out.reshape(nz, 1, own_rows, width)
        if plan.cube:
            core, y, _ = plan.bits()
            other = plan.swap_core(out)
            out = jnp.concatenate(
                [jnp.where(core == 0, out, other), jnp.where(core == 0, other, out)], axis=1
            )
            other = plan.swap_y(out)
            out = jnp.concatenate(
                [jnp.where(y == 0, out, other), jnp.where(y == 0, other, out)], axis=1
            )
        else:
            out = lax.all_gather(out, "fsdp", axis=1, tiled=True)
        out = out.reshape(width, width)
        return qkv, out, up, down

    small = jnp.concatenate(
        [norm1_gain, norm1_shift, b_query, b_value, b_out, norm2_gain, norm2_shift, b_down, b_up],
        axis=1,
    )
    small = lax.all_gather(small, OWNERS, axis=0, tiled=False)

    def vectors(layer):
        each = [
            small[:, layer, i * own_rows : (i + 1) * own_rows].reshape(width).astype(F32)
            for i in range(8)
        ]
        bias_up = small[:, layer, 8 * own_rows :].reshape(nz, nf, nr, piece)
        bias_up = lax.dynamic_index_in_dim(bias_up, fsdp, 1, keepdims=False)
        bias_up = lax.dynamic_index_in_dim(bias_up, replica, 1, keepdims=False)

        def mine(v):
            return lax.dynamic_slice_in_dim(
                jnp.pad(v, (0, group * span - width)), rank * span, span
            )

        bias_qkv = jnp.concatenate([mine(each[2]), jnp.zeros((span,), F32), mine(each[3])])
        return each, bias_qkv, bias_up.reshape(nz * piece).astype(F32)

    vecs = [vectors(layer) for layer in range(layers)]
    weights = [fetch(layer) for layer in range(layers)]

    hidden = plan.regroup(tokens[0]).astype(F32)
    codes = segments[0] * 65536 + seq * length + jnp.arange(length, dtype=jnp.int32)
    codes = plan.regroup(codes[None])
    codes = plan.gather_rows(codes)
    grad = plan.regroup(cotangent[0]).astype(F32)

    kept = []
    for layer in range(layers):
        qkv_w, out_w, up_w, down_w = weights[layer]
        (gain1, shift1, _, _, bias_out, gain2, shift2, bias_down), bias_qkv, bias_up = vecs[layer]
        unit1, inv1 = norm_parts(hidden)
        normed = plan.gather_rows((unit1 * gain1 + shift1).astype(BF))
        packed = (dot(normed, qkv_w, 1, 0) + bias_qkv).astype(BF)
        mixed, lse = attend(packed, codes, plan, total, scale)
        mixed = plan.exchange(mixed.reshape(group, length, span))
        mixed = plan.working_to_rank(mixed, 0)
        mixed = mixed.transpose(1, 0, 2).reshape(length, group * span)[:, :width]
        middle = hidden + (dot(mixed, out_w, 1, 0) + bias_out)
        unit2, inv2 = norm_parts(middle)
        normed_two = plan.gather_rows((unit2 * gain2 + shift2).astype(BF))
        lifted = dot(normed_two, up_w, 1, 0) + bias_up
        activated = gelu_tanh(lifted).astype(BF)
        lowered = plan.scatter_rows(dot(activated, down_w, 1, 0))
        kept.append(
            (unit1, inv1, normed, packed, lse, mixed, unit2, inv2, normed_two, lifted, activated)
        )
        hidden = middle + (lowered + bias_down)
    output = plan.regroup(hidden)

    def own_piece_columns(v):
        rows = v.shape[1]
        v = plan.gather_replica(v[..., None, :], 2)
        v = v.reshape(nf, rows, nr, nz, piece).transpose(1, 3, 0, 2, 4)
        return v.reshape(rows, nz * nf * nr * piece)

    results = [None] * layers
    smalls = [None] * layers
    for layer in reversed(range(layers)):
        qkv_w, out_w, up_w, down_w = weights[layer]
        (gain1, _, _, _, _, gain2, _, _), _, _ = vecs[layer]
        unit1, inv1, normed, packed, lse, mixed, unit2, inv2, normed_two, lifted, activated = kept[
            layer
        ]
        g_low = grad.astype(BF)
        g_full = plan.gather_rows(g_low)
        g_act = dot(g_full, down_w, 1, 1)
        g_lift32 = gelu_slope(lifted) * g_act
        g_lift = g_lift32.astype(BF)
        grad_down = dot(activated, g_full, 0, 0).astype(BF)
        grad_up = dot(normed_two, g_lift, 0, 0).astype(BF)
        g_n2 = plan.scatter_rows(dot(g_lift, up_w, 1, 1))
        grad_b_up = jnp.sum(g_lift.astype(F32), axis=0)
        g_mid = grad + norm_pull(g_n2, unit2, inv2, gain2)
        g_att = g_mid.astype(BF)
        g_mixed = dot(g_att, out_w, 1, 1).astype(BF)
        grad_out = dot(mixed, g_att, 0, 0)
        g_mixed = jnp.pad(g_mixed, ((0, 0), (0, group * span - width)))
        g_mixed = g_mixed.reshape(length, group, span).transpose(1, 0, 2)
        g_mixed = plan.exchange(plan.working_to_rank(g_mixed, 0))
        g_packed = attend_back(
            packed, codes, lse, g_mixed.reshape(group * length, span), plan, total, scale
        )
        grad_qkv = dot(normed, g_packed, 0, 0).astype(BF)
        g_n1 = plan.scatter_rows(dot(g_packed, qkv_w, 1, 1))
        g_b = jnp.sum(g_packed.astype(F32), axis=0)
        vector_grads = (
            jnp.sum(g_n1 * unit1, axis=0),
            jnp.sum(g_n1, axis=0),
            g_b,
            jnp.sum(g_att.astype(F32), axis=0),
            jnp.sum(g_n2 * unit2, axis=0),
            jnp.sum(g_n2, axis=0),
            jnp.sum(g_low.astype(F32), axis=0),
            grad_b_up,
        )
        grad = g_mid + norm_pull(g_n1, unit1, inv1, gain1)

        down = scatter_seq(grad_down)
        up = scatter_seq(grad_up)
        rows4 = grad_out.reshape(nz, nf, own_rows, width)
        if plan.cube:
            core, y, x = plan.bits()
            rows4 = rows4.reshape(nz, 2, 2, own_rows, width)

            def halve(v, bit, axis, swap):
                a = lax.index_in_dim(v, 0, axis, keepdims=False)
                b = lax.index_in_dim(v, 1, axis, keepdims=False)
                keep = jnp.where(bit == 0, a, b)
                send = jnp.where(bit == 0, b, a)
                return keep + swap(send.astype(BF)).astype(F32)

            rows4 = halve(rows4, core, 2, plan.swap_core)
            rows4 = halve(rows4, y, 1, plan.swap_y)
            rows4 = rows4.reshape(nz, own_rows, 2, width // 2)
            rows4 = halve(rows4, x, 2, plan.swap_x)
            outs = rows4.reshape(nz * own_rows, width // nr).astype(BF)
        else:
            outs = lax.psum_scatter(
                rows4.astype(BF), "fsdp", scatter_dimension=1, tiled=False
            ).reshape(nz * own_rows, width)
            outs = lax.psum_scatter(outs, "replica", scatter_dimension=1, tiled=True)
        part = width // (4 * nr)
        outs = outs.reshape(nz, own_rows, 4, part).transpose(0, 2, 1, 3)
        outs = scatter_seq(outs.reshape(nz * 4 * own_rows, part))
        outs = outs.reshape(4, own_rows, part).transpose(1, 0, 2).reshape(own_rows, 4 * part)
        qkv = scatter_seq(grad_qkv)

        down = plan.gather_replica(down, 0).astype(F32)
        up = own_piece_columns(plan.exchange_fsdp(up.reshape(nf, own_rows, nz * piece)))
        outs = plan.gather_replica(outs, 1).astype(F32)
        qkv = plan.exchange_fsdp(qkv.reshape(nf, own_rows, 3 * span))
        qkv = plan.gather_replica(qkv[..., None, :], 2)
        qkv = qkv.reshape(nf, own_rows, nr, 3, span)
        where = [None] * group
        for f in range(nf):
            for r in range(nr):
                where[plan.rank_of(f, r)] = qkv[f, :, r]
        qkv = jnp.concatenate(where, axis=2)[:, :, :width].reshape(own_rows, triple)
        results[layer] = (qkv.astype(F32), outs, up.astype(F32), down)
        smalls[layer] = vector_grads
    grad_tokens = plan.regroup(grad)

    def scattered(layer):
        n1g, n1s, g_b, b_o, n2g, n2s, b_d, b_u = smalls[layer]

        def place(v):
            full = lax.dynamic_update_slice_in_dim(
                jnp.zeros((group * span,), F32), v, rank * span, 0
            )
            return full[:width]

        b_u = lax.dynamic_update_slice(
            jnp.zeros((nz, nf, nr, piece), F32),
            b_u.reshape(nz, 1, 1, piece),
            (0, fsdp, replica, 0),
        )
        rows = [n1g, n1s, place(g_b[:span]), place(g_b[2 * span :]), b_o, n2g, n2s, b_d]
        return jnp.concatenate(
            [v.reshape(nz * nf, own_rows) for v in rows] + [b_u.reshape(nz * nf, own_hidden)],
            axis=1,
        )

    flat = jnp.concatenate([scattered(layer) for layer in range(layers)], axis=1)
    flat = lax.psum_scatter(flat, OWNERS, scatter_dimension=0, tiled=True)
    flat = lax.psum(flat, "replica").reshape(layers, -1)
    vec = [flat[:, i * own_rows : (i + 1) * own_rows] for i in range(8)]
    grad_b_up = flat[:, 8 * own_rows :]
    mats = [jnp.stack([results[layer][i] for layer in range(layers)]) for i in range(4)]
    return (
        output[None],
        grad_tokens[None],
        vec[0],
        vec[1],
        mats[0],
        vec[2],
        vec[3],
        mats[1],
        vec[4],
        vec[5],
        vec[6],
        mats[2],
        grad_b_up,
        mats[3],
        vec[7],
    )


def solution(mesh):
    plan = Plan(mesh)
    data = P(("fsdp", "replica"), "seq", None)
    vector = P(None, ("seq", "fsdp"))
    matrix = P(None, ("seq", "fsdp"), None)
    weights = (
        vector,
        vector,
        matrix,
        vector,
        vector,
        matrix,
        vector,
        vector,
        vector,
        matrix,
        vector,
        matrix,
        vector,
    )
    in_specs = (data, data, P(("fsdp", "replica"), "seq")) + weights
    out_specs = (data, data) + weights
    return jax.shard_map(
        functools.partial(shards, plan),
        mesh=mesh,
        in_specs=in_specs,
        out_specs=out_specs,
        check_vma=False,
    )
```

time: 3220 us -> 1520 us (0.47)
  waiting for transfers between devices: 1480 us -> 421 us
  blocking collectives: 1000 us -> 173 us
  matrix products: 334 us -> 166 us
  local copies, waits for them, and re-layouts: 218 us -> 378 us
  other arithmetic: 38.5 us -> 176 us
  starting transfers between devices: 102 us -> 183 us
    all_gather x15 -> x6, waiting for transfers between devices: 1240 us -> 0.03 us  [gather_seq(): return lax.all_gather(v, 'seq', axis=0, tiled=True)]
    unnamed x2 -> x0, blocking collectives: 964 us -> none
    ppermute x0 -> x120, waiting for transfers between devices: none -> 325 us  [the longest x41 188 us: swap_y(): return lax.ppermute(v, 'fsdp', [(f, f ^ 2) for f in range(self.nf)])]
    ppermute x0 -> x120, starting transfers between devices: none -> 181 us  [the longest x41 89.8 us: swap_y(): return lax.ppermute(v, 'fsdp', [(f, f ^ 2) for f in range(self.nf)])]
    dot_general x36, matrix products: 334 us -> 166 us  [the longest x24 133 us: dot(): lax.dot_general(a, b, (((ca,), (cb,)), ((), ())), preferred_element_type=...]
    unnamed x45 -> x20, waiting for transfers between devices: 244 us -> 93.3 us
    unnamed x330 -> x355, local copies, waits for them, and re-layouts: 187 us -> 50.1 us
    all_gather x2 -> x3, blocking collectives: 32.4 us -> 164 us  [the longest x2 141 us: gather_seq(): return lax.all_gather(v, 'seq', axis=0, tiled=True)]
  transfers between devices with their start and end apart: 35 -> 135, of which waited for: 22 -> 66; matrix products, arithmetic and copies ran while one was open for 43% -> 40% of each run, Pallas kernels for 0% -> 0%
where the time goes in v1:
time: 1520 us; the launch traced here: 1510 us
  waiting for transfers between devices  421 us (28%)
  local copies, waits for them, and re-layouts  378 us (25%)
  starting transfers between devices  183 us (12%)
  other arithmetic  176 us (12%)
  blocking collectives  173 us (11%)
  matrix products  166 us (11%)
  between operations  18 us (1%)
    ppermute x41, waiting for transfers between devices, swap_y(): return lax.ppermute(v, 'fsdp', [(f, f ^ 2) for f in range(self.nf)])  188 us
    all_gather x2, blocking collectives, gather_seq(): return lax.all_gather(v, 'seq', axis=0, tiled=True)  141 us
    dot_general x24, matrix products, dot(): lax.dot_general(a, b, (((ca,), (cb,)), ((), ())), preferred_element_type=...  133 us
    ppermute x41, waiting for transfers between devices, swap_x(): return lax.ppermute(v, 'replica', [(r, r ^ 1) for r in range(self.nr)])  117 us
    unnamed x20, waiting for transfers between devices  93.3 us
    ppermute x41, starting transfers between devices, swap_y(): return lax.ppermute(v, 'fsdp', [(f, f ^ 2) for f in range(self.nf)])  89.8 us
    ppermute x41, starting transfers between devices, swap_x(): return lax.ppermute(v, 'replica', [(r, r ^ 1) for r in range(self.nr)])  65.7 us
    unnamed x355, local copies, waits for them, and re-layouts  50.1 us
  transfers between devices with their start and end apart: 135, of which 66 were waited for; matrix products, arithmetic and copies ran while one was open for 40% of the time, Pallas kernels for 0%

profile of v1, /device:TPU:0, one launch (start us, length us, event | category | flops | bytes accessed | tf_op | source)
XLA Modules:
  0.0 1514.3 jit_solution(10812596844972196040)
XLA Ops:
  46.6 13.2 slice_reduce_fusion
  75.1 9.8 collective-permute-done.25
  92.6 97.2 %all-gather.1 = bf16[1,400,800]{2,0,1:T(2,128)(2,1)S(1)} all-gather(bf16[1,100,800]{2,0,1:T(2,128)(2,1)S(1)} %constant_dynamic-slice_fusion.5), channel_id=3, replica_groups=mesh['seq'=4,'fsdp'=4,'replica'=2] {'seq'}, dimensions={1}, use_global_device_ids=true | all-gather | bytes 800000 | tf_op jit(solution)/shard_map/all_gather | solution.py:199
  194.4 23.5 %all-gather.5 = bf16[16,2,1200]{2,1,0:T(2,128)(2,1)S(1)} all-gather(bf16[1,2,1200]{2,1,0:T(2,128)(2,1)S(1)} %bitcast.614), channel_id=2, replica_groups=mesh['seq'=4,'fsdp'=4,'replica'=2] {'seq','fsdp'}, dimensions={0}, use_global_device_ids=true | all-gather | bytes 81600 | tf_op jit(solution)/shard_map/all_gather | solution.py:321
  298.2 23.0 %collective-permute-done.18 = bf16[4,2,100,1600]{3,0,2,1:T(4,128)(2,1)} collective-permute-done((bf16[4,2,100,1600]{3,0,2,1:T(4,128)(2,1)}, bf16[4,2,100,1600]{3,0,2,1:T(4,128)(2,1)}, u32[]{:S(2)}, u32[]{:S(2)}) %collective-permute-start.18) | collective-permute-done | bytes 2560032 | tf_op jit(solution)/shard_map/ppermute | solution.py:90
  423.8 43.4 %all-gather.3 = bf16[1,400,800]{2,0,1:T(2,128)(2,1)S(1)} all-gather(bf16[1,100,800]{2,0,1:T(2,128)(2,1)S(1)} %constant_dynamic-slice_fusion.2), channel_id=5, replica_groups=mesh['seq'=4,'fsdp'=4,'replica'=2] {'seq'}, dimensions={1}, use_global_device_ids=true | all-gather | bytes 800000 | tf_op jit(solution)/shard_map/all_gather | solution.py:199
  484.7 10.0 collective-permute-done.29
  543.4 40.3 %collective-permute-start.60 = (bf16[128,1600]{0,1:T(8,128)(2,1)}, bf16[128,1600]{0,1:T(8,128)(2,1)}, u32[]{:S(2)}, u32[]{:S(2)}) collective-permute-start(bf16[128,1600]{0,1:T(8,128)(2,1)} %collective-permute-done.58), channel_id=1, source_target_pairs={{0,4},{2,6},{4,0},{6,2},{1,5},{3,7},{5,1},{7,3},{8,12},{10,14},{12... | collective-permute-start | bytes 1228808 | tf_op jit(solution)/shard_map/ppermute | solution.py:90
  626.1 25.9 %collective-permute-done.44 = bf16[4,2,100,1600]{3,0,2,1:T(4,128)(2,1)} collective-permute-done((bf16[4,2,100,1600]{3,0,2,1:T(4,128)(2,1)}, bf16[4,2,100,1600]{3,0,2,1:T(4,128)(2,1)}, u32[]{:S(2)}, u32[]{:S(2)}) %collective-permute-start.44) | collective-permute-done | bytes 2560032 | tf_op jit(solution)/shard_map/ppermute | solution.py:90
  738.7 8.7 convert_reduce_fusion
  874.4 10.5 reshape_reshape.61
  950.3 8.8 convert_reduce_fusion.1
  964.6 10.1 collective-permute-done.109
  986.5 15.5 %collective-permute-done.110 = bf16[4,100,800]{2,0,1:T(4,128)(2,1)S(1)} collective-permute-done((bf16[4,100,800]{2,0,1:T(4,128)(2,1)S(1)}, bf16[4,100,800]{2,0,1:T(4,128)(2,1)S(1)}, u32[]{:S(2)}, u32[]{:S(2)}) %collective-permute-start.110) | collective-permute-done | bytes 640032 | tf_op jit(solution)/shard_map/ppermute | solution.py:93
  1116.2 8.4 convolution_convert_fusion.3
  1143.3 10.5 reshape_reshape.60
  1167.0 8.6 collective-permute-start.116
  1187.5 18.8 %collective-permute-start.111 = (bf16[100,800]{0,1:T(8,128)(2,1)S(1)}, bf16[100,800]{0,1:T(8,128)(2,1)S(1)}, u32[]{:S(2)}, u32[]{:S(2)}) collective-permute-start(bf16[100,800]{0,1:T(8,128)(2,1)S(1)} %bitcast.566), channel_id=1, source_target_pairs={{0,1},{1,0},{2,3},{3,2},{4,5},{5,4},{6,7},{7,6},{8,9},{9,8},{10,11... | collective-permute-start | bytes 480008 | tf_op jit(solution)/shard_map/ppermute | solution.py:93
  1245.0 46.3 %all-reduce.13.cloned.1.call-done = f32[16,2400]{1,0:T(8,128)} async-done(((f32[16,2400]{1,0:T(8,128)}), f32[16,2400]{1,0:T(8,128)}) %all-reduce.13.cloned.1.call-update) | async-done | bytes 153616
  1292.9 8.8 psum.7
  1303.0 46.7 %reduce-scatter.29.cloned.1.call-done = bf16[200,1600]{1,0:T(8,128)(2,1)} async-done(((bf16[800,1600]{1,0:T(8,128)(2,1)}), bf16[200,1600]{1,0:T(8,128)(2,1)}) %reduce-scatter.29.cloned.1.call-update) | async-done | bytes 640016
  1353.9 14.0 collective-permute-done.118
  1386.8 10.5 collective-permute-done.106
  1477.3 11.1 collective-permute-done.103
  (1086 shorter events, 972.8 us)
Async XLA Ops:
  7.2 260.7 %all-gather.13.cloned.1.call-start = ((), (), s32[]{:S(2)}) async-start(), calls=%async_computation.8 | async-start | bytes 3072000 | tf_op jit(solution)/shard_map/all_gather | solution.py:199
  45.9 357.0 %all-gather.15.cloned.1.call-start = ((), (), s32[]{:S(2)}) async-start(), calls=%async_computation.9 | async-start | bytes 3584000 | tf_op jit(solution)/shard_map/all_gather | solution.py:199
  87.0 323.7 %all-gather.21.cloned.1.call-start = ((), (), s32[]{:S(2)}) async-start(), calls=%async_computation.16 | async-start | bytes 3328000 | tf_op jit(solution)/shard_map/all_gather | solution.py:199
  87.6 140.4 %collective-permute-start.8 = (s32[1,128]{1,0:T(1,128)}, s32[1,128]{1,0:T(1,128)}, u32[]{:S(2)}, u32[]{:S(2)}) collective-permute-start(s32[1,128]{1,0:T(1,128)} %iota_add_fusion), channel_id=1, source_target_pairs={{0,0},{1,8},{4,16},{5,24},{2,2},{3,10},{6,18},{7,26},{8,1},{9,9},{... | collective-permute-start | bytes 1544 | tf_op jit(solution)/shard_map/ppermute | solution.py:84
  89.4 131.1 %collective-permute-start = (bf16[128,1600]{0,1:T(8,128)(2,1)S(1)}, bf16[128,1600]{0,1:T(8,128)(2,1)S(1)}, u32[]{:S(2)}, u32[]{:S(2)}) collective-permute-start(bf16[128,1600]{0,1:T(8,128)(2,1)S(1)} %bitcast.615), channel_id=1, source_target_pairs={{0,0},{1,8},{4,16},{5,24},{2,2},{3,10},{6,18},{7,26},{8,1},{9,9},{... | collective-permute-start | bytes 1228808 | tf_op jit(solution)/shard_map/ppermute | solution.py:84
  194.1 408.5 %all-gather.17.cloned.1.call-start = ((), (), s32[]{:S(2)}) async-start(), calls=%async_computation.10 | async-start | bytes 3072000 | tf_op jit(solution)/shard_map/all_gather | solution.py:199
  396.0 334.9 %all-gather.19.cloned.1.call-start = ((), (), s32[]{:S(2)}) async-start(), calls=%async_computation.11 | async-start | bytes 3584000 | tf_op jit(solution)/shard_map/all_gather | solution.py:199
  479.7 259.0 %all-gather.23.cloned.1.call-start = ((), (), s32[]{:S(2)}) async-start(), calls=%async_computation.17 | async-start | bytes 3328000 | tf_op jit(solution)/shard_map/all_gather | solution.py:199
  516.6 71.6 %collective-permute-start.43 = (bf16[4,1,100,1600]{3,0,2,1:T(4,128)(2,1)}, bf16[4,1,100,1600]{3,0,2,1:T(4,128)(2,1)}, u32[]{:S(2)}, u32[]{:S(2)}) collective-permute-start(bf16[4,1,100,1600]{3,0,2,1:T(4,128)(2,1)} %copy.795), channel_id=1, source_target_pairs={{0,2},{2,0},{4,6},{6,4},{1,3},{3,1},{5,7},{7,5},{8,10},{10,8},{12,... | collective-permute-start | bytes 3840008 | tf_op jit(solution)/shard_map/ppermute | solution.py:87
  542.4 590.6 %reduce-scatter.23.cloned.1.call-start = ((), (), s32[]{:S(2)}) async-start(), calls=%async_computation.15 | async-start | bytes 3584000 | tf_op jit(solution)/shard_map/reduce_scatter | solution.py:203
  543.4 144.5 %collective-permute-start.60 = (bf16[128,1600]{0,1:T(8,128)(2,1)}, bf16[128,1600]{0,1:T(8,128)(2,1)}, u32[]{:S(2)}, u32[]{:S(2)}) collective-permute-start(bf16[128,1600]{0,1:T(8,128)(2,1)} %collective-permute-done.58), channel_id=1, source_target_pairs={{0,4},{2,6},{4,0},{6,2},{1,5},{3,7},{5,1},{7,3},{8,12},{10,14},{12... | collective-permute-start | bytes 1228808 | tf_op jit(solution)/shard_map/ppermute | solution.py:90
  583.7 106.0 %collective-permute-start.59 = (bf16[128,1600]{0,1:T(8,128)(2,1)}, bf16[128,1600]{0,1:T(8,128)(2,1)}, u32[]{:S(2)}, u32[]{:S(2)}) collective-permute-start(bf16[128,1600]{0,1:T(8,128)(2,1)} %collective-permute-done.58), channel_id=1, source_target_pairs={{0,1},{1,0},{2,3},{3,2},{4,5},{5,4},{6,7},{7,6},{8,9},{9,8},{10,11... | collective-permute-start | bytes 1228808 | tf_op jit(solution)/shard_map/ppermute | solution.py:93
  859.9 276.9 %reduce-scatter.31.cloned.1.call-start = ((), (), s32[]{:S(2)}) async-start(), calls=%async_computation.22 | async-start | bytes 3328000
  934.1 252.3 %reduce-scatter.27.cloned.1.call-start = ((), (), s32[]{:S(2)}) async-start(), calls=%async_computation.19 | async-start | bytes 1024000
  1004.5 208.7 %reduce-scatter.19.cloned.1.call-start = ((), (), s32[]{:S(2)}) async-start(), calls=%async_computation.13 | async-start | bytes 3072000 | tf_op jit(solution)/shard_map/reduce_scatter | solution.py:203
  1014.9 216.0 %reduce-scatter.21.cloned.1.call-start = ((), (), s32[]{:S(2)}) async-start(), calls=%async_computation.14 | async-start | bytes 3584000 | tf_op jit(solution)/shard_map/reduce_scatter | solution.py:203
  1048.7 242.6 %all-reduce.13.cloned.1.call-start = ((), (), s32[]{:S(2)}) async-start(), calls=%async_computation.20 | async-start | bytes 311296
  1116.1 233.6 %reduce-scatter.29.cloned.1.call-start = ((), (), s32[]{:S(2)}) async-start(), calls=%async_computation.21 | async-start | bytes 3328000
  1124.6 277.3 %reduce-scatter.17.cloned.1.call-start = ((), (), s32[]{:S(2)}) async-start(), calls=%async_computation.12 | async-start | bytes 3072000 | tf_op jit(solution)/shard_map/reduce_scatter | solution.py:203
  1213.2 190.3 %collective-permute-start.117 = (bf16[4,100,1,800]{3,0,2,1:T(4,128)(2,1)}, bf16[4,100,1,800]{3,0,2,1:T(4,128)(2,1)}, u32[]{:S(2)}, u32[]{:S(2)}) collective-permute-start(bf16[4,100,1,800]{3,0,2,1:T(4,128)(2,1)} %copy.902), channel_id=1, source_target_pairs={{0,1},{1,0},{2,3},{3,2},{4,5},{5,4},{6,7},{7,6},{8,9},{9,8},{10,11... | collective-permute-start | bytes 1920008 | tf_op jit(solution)/shard_map/ppermute | solution.py:93
  1222.8 218.5 %reduce-scatter.25.cloned.1.call-start = ((), (), s32[]{:S(2)}) async-start(), calls=%async_computation.18 | async-start | bytes 1024000
  1238.8 112.4 %collective-permute-start.97 = (f32[128,1600]{0,1:T(8,128)}, f32[128,1600]{0,1:T(8,128)S(1)}, u32[]{:S(2)}, u32[]{:S(2)}) collective-permute-start(f32[128,1600]{0,1:T(8,128)} %fusion.88), channel_id=1, source_target_pairs={{0,0},{1,8},{4,16},{5,24},{2,2},{3,10},{6,18},{7,26},{8,1},{9,9},{... | collective-permute-start | bytes 2457608 | tf_op jit(solution)/shard_map/ppermute | solution.py:84
  1241.1 110.1 %collective-permute-start.113 = (bf16[2,100,800]{1,2,0:T(8,128)(2,1)S(1)}, bf16[2,100,800]{1,2,0:T(8,128)(2,1)S(1)}, u32[]{:S(2)}, u32[]{:S(2)}) collective-permute-start(bf16[2,100,800]{1,2,0:T(8,128)(2,1)S(1)} %get-tuple-element.225), channel_id=1, source_target_pairs={{0,4},{2,6},{4,0},{6,2},{1,5},{3,7},{5,1},{7,3},{8,12},{10,14},{12... | collective-permute-start | bytes 960008 | tf_op jit(solution)/shard_map/ppermute | solution.py:90
  1244.7 125.5 %collective-permute-start.105 = (bf16[4,100,1600]{2,0,1:T(4,128)(2,1)}, bf16[4,100,1600]{2,0,1:T(4,128)(2,1)}, u32[]{:S(2)}, u32[]{:S(2)}) collective-permute-start(bf16[4,100,1600]{2,0,1:T(4,128)(2,1)} %copy.861), channel_id=1, source_target_pairs={{0,4},{2,6},{4,0},{6,2},{1,5},{3,7},{5,1},{7,3},{8,12},{10,14},{12... | collective-permute-start | bytes 3840008 | tf_op jit(solution)/shard_map/ppermute | solution.py:90
  (270 other events, 3333.5 us)
Sparse Core Ops, SparseCore 0:
  46.0 54.3 all-gather.12
  102.5 90.7 all-gather.14
  194.9 55.8 all-gather.20
  396.1 67.8 all-gather.16
  479.8 56.7 all-gather.18
  542.5 69.1 all-gather.22
  860.0 57.5 reduce-scatter.22
  934.2 53.6 reduce-scatter.30
  1004.6 25.2 reduce-scatter.26
  1032.1 49.0 reduce-scatter.18
  1084.1 93.3 reduce-scatter.20
  1180.8 110.4 all-reduce.12
  1293.6 56.1 reduce-scatter.28
  1351.9 49.9 reduce-scatter.16
  1404.6 23.1 reduce-scatter.24

commit v2 on v1

v2 whole, which is shorter than its diff:
```python
import functools
import math

import jax
import jax.numpy as jnp
from jax import lax
from jax.experimental import pallas as pl
from jax.experimental.pallas import tpu as pltpu
from jax.sharding import PartitionSpec as P


HEADS = 25
HD = 64
BF = jnp.bfloat16
F32 = jnp.float32
ALL = ("seq", "fsdp", "replica")
GROUP = ("fsdp", "replica")
OWNERS = ("seq", "fsdp")
CODE = 65536
LOW = -1e30


def dot(a, b, ca=1, cb=0):
    return lax.dot_general(a, b, (((ca,), (cb,)), ((), ())), preferred_element_type=F32)


def norm_parts(v):
    mean = jnp.mean(v, axis=-1, keepdims=True)
    centred = v - mean
    spread = jnp.mean(centred * centred, axis=-1, keepdims=True)
    inv = lax.rsqrt(spread + 1e-05)
    return centred * inv, inv


def norm_pull(grad, unit, inv, gain):
    scaled = grad * gain
    first = jnp.mean(scaled, axis=-1, keepdims=True)
    second = jnp.mean(scaled * unit, axis=-1, keepdims=True)
    return inv * (scaled - first - unit * second)


def gelu_both(value):
    tanh = jnp.tanh(0.7978845608028654 * (value + 0.044715 * value * value * value))
    inner = 0.7978845608028654 * (1.0 + 3.0 * 0.044715 * value * value)
    half = 0.5 * (1.0 + tanh)
    return value * half, half + 0.5 * value * (1.0 - tanh * tanh) * inner


class Plan:
    def __init__(self, mesh):
        self.nz = mesh.shape["seq"]
        self.nf = mesh.shape["fsdp"]
        self.nr = mesh.shape["replica"]
        self.group = self.nf * self.nr
        self.cube = self.nf == 4 and self.nr == 2
        self.heads = 2 * -(-HEADS // (2 * self.group))
        self.span = self.heads * HD
        order = sorted(
            (self.rank_of(f, r), f * self.nr + r) for f in range(self.nf) for r in range(self.nr)
        )
        self.place = [member for _, member in order]
        self.back = [0] * self.group
        for rank, member in order:
            self.back[member] = rank

    def rank_of(self, f, r):
        half = self.group // 2
        if self.nf % 2:
            return f * self.nr + r
        return (f % 2) * half + (f // 2) * self.nr + r

    def rank(self):
        return self.rank_of(lax.axis_index("fsdp"), lax.axis_index("replica"))

    def regroup(self, v, back=False):
        nz = self.nz
        pairs = []
        for z in range(nz):
            for g in range(self.group):
                goal = g % nz
                slot = (g // nz) * nz + (z ^ goal if nz & (nz - 1) == 0 else z)
                pairs.append((z * self.group + self.place[g], goal * self.group + self.place[slot]))
        if back:
            pairs = [(there, here) for here, there in pairs]
        return lax.ppermute(v, ALL, pairs)

    def swap_core(self, v):
        return lax.ppermute(v, "fsdp", [(f, f ^ 1) for f in range(self.nf)])

    def swap_y(self, v):
        return lax.ppermute(v, "fsdp", [(f, f ^ 2) for f in range(self.nf)])

    def swap_x(self, v):
        return lax.ppermute(v, "replica", [(r, r ^ 1) for r in range(self.nr)])

    def swap_xy(self, v):
        pairs = [
            (f * self.nr + r, (f ^ 2) * self.nr + (r ^ 1))
            for f in range(self.nf)
            for r in range(self.nr)
        ]
        return lax.ppermute(v, GROUP, pairs)

    def source(self):
        base = jnp.arange(self.group, dtype=jnp.int32)
        return base ^ self.rank() if self.cube else base

    def gather_pieces(self, v):
        if not self.cube:
            full = lax.all_gather(v, GROUP, axis=0, tiled=False)
            return [full[member] for member in self.place]
        near = [v, self.swap_x(v), self.swap_y(v), self.swap_xy(v)]
        return near + [self.swap_core(piece) for piece in near]

    def gather_doubling(self, v):
        if not self.cube:
            return jnp.concatenate(self.gather_pieces(v))
        for swap in (self.swap_x, self.swap_y, self.swap_core):
            v = jnp.concatenate([v, swap(v)])
        return v

    def scatter_parts(self, near, far):
        if not self.cube:
            blocks = jnp.concatenate([near.astype(BF), far])
            rows = blocks.shape[0] // self.group
            blocks = blocks.reshape(self.group, rows, -1)[jnp.array(self.back)]
            blocks = blocks.reshape(self.group * rows, -1)
            return lax.psum_scatter(blocks, GROUP, scatter_dimension=0, tiled=True).astype(F32)
        rows, columns = near.shape[0] // 4, near.shape[1]
        own, to_x, to_y, to_xy = call(
            fold_kernel,
            [sds((rows, columns), F32)] + [sds((rows, lanes(columns)), BF)] * 3,
            [],
            0,
            [near, self.swap_core(far)],
        )
        parts = self.swap_xy(to_xy), self.swap_x(to_x), self.swap_y(to_y)
        parts = [part[:, :columns].astype(F32) for part in parts]
        return own + parts[0] + parts[1] + parts[2]

    def exchange(self, v):
        if not self.cube:
            v = v.reshape(self.group, -1, v.shape[1])[jnp.array(self.back)]
            v = lax.all_to_all(v, GROUP, split_axis=0, concat_axis=0, tiled=True)
            return [v[member] for member in self.place]
        rows = v.shape[0] // 8
        half = 4 * rows
        far = self.swap_core(v[half:])
        out = [[v[:rows], far[:rows]]]
        for i, swap in ((1, self.swap_x), (2, self.swap_y), (3, self.swap_xy)):
            both = swap(
                jnp.concatenate([v[i * rows : (i + 1) * rows], far[i * rows : (i + 1) * rows]])
            )
            out.append([both[:rows], both[rows:]])
        return [pair[0] for pair in out] + [pair[1] for pair in out]

    def flips(self, v):
        f = lax.axis_index("fsdp")
        v = v.reshape((2, 2) + v.shape[1:])
        v = jnp.where(f // 2 == 1, jnp.flip(v, 0), v)
        return jnp.where(f % 2 == 1, jnp.flip(v, 1), v)

    def gather_owners(self, v):
        if not self.cube or self.nz != 4:
            return lax.all_gather(v, OWNERS, axis=0, tiled=False)
        z, f = lax.axis_index("seq"), lax.axis_index("fsdp")
        far = [
            lax.ppermute(v, "seq", [(i, i ^ d) for i in range(4)]) if d else v for d in range(4)
        ]
        v = jnp.stack(far).reshape((2, 2) + v.shape)
        v = jnp.where(z // 2 == 1, jnp.flip(v, 0), v)
        v = jnp.where(z % 2 == 1, jnp.flip(v, 1), v)
        other = self.swap_core(v)
        v = jnp.stack([jnp.where(f % 2 == 0, v, other), jnp.where(f % 2 == 0, other, v)], axis=2)
        other = self.swap_y(v)
        v = jnp.stack([jnp.where(f // 2 == 0, v, other), jnp.where(f // 2 == 0, other, v)], axis=2)
        return v.reshape((16,) + v.shape[4:])

    def exchange_fsdp(self, v):
        if not self.cube:
            return lax.all_to_all(v, "fsdp", split_axis=0, concat_axis=0, tiled=True)
        shape = v.shape
        v = self.flips(v)
        both = jnp.stack([v[:, 0], self.swap_core(v[:, 1])], axis=1)
        return self.flips(jnp.stack([both[0], self.swap_y(both[1])]).reshape(shape)).reshape(shape)

    def scatter_small(self, v):
        if not self.cube or self.nz != 4:
            return lax.psum_scatter(v, "seq", scatter_dimension=0, tiled=False)
        z = lax.axis_index("seq")
        total = lax.dynamic_index_in_dim(v, z, 0, keepdims=False)
        for d in range(1, 4):
            other = lax.dynamic_index_in_dim(v, z ^ d, 0, keepdims=False)
            total = total + lax.ppermute(other, "seq", [(i, i ^ d) for i in range(4)])
        return total

    def to_owners_small(self, v):
        if not self.cube:
            v = lax.all_to_all(v, "fsdp", split_axis=0, concat_axis=0, tiled=True)
            v = lax.all_gather(v, "replica", axis=1, tiled=False)
            return jnp.stack([v[m // self.nr, m % self.nr] for m in self.place])
        v = self.flips(v)
        far = self.swap_core(v[:, 1])
        here = jnp.stack([v[0, 0], far[0]])
        there = jnp.stack([v[1, 0], far[1]])
        return jnp.stack(
            [here, self.swap_x(here), self.swap_y(there), self.swap_xy(there)], axis=1
        ).reshape((8,) + v.shape[2:])

    def to_owners(self, v):
        if not self.cube:
            return self.to_owners_small(v)
        nf, rows, columns = v.shape
        f = lax.axis_index("fsdp")
        pick = (f ^ jnp.arange(nf, dtype=jnp.int32)).astype(jnp.int32)
        pair = sds((2, rows, columns), BF)
        near, far = pl.pallas_call(
            pick_kernel,
            grid_spec=pltpu.PrefetchScalarGridSpec(
                num_scalar_prefetch=1,
                grid=(1,),
                in_specs=[pl.BlockSpec(v.shape, lambda i, s: (0, 0, 0))],
                out_specs=[pl.BlockSpec(pair.shape, lambda i, s: (0, 0, 0))] * 2,
            ),
            out_shape=[pair] * 2,
            compiler_params=pltpu.CompilerParams(vmem_limit_bytes=44 * 1024 * 1024),
        )(pick, v)
        here, there = call(pair_kernel, [pair] * 2, [], 0, [near, self.swap_core(far)])
        return [here, self.swap_x(here), self.swap_y(there), self.swap_xy(there)]


def pick_kernel(order, v, near, far):
    for y in range(2):
        near[y] = v[order[2 * y]]
        far[y] = v[order[2 * y + 1]]


def pair_kernel(near, far, here, there):
    for y, out in enumerate((here, there)):
        out[0] = near[y]
        out[1] = far[y]


def gather_seq(v, lead=False):
    if lead:
        return lax.all_gather(v[None], "seq", axis=1, tiled=True)[0]
    return lax.all_gather(v, "seq", axis=0, tiled=True)


def scatter_seq(v, lead=False):
    if lead:
        return lax.psum_scatter(v[None], "seq", scatter_dimension=1, tiled=True)[0]
    return lax.psum_scatter(v, "seq", scatter_dimension=0, tiled=True)


def call(kernel, outs, scratch, flops, operands, **more):
    params = pltpu.CompilerParams(vmem_limit_bytes=44 * 1024 * 1024)
    size = sum(math.prod(o.shape) * o.dtype.itemsize for o in list(outs) + list(operands))
    return pl.pallas_call(
        kernel,
        out_shape=tuple(outs),
        scratch_shapes=scratch,
        compiler_params=params,
        cost_estimate=pl.CostEstimate(
            flops=int(flops), bytes_accessed=int(size), transcendentals=0
        ),
        **more,
    )(*operands)


def lanes(columns):
    return -(-columns // 128) * 128


def widen(v):
    return jnp.pad(v, ((0, 0), (0, lanes(v.shape[1]) - v.shape[1])))


def sds(shape, dtype):
    return jax.ShapeDtypeStruct(shape, dtype)


def fold_kernel(near, far, own, to_x, to_y, to_xy):
    rows, columns = own.shape
    own[...] = near[:rows, :] + far[:rows, :columns].astype(F32)
    for i, out in ((1, to_x), (2, to_y), (3, to_xy)):
        at = slice(i * rows, (i + 1) * rows)
        out[:, :columns] = (near[at, :] + far[at, :columns].astype(F32)).astype(BF)


def wgrad_kernel(left, right, out):
    tall = out.shape[0]
    block = 256

    def body(i, carry):
        at = pl.ds(pl.multiple_of(i * block, block), block)
        out[at, :] = dot(left[:, at], right[...], 0, 0).astype(BF)
        return carry

    whole = tall // block
    lax.fori_loop(0, whole, body, 0)
    if tall % block:
        out[whole * block :, :] = dot(left[:, whole * block :], right[...], 0, 0).astype(BF)


def wgrad(plan, left, right):
    if not plan.cube:
        return dot(left, right, 0, 0).astype(BF)
    tall, width = left.shape[1], right.shape[1]
    return call(
        wgrad_kernel, [sds((tall, width), BF)], [], 2 * left.size * width, [left, right]
    )[0]


def after(v, other):
    return lax.optimization_barrier((v, other))[0]


def first_half(shape):
    return lax.broadcasted_iota(jnp.int32, shape, 1) < HD


def attend_kernel(count, total, span, scale, *refs):
    pieces = refs[:count]
    w, bias, code_col, code_row, full, packed, lse, mixed = refs[count:]
    rows = pieces[0].shape[0]
    for i, piece in enumerate(pieces):
        full[i * rows : (i + 1) * rows, :] = piece[:, : full.shape[1]]
    block = 2 * rows

    def project(i, carry):
        at = pl.ds(pl.multiple_of(i * block, block), block)
        packed[at, :] = (dot(full[at, :], w[...]) + bias[...]).astype(BF)
        return carry

    lax.fori_loop(0, count // 2, project, 0)
    blocks = total // rows
    left = first_half((rows, 2 * HD))
    lane = lax.broadcasted_iota(jnp.int32, (rows, 128), 1)

    def queries(i, carry):
        at = pl.ds(pl.multiple_of(i * rows, rows), rows)
        seq = i // blocks
        keys_at = pl.ds(pl.multiple_of(seq * total, total), total)
        code_q = code_col[at, :]
        code_k = code_row[pl.ds(seq, 1), :]
        allowed = (code_k <= code_q) & (code_k >= (code_q // CODE) * CODE)
        stats = jnp.zeros((rows, 128), F32)
        for pair in range(span // 128):
            q = packed[at, pair * 128 : pair * 128 + 128]
            k = packed[keys_at, span + pair * 128 : span + pair * 128 + 128]
            v = packed[keys_at, 2 * span + pair * 128 : 2 * span + pair * 128 + 128]
            both = []
            for side in range(2):
                own = left if side == 0 else ~left
                scores = dot(jnp.where(own, q, jnp.zeros_like(q)), k, 1, 1) * scale
                scores = jnp.where(allowed, scores, LOW)
                top = jnp.max(scores, axis=1, keepdims=True)
                expo = jnp.exp(scores - top)
                denom = jnp.sum(expo, axis=1, keepdims=True)
                probs = (expo * (1.0 / denom)).astype(BF)
                both.append(dot(probs, v))
                stats = jnp.where(lane == 2 * pair + side, top + jnp.log(denom), stats)
            mixed[at, pair * 128 : pair * 128 + 128] = jnp.where(left, both[0], both[1]).astype(BF)
        lse[:, at] = stats.T[: lse.shape[0], :]
        return carry

    lax.fori_loop(0, count, queries, 0)


def attend(plan, pieces, w, bias, codes, total, scale):
    rows, width = pieces[0].shape[0], w.shape[0]
    count, span = plan.group, plan.span
    if not plan.cube:
        full = jnp.concatenate(pieces)[:, :width]
        packed = (dot(full, w) + bias).astype(BF)
        q, k, v = (
            packed[:, i * span : (i + 1) * span].reshape(-1, total, plan.heads, HD)
            for i in range(3)
        )
        allowed = mask_of(codes, total)
        scores = jnp.einsum("sqhd,skhd->shqk", q, k, preferred_element_type=F32) * scale
        scores = jnp.where(allowed[:, None], scores, LOW)
        top = jnp.max(scores, axis=-1, keepdims=True)
        expo = jnp.exp(scores - top)
        denom = jnp.sum(expo, axis=-1, keepdims=True)
        probs = (expo / denom).astype(BF)
        mixed = jnp.einsum("shqk,skhd->sqhd", probs, v, preferred_element_type=F32)
        return full, packed, top + jnp.log(denom), mixed.reshape(-1, span).astype(BF)
    tall = count * rows
    return call(
        functools.partial(attend_kernel, count, total, span, scale),
        [
            sds((tall, width), BF),
            sds((tall, 3 * span), BF),
            sds((8, tall), F32),
            sds((tall, span), BF),
        ],
        [],
        2 * tall * width * 3 * span + 8 * tall * total * span,
        [*pieces, w, bias[None], codes.reshape(-1, 1), codes.reshape(-1, total)],
    )


def mask_of(codes, total):
    code = codes.reshape(-1, total)
    low = (code // CODE) * CODE
    return (code[:, None, :] <= code[:, :, None]) & (code[:, None, :] >= low[:, :, None])


def attend_back_kernel(count, total, span, scale, *refs):
    pieces = refs[:count]
    packed, lse, code_col, code_row, w, g_packed, g_bias, near, far, gm, g_k, g_v = refs[count:]
    rows = pieces[0].shape[0]
    for i, piece in enumerate(pieces):
        gm[i * rows : (i + 1) * rows, :] = piece[...]
    blocks = total // rows
    left = first_half((rows, 2 * HD))

    def sequence(seq, carry):
        keys_at = pl.ds(pl.multiple_of(seq * total, total), total)
        code_k = code_col[keys_at, :]
        for pair in range(span // 128):
            lanes = slice(pair * 128, pair * 128 + 128)
            k_lanes = slice(span + pair * 128, span + pair * 128 + 128)
            v_lanes = slice(2 * span + pair * 128, 2 * span + pair * 128 + 128)
            k = packed[keys_at, k_lanes]
            v = packed[keys_at, v_lanes]
            g_k[...] = jnp.zeros_like(g_k)
            g_v[...] = jnp.zeros_like(g_v)

            def queries(i, inner):
                at = pl.ds(pl.multiple_of(seq * total + i * rows, rows), rows)
                code_q = code_row[pl.ds(seq * blocks + i, 1), :]
                allowed = (code_k <= code_q) & (code_k >= (code_q // CODE) * CODE)
                q = packed[at, lanes]
                g = gm[at, lanes]
                both = []
                for side in range(2):
                    own = left if side == 0 else ~left
                    q_own = jnp.where(own, q, jnp.zeros_like(q))
                    g_own = jnp.where(own, g, jnp.zeros_like(g))
                    scores = dot(k, q_own, 1, 1) * scale
                    row = 2 * pair + side
                    probs = jnp.exp(jnp.where(allowed, scores, LOW) - lse[row : row + 1, at])
                    g_probs = dot(v, g_own, 1, 1)
                    each = jnp.sum(g_probs * probs, axis=0, keepdims=True)
                    g_scores = (probs * (g_probs - each)).astype(BF)
                    g_v[...] += dot(probs.astype(BF), g_own)
                    g_k[...] += dot(g_scores, q_own)
                    both.append(dot(g_scores, k, 0, 0))
                g_packed[at, lanes] = (jnp.where(left, both[0], both[1]) * scale).astype(BF)
                return inner

            lax.fori_loop(0, blocks, queries, 0)
            g_packed[keys_at, k_lanes] = (g_k[...] * scale).astype(BF)
            g_packed[keys_at, v_lanes] = g_v[...].astype(BF)
        return carry

    lax.fori_loop(0, count // blocks, sequence, 0)
    g_bias[...] = jnp.sum(g_packed[...].astype(F32), axis=0, keepdims=True)
    spread_out(g_packed, w, near, far, 2 * rows)


def spread_out(left, right, near, far, block):
    half = near.shape[0]

    def first(i, carry):
        at = pl.ds(pl.multiple_of(i * block, block), block)
        near[at, :] = dot(left[at, :], right[...], 1, 1)
        return carry

    def second(i, carry):
        at = pl.ds(pl.multiple_of(i * block, block), block)
        far[at, : near.shape[1]] = dot(
            left[pl.ds(pl.multiple_of(half + i * block, block), block), :], right[...], 1, 1
        ).astype(BF)
        return carry

    lax.fori_loop(0, half // block, first, 0)
    lax.fori_loop(0, half // block, second, 0)


def halves(v):
    half = v.shape[0] // 2
    return v[:half], v[half:].astype(BF)


def attend_back(plan, pieces, packed, lse, codes, w, total, scale):
    count, span = plan.group, plan.span
    rows = pieces[0].shape[0]
    width = w.shape[0]
    if not plan.cube:
        q, k, v = (
            packed[:, i * span : (i + 1) * span].reshape(-1, total, plan.heads, HD)
            for i in range(3)
        )
        gm = jnp.concatenate(pieces).reshape(-1, total, plan.heads, HD)
        allowed = mask_of(codes, total)
        scores = jnp.einsum("sqhd,skhd->shqk", q, k, preferred_element_type=F32) * scale
        probs = jnp.exp(jnp.where(allowed[:, None], scores, LOW) - lse)
        g_probs = jnp.einsum("sqhd,skhd->shqk", gm, v, preferred_element_type=F32)
        g_v = jnp.einsum("shqk,sqhd->skhd", probs.astype(BF), gm, preferred_element_type=F32)
        row = jnp.sum(g_probs * probs, axis=-1, keepdims=True)
        g_s = (probs * (g_probs - row)).astype(BF)
        g_q = jnp.einsum("shqk,skhd->sqhd", g_s, k, preferred_element_type=F32) * scale
        g_k = jnp.einsum("shqk,sqhd->skhd", g_s, q, preferred_element_type=F32) * scale
        g_packed = jnp.concatenate(
            [u.reshape(-1, span).astype(BF) for u in (g_q, g_k, g_v)], axis=1
        )
        near, far = halves(dot(g_packed, w, 1, 1))
        return g_packed, jnp.sum(g_packed.astype(F32), axis=0), near, far
    tall = count * rows
    g_packed, g_bias, near, far = call(
        functools.partial(attend_back_kernel, count, total, span, scale),
        [
            sds((tall, 3 * span), BF),
            sds((1, 3 * span), F32),
            sds((tall // 2, width), F32),
            sds((tall // 2, lanes(width)), BF),
        ],
        [pltpu.VMEM((tall, span), BF)] + [pltpu.VMEM((total, 128), F32)] * 2,
        2 * tall * width * 3 * span + 20 * tall * total * span,
        [*pieces, packed, lse, codes.reshape(-1, 1), codes.reshape(-1, rows), w],
    )
    return g_packed, g_bias[0], near, far


def hidden_kernel(count, *refs):
    pieces = refs[:count]
    up, bias, down, full, slope, activated, near, far = refs[count:]
    rows = pieces[0].shape[0]
    for i, piece in enumerate(pieces):
        full[i * rows : (i + 1) * rows, :] = piece[:, : full.shape[1]]
    block = 2 * rows
    half = near.shape[0]

    def lift(at):
        value, pull = gelu_both(dot(full[at, :], up[...]) + bias[...])
        value = value.astype(BF)
        activated[at, :] = value
        slope[at, :] = pull.astype(BF)
        return dot(value, down[...])

    def first(i, carry):
        at = pl.ds(pl.multiple_of(i * block, block), block)
        near[at, :] = lift(at)
        return carry

    def second(i, carry):
        at = pl.ds(pl.multiple_of(i * block, block), block)
        out = lift(pl.ds(pl.multiple_of(half + i * block, block), block))
        far[at, : near.shape[1]] = out.astype(BF)
        return carry

    lax.fori_loop(0, half // block, first, 0)
    lax.fori_loop(0, half // block, second, 0)


def hidden_units(plan, pieces, up, bias, down):
    rows, width = pieces[0].shape[0], up.shape[0]
    if not plan.cube:
        full = jnp.concatenate(pieces)[:, :width]
        value, pull = gelu_both(dot(full, up) + bias)
        value = value.astype(BF)
        return (full, pull.astype(BF), value) + halves(dot(value, down))
    tall, units = plan.group * rows, up.shape[1]
    return call(
        functools.partial(hidden_kernel, plan.group),
        [
            sds((tall, width), BF),
            sds((tall, units), BF),
            sds((tall, units), BF),
            sds((tall // 2, width), F32),
            sds((tall // 2, lanes(width)), BF),
        ],
        [],
        4 * tall * width * units,
        [*pieces, up, bias[None], down],
    )


def hidden_back_kernel(count, *refs):
    pieces = refs[:count]
    slope, down, up, g_lift, g_bias, near, far, full = refs[count:]
    rows = pieces[0].shape[0]
    for i, piece in enumerate(pieces):
        full[i * rows : (i + 1) * rows, :] = piece[:, : full.shape[1]]
    block = 2 * rows

    def pull(i, carry):
        at = pl.ds(pl.multiple_of(i * block, block), block)
        g_lift[at, :] = (dot(full[at, :], down[...], 1, 1) * slope[at, :].astype(F32)).astype(BF)
        return carry

    lax.fori_loop(0, count // 2, pull, 0)
    spread_out(g_lift, up, near, far, block)
    g_bias[...] = jnp.sum(g_lift[...].astype(F32), axis=0, keepdims=True)


def hidden_back(plan, pieces, slope, down, up):
    rows, width = pieces[0].shape[0], up.shape[0]
    if not plan.cube:
        full = jnp.concatenate(pieces)[:, :width]
        g_lift = (dot(full, down, 1, 1) * slope.astype(F32)).astype(BF)
        return (g_lift, jnp.sum(g_lift.astype(F32), axis=0)) + halves(dot(g_lift, up, 1, 1))
    tall, units = plan.group * rows, up.shape[1]
    g_lift, g_bias, near, far = call(
        functools.partial(hidden_back_kernel, plan.group),
        [
            sds((tall, units), BF),
            sds((1, units), F32),
            sds((tall // 2, width), F32),
            sds((tall // 2, lanes(width)), BF),
        ],
        [pltpu.VMEM((tall, width), BF)],
        4 * tall * width * units,
        [*pieces, slope, down, up],
    )
    return g_lift, g_bias[0], near, far


def down_grad_kernel(count, *refs):
    left, out, full = refs[count:]
    rows = refs[0].shape[0]
    for i, piece in enumerate(refs[:count]):
        full[i * rows : (i + 1) * rows, :] = piece[:, : full.shape[1]]
    wgrad_kernel(left, full, out)


def down_grad(plan, left, pieces, width):
    if not plan.cube:
        return dot(left, jnp.concatenate(pieces)[:, :width], 0, 0).astype(BF)
    tall, units = left.shape
    return call(
        functools.partial(down_grad_kernel, plan.group),
        [sds((units, width), BF)],
        [pltpu.VMEM((tall, width), BF)],
        2 * left.size * width,
        [*pieces, left],
    )[0]


def head_columns_kernel(nf, ranks, span, x_ref, w_ref, out, wide):
    width = w_ref.shape[2] // 3
    padded = wide.shape[1] // 3
    w = w_ref[0].astype(F32)
    for i in range(3):
        wide[:, i * padded : i * padded + width] = w[:, i * width : (i + 1) * width]
        if padded > width:
            wide[:, i * padded + width : (i + 1) * padded] = jnp.zeros(
                (wide.shape[0], padded - width), F32
            )
    for x, row in enumerate(ranks):

        @pl.when(x_ref[0] == x)
        def _():
            for f in range(nf):
                for i in range(3):
                    start = i * padded + row[f] * span
                    out[0, f, :, i * span : (i + 1) * span] = wide[:, start : start + span].astype(
                        BF
                    )


def unit_columns_kernel(nz, nf, nr, piece, piece_rows, x_ref, w_ref, out):
    w = w_ref[0].astype(F32)
    for x in range(nr):

        @pl.when(x_ref[0] == x)
        def _():
            for f in range(nf):
                part = []
                for z in range(nz):
                    start = ((z * nf + f) * nr + x) * piece
                    part.append(w[:, start : start + piece])
                    if piece_rows > piece:
                        part.append(jnp.zeros((w.shape[0], piece_rows - piece), F32))
                out[0, f] = jnp.concatenate(part, axis=1).astype(BF)


def layered(kernel, x, w, columns, nf, scratch):
    layers, rows, full = w.shape
    return pl.pallas_call(
        kernel,
        grid_spec=pltpu.PrefetchScalarGridSpec(
            num_scalar_prefetch=1,
            grid=(layers,),
            in_specs=[pl.BlockSpec((1, rows, full), lambda i, s: (i, 0, 0))],
            out_specs=pl.BlockSpec((1, nf, rows, columns), lambda i, s: (i, 0, 0, 0)),
            scratch_shapes=scratch,
        ),
        out_shape=sds((layers, nf, rows, columns), BF),
        compiler_params=pltpu.CompilerParams(vmem_limit_bytes=44 * 1024 * 1024),
        cost_estimate=pl.CostEstimate(flops=0, bytes_accessed=4 * w.size, transcendentals=0),
    )(x, w)


def head_columns(plan, w):
    layers, rows, triple = w.shape
    nf, nr, span, group = plan.nf, plan.nr, plan.span, plan.group
    ranks = [[plan.rank_of(f, r) for f in range(nf)] for r in range(nr)]
    x = lax.axis_index("replica")
    if not plan.cube:
        width = triple // 3
        v = w.reshape(layers, rows, 3, width)
        v = jnp.pad(v, ((0, 0), (0, 0), (0, 0), (0, group * span - width)))
        v = jnp.take(v.reshape(layers, rows, 3, group, span), jnp.array(ranks)[x], axis=3)
        return v.transpose(0, 3, 1, 2, 4).reshape(layers, nf, rows, 3 * span)
    return layered(
        functools.partial(head_columns_kernel, nf, ranks, span),
        x.astype(jnp.int32).reshape(1),
        w,
        3 * span,
        nf,
        [pltpu.VMEM((rows, 3 * group * span), F32)],
    )


def unit_columns(plan, w, piece, piece_rows):
    layers, rows, _ = w.shape
    nz, nf, nr = plan.nz, plan.nf, plan.nr
    x = lax.axis_index("replica")
    if not plan.cube:
        v = w.reshape(layers, rows, nz, nf, nr, piece)
        v = lax.dynamic_index_in_dim(v, x, 4, keepdims=False)
        v = jnp.pad(v, ((0, 0),) * 4 + ((0, piece_rows - piece),))
        return v.transpose(0, 3, 1, 2, 4).reshape(layers, nf, rows, nz * piece_rows)
    return layered(
        functools.partial(unit_columns_kernel, nz, nf, nr, piece, piece_rows),
        x.astype(jnp.int32).reshape(1),
        w,
        nz * piece_rows,
        nf,
        [],
    )


def stacked(pairs, block):
    for i, pair in enumerate(pairs):
        for core in range(2):
            block[4 * core + i] = pair[core]


def heads_back_kernel(group, span, src_ref, *refs):
    out, wide, v_ref = refs[-3:]
    stacked(refs[:4], v_ref)
    width = out.shape[2] // 3
    padded = group * span
    for rank in range(group):
        block = v_ref[src_ref[rank]].astype(F32)
        for i in range(3):
            wide[:, i * padded + rank * span : i * padded + (rank + 1) * span] = block[
                :, i * span : (i + 1) * span
            ]
    for i in range(3):
        out[0, :, i * width : (i + 1) * width] = wide[:, i * padded : i * padded + width]


def units_back_kernel(nz, nf, nr, piece, piece_rows, ranks, src_ref, *refs):
    out, v_ref = refs[-2:]
    stacked(refs[:4], v_ref)
    for f in range(nf):
        blocks = [v_ref[src_ref[ranks[f][r]]].astype(F32) for r in range(nr)]
        for z in range(nz):
            part = [block[:, z * piece_rows : z * piece_rows + piece] for block in blocks]
            start = (z * nf + f) * nr * piece
            out[0, :, start : start + nr * piece] = jnp.concatenate(part, axis=1)


def into_layer(kernel, plan, pairs, shape, layer, previous, scratch):
    operands = [plan.source().astype(jnp.int32), *pairs]
    in_specs = [pl.BlockSpec(v.shape, lambda i, s: (0, 0, 0)) for v in pairs]
    scratch = scratch + [pltpu.VMEM((8,) + pairs[0].shape[1:], BF)]
    aliases = {}
    if previous is not None:
        operands.append(previous)
        in_specs.append(pl.BlockSpec(memory_space=pl.ANY))
        aliases = {5: 0}
    return pl.pallas_call(
        kernel,
        grid_spec=pltpu.PrefetchScalarGridSpec(
            num_scalar_prefetch=1,
            grid=(1,),
            in_specs=in_specs,
            out_specs=pl.BlockSpec((1,) + shape[1:], lambda i, s: (layer, 0, 0)),
            scratch_shapes=scratch,
        ),
        out_shape=sds(shape, F32),
        input_output_aliases=aliases,
        compiler_params=pltpu.CompilerParams(vmem_limit_bytes=44 * 1024 * 1024),
        cost_estimate=pl.CostEstimate(flops=0, bytes_accessed=48 * pairs[0].size, transcendentals=0),
    )(*operands)


def rows_back_kernel(kept, x_ref, own, other, own_out, other_out, *refs):
    down, out = refs[-2:]
    units = down.shape[1] // 2
    for x in range(2):

        @pl.when(x_ref[0] == x)
        def _():
            first, second = (own, other) if x == 0 else (other, own)
            down[0, :units, :] = first[:units, :].astype(F32)
            down[0, units:, :] = second[:units, :].astype(F32)
            first, second = (own_out, other_out) if x == 0 else (other_out, own_out)
            out[0] = jnp.concatenate(
                [first[...].astype(F32)[:kept], second[...].astype(F32)[:kept]]
            )


def shards(
    plan,
    tokens,
    cotangent,
    segments,
    norm1_gain,
    norm1_shift,
    w_qkv,
    b_query,
    b_value,
    w_out,
    b_out,
    norm2_gain,
    norm2_shift,
    w_up,
    b_up,
    w_down,
    b_down,
):
    nz, nf, nr, group, span = plan.nz, plan.nf, plan.nr, plan.group, plan.span
    layers, own_rows, triple = w_qkv.shape
    width = triple // 3
    own_hidden = w_down.shape[1]
    piece = own_hidden // nr
    part = -(-own_rows // nr)
    part_rows = -(-part // 16) * 16
    piece_rows = -(-piece // 16) * 16
    units = nz * piece_rows
    length = tokens.shape[1]
    total = length * nz
    scale = 1.0 / math.sqrt(HD)
    fsdp = lax.axis_index("fsdp")
    replica = lax.axis_index("replica")
    seq = lax.axis_index("seq")
    rank = plan.rank()

    def rest_of(down, out):
        down = lax.dynamic_slice_in_dim(down, replica * piece, piece, 0)
        down = jnp.pad(down, ((0, piece_rows - piece), (0, 0)))
        out = jnp.pad(out, ((0, nr * part + part_rows - own_rows), (0, 0)))
        out = lax.dynamic_slice_in_dim(out, replica * part, part_rows, 0)
        valid = lax.broadcasted_iota(jnp.int32, out.shape, 0)
        valid = (valid < part) & (valid + replica * part < own_rows)
        return jnp.concatenate([down, jnp.where(valid, out, jnp.zeros_like(out))])

    qkv_send = head_columns(plan, w_qkv)
    first = plan.exchange_fsdp(qkv_send[0]).reshape(nf * own_rows, 3 * span)
    both = plan.regroup(jnp.concatenate([tokens[0], cotangent[0]]))
    small = jnp.concatenate(
        [norm1_gain, norm1_shift, b_query, b_value, b_out, norm2_gain, norm2_shift, b_down, b_up],
        axis=1,
    )
    each_small = small.shape[1]
    small = small.reshape(-1)
    flat_rows = -(-small.shape[0] // 2048) * 16
    small = jnp.pad(small, (0, flat_rows * 128 - small.shape[0])).reshape(flat_rows, 128)
    small = plan.gather_owners(small)
    small = small.reshape(nz * nf, flat_rows * 128)[:, : layers * each_small]
    small = small.reshape(nz * nf, layers, each_small)

    codes = segments[0] * CODE + seq * length + jnp.arange(length, dtype=jnp.int32)
    codes = plan.gather_doubling(plan.regroup(codes[None]))

    first, both, qkv_send, w_up, w_down, w_out, small, codes = lax.optimization_barrier(
        (first, both, qkv_send, w_up, w_down, w_out, small, codes)
    )
    hidden = both[:length].astype(F32)
    grad = both[length:].astype(F32)
    up_send = unit_columns(plan, w_up, piece, piece_rows)
    prepared = []
    for layer in range(layers):
        qkv = first
        if layer:
            qkv = plan.exchange_fsdp(qkv_send[layer]).reshape(nf * own_rows, 3 * span)
        up = plan.exchange_fsdp(up_send[layer]).reshape(nf * own_rows, units)
        prepared.append((qkv, up, rest_of(w_down[layer], w_out[layer])))
    early = [prepared[0][1:], prepared[1:]]
    codes, early = lax.optimization_barrier((codes, early))
    prepared = [(first, *early[0])] + early[1]

    def fetch(layer):
        qkv, up, rest = prepared[layer]
        qkv = gather_seq(qkv)
        rest = gather_seq(rest, lead=layer % 2 == 0)
        up = gather_seq(up)
        return qkv, rest, up

    def unpack(rest):
        rest = rest.reshape(nz, piece_rows + part_rows, width)
        down = rest[:, :piece_rows].reshape(units, width)
        out = rest[:, piece_rows:].reshape(nz * part_rows, width)
        return jnp.concatenate(plan.gather_pieces(out)), down

    source = plan.source()
    feature_heads = (source[:, None] * span + jnp.arange(span, dtype=jnp.int32)).reshape(-1)
    fs = jnp.array(plan.place, dtype=jnp.int32)[source]
    inner = jnp.arange(part_rows, dtype=jnp.int32)
    within = (fs % nr)[:, None, None] * part + inner
    feature_rows = (
        jnp.arange(nz, dtype=jnp.int32)[None, :, None] * (nf * own_rows)
        + (fs // nr)[:, None, None] * own_rows
        + within
    )
    feature_rows = jnp.where((inner < part) & (within < own_rows), feature_rows, -1).reshape(-1)
    select = (feature_heads[:, None] == feature_rows[None, :]).astype(BF)

    def vectors(layer):
        each = [
            small[:, layer, i * own_rows : (i + 1) * own_rows].reshape(width).astype(F32)
            for i in range(8)
        ]
        bias_up = small[:, layer, 8 * own_rows :].reshape(nz, nf, nr, piece)
        bias_up = lax.dynamic_index_in_dim(bias_up, fsdp, 1, keepdims=False)
        bias_up = lax.dynamic_index_in_dim(bias_up, replica, 1, keepdims=False)

        def mine(v):
            return lax.dynamic_slice_in_dim(
                jnp.pad(v, (0, group * span - width)), rank * span, span
            )

        bias_qkv = jnp.concatenate([mine(each[2]), jnp.zeros((span,), F32), mine(each[3])])
        bias_up = jnp.pad(bias_up, ((0, 0), (0, piece_rows - piece)))
        return each, bias_qkv, bias_up.reshape(units).astype(F32)

    vecs = [vectors(layer) for layer in range(layers)]

    weights = [fetch(layer) for layer in range(layers)]

    kept = []
    for layer in range(layers):
        qkv_w, rest, up_w = weights[layer]
        (gain1, shift1, _, _, bias_out, gain2, shift2, bias_down), bias_qkv, bias_up = vecs[layer]
        unit1, inv1 = norm_parts(hidden)
        pieces = plan.gather_pieces(widen((unit1 * gain1 + shift1).astype(BF)))
        if layer == layers - 1:
            grad_pieces = plan.gather_pieces(widen(grad.astype(BF)))
            pieces, grad_pieces = lax.optimization_barrier((pieces, grad_pieces))
        normed, packed, lse, mixed = attend(
            plan, pieces, qkv_w, bias_qkv, codes, total, scale
        )
        out_w, down_w = unpack(after(rest, packed))
        weights[layer] = qkv_w, out_w, up_w, down_w
        mixed = jnp.concatenate(plan.exchange(mixed), axis=1)
        mixed = dot(mixed, select).astype(BF)
        block = nz * part_rows
        mixed_own = plan.exchange(
            jnp.concatenate([mixed[:, i * block : (i + 1) * block] for i in range(group)])
        )
        middle = hidden + (dot(mixed, out_w) + bias_out)
        unit2, inv2 = norm_parts(middle)
        pieces = plan.gather_pieces(widen((unit2 * gain2 + shift2).astype(BF)))
        normed_two, slope, activated, near, far = hidden_units(plan, pieces, up_w, bias_up, down_w)
        kept.append(
            (
                unit1,
                inv1,
                normed,
                packed,
                lse,
                jnp.concatenate(mixed_own),
                unit2,
                inv2,
                normed_two,
                slope,
                activated,
            )
        )
        if layer < layers - 1:
            hidden = middle + (plan.scatter_parts(near, far) + bias_down)
    hidden = middle + (plan.scatter_parts(near, far) + bias_down)
    output = plan.regroup(hidden.astype(BF), back=True)

    def late_up(layer, up, rest, qkv):
        up = plan.to_owners(up)
        if plan.cube:
            ranks = [[plan.rank_of(f, r) for r in range(nr)] for f in range(nf)]
            return into_layer(
                functools.partial(units_back_kernel, nz, nf, nr, piece, piece_rows, ranks),
                plan,
                up,
                (layers, own_rows, nf * nz * nr * piece),
                layer,
                into_up,
                [],
            )
        up = jnp.stack([up[plan.back[m]] for m in range(group)])
        up = up.reshape(nf, nr, own_rows, nz, piece_rows)[..., :piece].transpose(2, 3, 0, 1, 4)
        up = up.reshape(1, own_rows, -1).astype(F32)
        return up if into_up is None else jnp.concatenate([up, into_up])

    def late_qkv(layer, up, rest, qkv):
        qkv = plan.to_owners(qkv)
        if plan.cube:
            return into_layer(
                functools.partial(heads_back_kernel, group, span),
                plan,
                qkv,
                (layers, own_rows, triple),
                layer,
                into_qkv,
                [pltpu.VMEM((own_rows, 3 * group * span), F32)],
            )
        qkv = qkv.reshape(group, own_rows, 3, span).transpose(1, 2, 0, 3)
        qkv = qkv.reshape(own_rows, 3, group * span)[:, :, :width]
        qkv = qkv.reshape(1, own_rows, triple).astype(F32)
        return qkv if into_qkv is None else jnp.concatenate([qkv, into_qkv])

    def late_rest(layer, up, rest, qkv):
        down, out = rest
        if not plan.cube:
            down = lax.all_gather(down, "replica", axis=0, tiled=False)
            out = lax.all_gather(out, "replica", axis=0, tiled=False)
            down = down[:, :piece].reshape(1, own_hidden, width).astype(F32)
            out = out[:, :part].reshape(nr * part, width)[None, :own_rows].astype(F32)
            if into_down is None:
                return down, out
            return jnp.concatenate([down, into_down]), jnp.concatenate([out, into_out])
        operands = [down, plan.swap_x(down), out, plan.swap_x(out)]
        in_specs = [pl.BlockSpec(v.shape, lambda i, s: (0, 0)) for v in operands]
        operands = [replica.astype(jnp.int32).reshape(1)] + operands
        aliases = {}
        if into_down is not None:
            operands += [into_down, into_out]
            in_specs += [pl.BlockSpec(memory_space=pl.ANY)] * 2
            aliases = {5: 0, 6: 1}
        return pl.pallas_call(
            functools.partial(rows_back_kernel, part),
            grid_spec=pltpu.PrefetchScalarGridSpec(
                num_scalar_prefetch=1,
                grid=(1,),
                in_specs=in_specs,
                out_specs=[
                    pl.BlockSpec((1, own_hidden, width), lambda i, s: (layer, 0, 0)),
                    pl.BlockSpec((1, own_rows, width), lambda i, s: (layer, 0, 0)),
                ],
            ),
            out_shape=[
                sds((layers, own_hidden, width), F32),
                sds((layers, own_rows, width), F32),
            ],
            input_output_aliases=aliases,
            compiler_params=pltpu.CompilerParams(vmem_limit_bytes=44 * 1024 * 1024),
            cost_estimate=pl.CostEstimate(
                flops=0, bytes_accessed=12 * down.size, transcendentals=0
            ),
        )(*operands)

    into_qkv = into_up = into_down = into_out = None
    smalls = [None] * layers
    late = None
    for layer in reversed(range(layers)):
        qkv_w, out_w, up_w, down_w = weights[layer]
        (gain1, _, _, _, _, gain2, _, _), _, _ = vecs[layer]
        unit1, inv1, normed, packed, lse, mixed, unit2, inv2, normed_two, slope, activated = kept[
            layer
        ]
        g_low = grad.astype(BF)
        grad_down = down_grad(plan, activated, grad_pieces, width)
        if late is not None:
            out = scatter_seq(down_grad(plan, *late[2][1], width))
            late = (late[0], late[1], (late[2][0], out), late[3])
            into_up = late_up(*late)
            into_down, into_out = late_rest(*late)
        if late is None:
            grad_pieces, grad_down = lax.optimization_barrier((grad_pieces, grad_down))
        down = scatter_seq(grad_down, lead=True)
        g_lift, grad_b_up, near, far = hidden_back(
            plan, grad_pieces, slope, down_w, up_w
        )
        grad_up = wgrad(plan, normed_two, g_lift)
        g_n2 = plan.scatter_parts(near, far)
        up = scatter_seq(grad_up).reshape(nf, own_rows, units)
        g_mid = grad + norm_pull(g_n2, unit2, inv2, gain2)
        g_att = g_mid.astype(BF)
        g_mixed = dot(g_att, out_w, 1, 1).astype(BF)
        g_mixed = dot(g_mixed, select, 1, 1).astype(BF)
        g_mixed = jnp.concatenate(
            [g_mixed[:, i * span : (i + 1) * span] for i in range(group)]
        )
        g_mixed = plan.exchange(g_mixed)
        att_pieces = plan.gather_pieces(widen(g_att))
        g_packed, g_b, near, far = attend_back(
            plan, g_mixed, packed, lse, codes, qkv_w, total, scale
        )
        grad_qkv = wgrad(plan, normed, g_packed)
        g_n1 = plan.scatter_parts(near, far)
        qkv = scatter_seq(grad_qkv)
        qkv = qkv.reshape(nf, own_rows, 3 * span)
        if late is not None:
            into_qkv = late_qkv(*late[:3], after(late[3], g_n1))
        late = (layer, up, (down, (after(mixed, g_n1), att_pieces)), qkv)
        smalls[layer] = (
            jnp.sum(g_n1 * unit1, axis=0),
            jnp.sum(g_n1, axis=0),
            g_b,
            jnp.sum(g_att.astype(F32), axis=0),
            jnp.sum(g_n2 * unit2, axis=0),
            jnp.sum(g_n2, axis=0),
            jnp.sum(g_low.astype(F32), axis=0),
            grad_b_up,
        )
        grad = g_mid + norm_pull(g_n1, unit1, inv1, gain1)
        if layer:
            grad_pieces = plan.gather_pieces(widen(grad.astype(BF)))
    out = scatter_seq(down_grad(plan, *late[2][1], width))
    late = (late[0], late[1], (late[2][0], out), late[3])
    grad_tokens = plan.regroup(grad.astype(BF), back=True).astype(F32)
    output = after(output, grad).astype(F32)
    into_up = late_up(*late)
    into_down, into_out = late_rest(*late)
    into_qkv = late_qkv(*late)

    def scattered(layer):
        n1g, n1s, g_b, b_o, n2g, n2s, b_d, b_u = smalls[layer]

        def place(v):
            full = lax.dynamic_update_slice_in_dim(
                jnp.zeros((group * span,), F32), v, rank * span, 0
            )
            return full[:width]

        b_u = lax.dynamic_update_slice(
            jnp.zeros((nz, nf, nr, piece), F32),
            b_u.reshape(nz, 1, 1, piece_rows)[..., :piece],
            (0, fsdp, replica, 0),
        )
        rows = [n1g, n1s, place(g_b[:span]), place(g_b[2 * span :]), b_o, n2g, n2s, b_d]
        return jnp.concatenate(
            [v.reshape(nz * nf, own_rows) for v in rows] + [b_u.reshape(nz * nf, own_hidden)],
            axis=1,
        )

    flat = jnp.concatenate([scattered(layer) for layer in range(layers)], axis=1)
    wide = lanes(-(-flat.shape[1] // 2))
    flat = jnp.pad(flat, ((0, 0), (0, 2 * wide - flat.shape[1])))
    flat = plan.scatter_small(flat.reshape(nz, nf, 2, wide))
    flat = jnp.sum(plan.to_owners_small(flat), axis=0).reshape(-1)
    flat = flat[: layers * each_small].reshape(layers, each_small)
    vec = [flat[:, i * own_rows : (i + 1) * own_rows] for i in range(8)]
    return (
        output[None],
        grad_tokens[None],
        vec[0],
        vec[1],
        into_qkv,
        vec[2],
        vec[3],
        into_out,
        vec[4],
        vec[5],
        vec[6],
        into_up,
        flat[:, 8 * own_rows :],
        into_down,
        vec[7],
    )


def solution(mesh):
    plan = Plan(mesh)
    data = P(("fsdp", "replica"), "seq", None)
    vector = P(None, ("seq", "fsdp"))
    matrix = P(None, ("seq", "fsdp"), None)
    weights = (
        vector,
        vector,
        matrix,
        vector,
        vector,
        matrix,
        vector,
        vector,
        vector,
        matrix,
        vector,
        matrix,
        vector,
    )
    in_specs = (data, data, P(("fsdp", "replica"), "seq")) + weights
    out_specs = (data, data) + weights
    return jax.shard_map(
        functools.partial(shards, plan),
        mesh=mesh,
        in_specs=in_specs,
        out_specs=out_specs,
        check_vma=False,
    )
```

time: 1520 us -> 1090 us (0.72)
  Pallas kernels: 0 us -> 205 us
  local copies, waits for them, and re-layouts: 378 us -> 192 us
  blocking collectives: 173 us -> 0 us
  matrix products: 166 us -> 34.7 us
  other arithmetic: 176 us -> 50.1 us
  waiting for transfers between devices: 421 us -> 403 us
    pallas_call x0 -> x38, Pallas kernels: none -> 205 us  [the longest x26 184 us: call(): pl.pallas_call(kernel, out_shape=tuple(outs), scratch_shapes=scratch, com...]
    all_gather x3 -> x0, blocking collectives: 164 us -> none  [the longest x2 141 us: gather_seq(): return lax.all_gather(v, 'seq', axis=0, tiled=True)]
    ppermute x4 -> x27, waiting for transfers between devices: 2.79 us -> 101 us  [swap_xy(): return lax.ppermute(v, GROUP, pairs)]
    dot_general x24 -> x6, matrix products: 133 us -> 34.7 us  [dot(): lax.dot_general(a, b, (((ca,), (cb,)), ((), ())), preferred_element_type=...]
    unnamed x20 -> x14, waiting for transfers between devices: 93.3 us -> 0.86 us
    concatenate x24 -> x6, local copies, waits for them, and re-layouts: 76.4 us -> 5.22 us  [the longest x2 3.1 us: unpack(): return (jnp.concatenate(plan.gather_pieces(out)), down)]
    another operation x42 -> x18, local copies, waits for them, and re-layouts: 67.8 us -> 4.59 us  [the longest x2 2.3 us: shards(): up = plan.exchange_fsdp(up_send[layer]).reshape(nf * own_rows, units)]
    ppermute x4 -> x27, starting transfers between devices: 3.31 us -> 61 us  [swap_xy(): return lax.ppermute(v, GROUP, pairs)]
  transfers between devices with their start and end apart: 135 -> 179, of which waited for: 66 -> 65; matrix products, arithmetic and copies ran while one was open for 40% -> 20% of each run, Pallas kernels for 0% -> 15%
where the time goes in v2:
time: 1090 us; the launch traced here: 1070 us
  waiting for transfers between devices  403 us (37%)
  Pallas kernels  205 us (19%)
  local copies, waits for them, and re-layouts  192 us (18%)
  starting transfers between devices  172 us (16%)
  other arithmetic  50.1 us (5%)
  matrix products  34.7 us (3%)
  between operations  16.8 us (2%)
    pallas_call x26, Pallas kernels, call(): pl.pallas_call(kernel, out_shape=tuple(outs), scratch_shapes=scratch, com...  184 us
    ppermute x33, waiting for transfers between devices, swap_y(): return lax.ppermute(v, 'fsdp', [(f, f ^ 2) for f in range(self.nf)])  134 us
    ppermute x32, waiting for transfers between devices, swap_x(): return lax.ppermute(v, 'replica', [(r, r ^ 1) for r in range(self.nr)])  128 us
    unnamed x324, local copies, waits for them, and re-layouts  106 us
    ppermute x27, waiting for transfers between devices, swap_xy(): return lax.ppermute(v, GROUP, pairs)  101 us
    ppermute x27, starting transfers between devices, swap_xy(): return lax.ppermute(v, GROUP, pairs)  61 us
    ppermute x33, starting transfers between devices, swap_y(): return lax.ppermute(v, 'fsdp', [(f, f ^ 2) for f in range(self.nf)])  39.4 us
    dot_general x6, matrix products, dot(): lax.dot_general(a, b, (((ca,), (cb,)), ((), ())), preferred_element_type=...  34.7 us
  transfers between devices with their start and end apart: 179, of which 65 were waited for; matrix products, arithmetic and copies ran while one was open for 20% of the time, Pallas kernels for 15%

profile of v2, /device:TPU:0, one launch (start us, length us, event | category | flops | bytes accessed | tf_op | source)
XLA Modules:
  0.0 1073.6 jit_solution(8756688151596145732)
XLA Ops:
  42.7 18.4 %collective-permute-done.1 = bf16[2,100,768]{2,1,0:T(8,128)(2,1)S(1)} collective-permute-done((bf16[2,100,768]{2,1,0:T(8,128)(2,1)S(1)}, bf16[2,100,768]{2,1,0:T(8,128)(2,1)S(1)}, u32[]{:S(2)}, u32[]{:S(2)}) %collective-permute-start.1) | collective-permute-done | bytes 307232 | tf_op jit(solution)/shard_map/ppermute | solution.py:91
  106.2 15.8 %collective-permute-start.14 = (bf16[128,1664]{1,0:T(8,128)(2,1)S(1)}, bf16[128,1664]{1,0:T(8,128)(2,1)S(1)}, u32[]{:S(2)}, u32[]{:S(2)}) collective-permute-start(bf16[128,1664]{1,0:T(8,128)(2,1)S(1)} %pad.80.refs_0_), channel_id=1, source_target_pairs={{0,5},{1,4},{2,7},{3,6},{4,1},{5,0},{6,3},{7,2},{8,13},{9,12},{10,... | collective-permute-start | bytes 1277960 | tf_op jit(solution)/shard_map/ppermute | solution.py:102
  123.9 8.7 collective-permute-done.14.refs_3_
  146.7 17.7 %shard_map.282 = (bf16[1024,1600]{1,0:T(8,128)(2,1)}, bf16[1024,768]{1,0:T(8,128)(2,1)S(1)}, f32[8,1024]{1,0:T(8,128)S(1)}, bf16[1024,256]{1,0:T(8,128)(2,1)S(1)}) custom-call(bf16[128,1664]{1,0:T(8,128)(2,1)S(1)} %pad.80.refs_0_, bf16[128,1664]{1,0:T(8,128)(2,1)S(1)} %collective-permute-done.12.refs_1_, ...), custom_call_target="tpu_custom_call" | custom-call | flops 3590324224 | bytes 11283456 | tf_op jit(solution)/shard_map/pallas_call | solution.py:259
  177.4 24.2 %all-gather.18.cloned.1.call-done = bf16[1088,1600]{1,0:T(8,128)(2,1)} async-done(((bf16[272,1600]{1,0:T(8,128)(2,1)}), bf16[1088,1600]{1,0:T(8,128)(2,1)}) %all-gather.18.cloned.1.call-update) | async-done | bytes 3481616 | tf_op jit(solution)/shard_map/all_gather | solution.py:246
  213.6 29.1 %collective-permute-done.29 = bf16[256,1600]{0,1:T(8,128)(2,1)} collective-permute-done((bf16[256,1600]{0,1:T(8,128)(2,1)}, bf16[256,1600]{0,1:T(8,128)(2,1)}, u32[]{:S(2)}, u32[]{:S(2)}) %collective-permute-start.29) | collective-permute-done | bytes 819232 | tf_op jit(solution)/shard_map/ppermute | solution.py:94
  276.2 9.5 collective-permute-done.38.refs_3_
  298.7 13.1 %shard_map.283 = (bf16[1024,1600]{1,0:T(8,128)(2,1)}, bf16[1024,832]{1,0:T(8,128)(2,1)S(1)}, bf16[1024,832]{1,0:T(8,128)(2,1)S(1)}, f32[512,1600]{1,0:T(8,128)}, bf16[512,1664]{1,0:T(8,128)(2,1)S(1)}) custom-call(bf16[128,1664]{1,0:T(8,128)(2,1)S(1)} %pad.89.refs_0_, bf16[128,1664]{1,0:T(8,128)(2,1)S(1)} %collective-permute-done.36.refs_1_, ...), custom_call_target="tpu_custom_call" | custom-call | flops 5452595200 | bytes 20401408 | tf_op jit(solution)/shard_map/pallas_call | solution.py:259
  328.3 17.6 %collective-permute-done.55.refs_2_ = bf16[128,1664]{1,0:T(8,128)(2,1)S(1)} collective-permute-done((bf16[128,1664]{1,0:T(8,128)(2,1)S(1)}, bf16[128,1664]{1,0:T(8,128)(2,1)S(1)}, u32[]{:S(2)}, u32[]{:S(2)}) %collective-permute-start.55) | collective-permute-done | bytes 426016 | tf_op jit(solution)/shard_map/ppermute | solution.py:91
  383.9 18.2 %shard_map.285 = (bf16[1024,1600]{1,0:T(8,128)(2,1)}, bf16[1024,768]{1,0:T(8,128)(2,1)S(1)}, f32[8,1024]{1,0:T(8,128)S(1)}, bf16[1024,256]{1,0:T(8,128)(2,1)S(1)}) custom-call(bf16[128,1664]{1,0:T(8,128)(2,1)S(1)} %pad.91.refs_0_, bf16[128,1664]{1,0:T(8,128)(2,1)} %collective-permute-done.47.refs_1_, bf16[128,1664]{1,0:T(8,128)(2,1)} %collective-permute-done.48.refs_2_, ...), custom_call_target="tpu_custom_call" | custom-call | flops 3590324224 | bytes 11283456 | tf_op jit(solution)/shard_map/pallas_call | solution.py:259
  412.1 35.5 %collective-permute-done.62 = bf16[256,256]{1,0:T(8,128)(2,1)S(1)} collective-permute-done((bf16[256,256]{1,0:T(8,128)(2,1)S(1)}, bf16[256,256]{1,0:T(8,128)(2,1)S(1)}, u32[]{:S(2)}, u32[]{:S(2)}) %collective-permute-start.62) | collective-permute-done | bytes 131104 | tf_op jit(solution)/shard_map/ppermute | solution.py:94
  501.7 10.1 collective-permute-done.74.refs_3_
  526.6 13.6 %shard_map.286 = (bf16[1024,1600]{1,0:T(8,128)(2,1)}, bf16[1024,832]{1,0:T(8,128)(2,1)S(1)}, bf16[1024,832]{1,0:T(8,128)(2,1)S(1)}, f32[512,1600]{1,0:T(8,128)}, bf16[512,1664]{1,0:T(8,128)(2,1)S(1)}) custom-call(bf16[128,1664]{1,0:T(8,128)(2,1)S(1)} %pad.97.refs_0_, bf16[128,1664]{1,0:T(8,128)(2,1)} %collective-permute-done.72.refs_1_, ...), custom_call_target="tpu_custom_call" | custom-call | flops 5452595200 | bytes 20401408 | tf_op jit(solution)/shard_map/pallas_call | solution.py:259
  548.4 14.3 %shard_map.289 = (bf16[1024,832]{1,0:T(8,128)(2,1)S(1)}, f32[1,832]{1,0:T(1,128)S(1)}, f32[512,1600]{1,0:T(8,128)}, bf16[512,1664]{1,0:T(8,128)(2,1)S(1)}) custom-call(bf16[128,1664]{1,0:T(8,128)(2,1)S(1)} %pad.92.refs_0_, bf16[128,1664]{1,0:T(8,128)(2,1)} %collective-permute-done.54.refs_1_, bf16[128,1664]{1,0:T(8,128)(2,1)S(1)} %collective-permute-done.55.refs_2_, ...), custom_call_target="tpu_custom_call" | custom-call | flops 5452595200 | bytes 17124608 | tf_op jit(solution)/shard_map/pallas_call | solution.py:259
  610.8 8.6 collective-permute-done.81
  641.4 20.3 %shard_map.291 = (bf16[1024,768]{1,0:T(8,128)(2,1)S(1)}, f32[1,768]{1,0:T(1,128)S(1)}, f32[512,1600]{1,0:T(8,128)}, bf16[512,1664]{1,0:T(8,128)(2,1)S(1)}) custom-call(bf16[128,256]{1,0:T(8,128)(2,1)S(1)} %get-tuple-element.435.refs_0_, bf16[128,256]{1,0:T(8,128)(2,1)S(1)} %get-tuple-element.478.refs_1_, bf16[128,256]{1,0:T(8,128)(2,1)S(1)} %get-tuple-element.476.refs_2_, ...), custom_call_target="tpu_custom_call" | custom-call | flops 5200936960 | bytes 11152384 | tf_op jit(solution)/shard_map/pallas_call | solution.py:259
  694.4 8.6 collective-permute-done.93
  729.2 10.1 collective-permute-done.98.refs_3_
  750.2 14.8 %shard_map.293 = (bf16[1024,832]{1,0:T(8,128)(2,1)S(1)}, f32[1,832]{1,0:T(1,128)S(1)}, f32[512,1600]{1,0:T(8,128)}, bf16[512,1664]{1,0:T(8,128)(2,1)}) custom-call(bf16[128,1664]{1,0:T(8,128)(2,1)S(1)} %pad.99.refs_0_, bf16[128,1664]{1,0:T(8,128)(2,1)S(1)} %collective-permute-done.96.refs_1_, bf16[128,1664]{1,0:T(8,128)(2,1)S(1)} %collective-permute-done.97.refs_2_, ...), custom_call_target="tpu_custom_call" | custom-call | flops 5452595200 | bytes 17124608 | tf_op jit(solution)/shard_map/pallas_call | solution.py:259
  777.4 10.1 collective-permute-done.104
  799.1 9.3 fusion.27
  821.7 19.9 %shard_map.295 = (bf16[1024,768]{1,0:T(8,128)(2,1)S(1)}, f32[1,768]{1,0:T(1,128)S(1)}, f32[512,1600]{1,0:T(8,128)}, bf16[512,1664]{1,0:T(8,128)(2,1)S(1)}) custom-call(bf16[128,256]{1,0:T(8,128)(2,1)S(1)} %get-tuple-element.427.refs_0_, bf16[128,256]{1,0:T(8,128)(2,1)S(1)} %get-tuple-element.472.refs_1_, bf16[128,256]{1,0:T(8,128)(2,1)S(1)} %get-tuple-element.470.refs_2_, ...), custom_call_target="tpu_custom_call" | custom-call | flops 5200936960 | bytes 11152384 | tf_op jit(solution)/shard_map/pallas_call | solution.py:259
  902.2 12.0 %collective-permute-done.164.refs_3_ = bf16[2,100,832]{2,1,0:T(8,128)(2,1)} collective-permute-done((bf16[2,100,832]{2,1,0:T(8,128)(2,1)}, bf16[2,100,832]{2,1,0:T(8,128)(2,1)}, u32[]{:S(2)}, u32[]{:S(2)}) %collective-permute-start.164) | collective-permute-done | bytes 332832 | tf_op jit(solution)/shard_map/ppermute | solution.py:102
  917.8 9.6 collective-permute-done.156.other_out
  (1011 shorter events, 687.5 us)
Async XLA Ops:
  7.2 136.8 %all-gather.8.cloned.1.call-start = ((), (), s32[]{:S(2)}) async-start(), calls=%async_computation.8 | async-start | bytes 3072000 | tf_op jit(solution)/shard_map/all_gather | solution.py:247
  17.4 45.0 %collective-permute-start.2 = (bf16[256,1600]{0,1:T(8,128)(2,1)}, bf16[256,1600]{0,1:T(8,128)(2,1)}, u32[]{:S(2)}, u32[]{:S(2)}) collective-permute-start(bf16[256,1600]{0,1:T(8,128)(2,1)} %pad_maximum_fusion), channel_id=1, source_target_pairs={{0,0},{1,9},{4,20},{5,29},{2,2},{3,11},{6,22},{7,31},{8,1},{9,8},{... | collective-permute-start | bytes 2457608 | tf_op jit(solution)/shard_map/ppermute | solution.py:85
  62.4 139.1 %all-gather.18.cloned.1.call-start = ((), (), s32[]{:S(2)}) async-start(), calls=%async_computation.21 | async-start | bytes 4526080 | tf_op jit(solution)/shard_map/all_gather | solution.py:246
  100.8 197.9 %all-gather.10.cloned.1.call-start = ((), (), s32[]{:S(2)}) async-start(), calls=%async_computation.9 | async-start | bytes 3584000 | tf_op jit(solution)/shard_map/all_gather | solution.py:247
  101.5 280.6 %all-gather.12.cloned.1.call-start = ((), (), s32[]{:S(2)}) async-start(), calls=%async_computation.10 | async-start | bytes 3072000 | tf_op jit(solution)/shard_map/all_gather | solution.py:247
  166.2 237.9 %all-gather.14.cloned.1.call-start = ((), (), s32[]{:S(2)}) async-start(), calls=%async_computation.11 | async-start | bytes 4526080 | tf_op jit(solution)/shard_map/all_gather | solution.py:247
  204.0 40.2 %collective-permute-start.31 = (bf16[256,1600]{0,1:T(8,128)(2,1)}, bf16[256,1600]{0,1:T(8,128)(2,1)}, u32[]{:S(2)}, u32[]{:S(2)}) collective-permute-start(bf16[256,1600]{0,1:T(8,128)(2,1)} %copy.261), channel_id=1, source_target_pairs={{0,5},{1,4},{2,7},{3,6},{4,1},{5,0},{6,3},{7,2},{8,13},{9,12},{10,... | collective-permute-start | bytes 2457608 | tf_op jit(solution)/shard_map/ppermute | solution.py:102
  207.5 41.4 %collective-permute-start.32 = (bf16[256,1600]{0,1:T(8,128)(2,1)}, bf16[256,1600]{0,1:T(8,128)(2,1)}, u32[]{:S(2)}, u32[]{:S(2)}) collective-permute-start(bf16[256,1600]{0,1:T(8,128)(2,1)} %copy.261), channel_id=1, source_target_pairs={{0,2},{2,0},{4,6},{6,4},{1,3},{3,1},{5,7},{7,5},{8,10},{10,8},{12,... | collective-permute-start | bytes 2457608 | tf_op jit(solution)/shard_map/ppermute | solution.py:88
  275.6 249.0 %all-gather.16.cloned.1.call-start = ((), (), s32[]{:S(2)}) async-start(), calls=%async_computation.12 | async-start | bytes 3584000 | tf_op jit(solution)/shard_map/all_gather | solution.py:247
  380.3 490.3 %reduce-scatter.23.cloned.1.call-start = ((), (), s32[]{:S(2)}) async-start(), calls=%async_computation.20 | async-start | bytes 3584000 | tf_op jit(solution)/shard_map/reduce_scatter | solution.py:253
  406.6 66.3 %collective-permute-start.68 = (bf16[256,1600]{0,1:T(8,128)(2,1)}, bf16[256,1600]{0,1:T(8,128)(2,1)}, u32[]{:S(2)}, u32[]{:S(2)}) collective-permute-start(bf16[256,1600]{0,1:T(8,128)(2,1)} %copy.278), channel_id=1, source_target_pairs={{0,2},{2,0},{4,6},{6,4},{1,3},{3,1},{5,7},{7,5},{8,10},{10,8},{12,... | collective-permute-start | bytes 2457608 | tf_op jit(solution)/shard_map/ppermute | solution.py:88
  406.9 60.6 %collective-permute-start.67 = (bf16[256,1600]{0,1:T(8,128)(2,1)}, bf16[256,1600]{0,1:T(8,128)(2,1)}, u32[]{:S(2)}, u32[]{:S(2)}) collective-permute-start(bf16[256,1600]{0,1:T(8,128)(2,1)} %copy.278), channel_id=1, source_target_pairs={{0,5},{1,4},{2,7},{3,6},{4,1},{5,0},{6,3},{7,2},{8,13},{9,12},{10,... | collective-permute-start | bytes 2457608 | tf_op jit(solution)/shard_map/ppermute | solution.py:102
  408.2 59.8 %collective-permute-start.66 = (bf16[256,1600]{0,1:T(8,128)(2,1)}, bf16[256,1600]{0,1:T(8,128)(2,1)}, u32[]{:S(2)}, u32[]{:S(2)}) collective-permute-start(bf16[256,1600]{0,1:T(8,128)(2,1)} %copy.278), channel_id=1, source_target_pairs={{0,4},{2,6},{4,0},{6,2},{1,5},{3,7},{5,1},{7,3},{8,12},{10,14},{12... | collective-permute-start | bytes 2457608 | tf_op jit(solution)/shard_map/ppermute | solution.py:91
  409.0 56.8 %collective-permute-start.65 = (bf16[256,1600]{0,1:T(8,128)(2,1)}, bf16[256,1600]{0,1:T(8,128)(2,1)}, u32[]{:S(2)}, u32[]{:S(2)}) collective-permute-start(bf16[256,1600]{0,1:T(8,128)(2,1)} %copy.278), channel_id=1, source_target_pairs={{0,1},{1,0},{2,3},{3,2},{4,5},{5,4},{6,7},{7,6},{8,9},{9,8},{10,11... | collective-permute-start | bytes 2457608 | tf_op jit(solution)/shard_map/ppermute | solution.py:94
  570.5 311.0 %reduce-scatter.17.cloned.1.call-start = ((), (), s32[]{:S(2)}) async-start(), calls=%async_computation.17 | async-start | bytes 3461120 | tf_op jit(solution)/shard_map/reduce_scatter | solution.py:252
  582.8 311.0 %reduce-scatter.19.cloned.1.call-start = ((), (), s32[]{:S(2)}) async-start(), calls=%async_computation.18 | async-start | bytes 1064960 | tf_op jit(solution)/shard_map/reduce_scatter | solution.py:253
  714.7 229.6 %reduce-scatter.11.cloned.1.call-start = ((), (), s32[]{:S(2)}) async-start(), calls=%async_computation.14 | async-start | bytes 3072000 | tf_op jit(solution)/shard_map/reduce_scatter | solution.py:253
  721.8 266.2 %reduce-scatter.21.cloned.1.call-start = ((), (), s32[]{:S(2)}) async-start(), calls=%async_computation.19 | async-start | bytes 3584000 | tf_op jit(solution)/shard_map/reduce_scatter | solution.py:253
  771.9 218.9 %reduce-scatter.9.cloned.1.call-start = ((), (), s32[]{:S(2)}) async-start(), calls=%async_computation.13 | async-start | bytes 3072000 | tf_op jit(solution)/shard_map/reduce_scatter | solution.py:253
  848.5 163.9 %reduce-scatter.13.cloned.1.call-start = ((), (), s32[]{:S(2)}) async-start(), calls=%async_computation.15 | async-start | bytes 3461120 | tf_op jit(solution)/shard_map/reduce_scatter | solution.py:252
  856.1 165.2 %reduce-scatter.15.cloned.1.call-start = ((), (), s32[]{:S(2)}) async-start(), calls=%async_computation.16 | async-start | bytes 1064960 | tf_op jit(solution)/shard_map/reduce_scatter | solution.py:253
  915.1 39.6 %collective-permute-start.132 = (bf16[128,1664]{1,0:T(8,128)(2,1)}, bf16[128,1664]{1,0:T(8,128)(2,1)}, u32[]{:S(2)}, u32[]{:S(2)}) collective-permute-start(bf16[128,1664]{1,0:T(8,128)(2,1)} %pad.101.refs_0_), channel_id=1, source_target_pairs={{0,1},{1,0},{2,3},{3,2},{4,5},{5,4},{6,7},{7,6},{8,9},{9,8},{10,11... | collective-permute-start | bytes 1277960 | tf_op jit(solution)/shard_map/ppermute | solution.py:94
  916.2 38.6 %collective-permute-start.112 = (bf16[128,1664]{1,0:T(8,128)(2,1)}, bf16[128,1664]{1,0:T(8,128)(2,1)}, u32[]{:S(2)}, u32[]{:S(2)}) collective-permute-start(bf16[128,1664]{1,0:T(8,128)(2,1)} %get-tuple-element.220), channel_id=1, source_target_pairs={{0,5},{1,4},{2,7},{3,6},{4,1},{5,0},{6,3},{7,2},{8,13},{9,12},{10,... | collective-permute-start | bytes 1277960 | tf_op jit(solution)/shard_map/ppermute | solution.py:102
  1013.2 43.1 %collective-permute-start.131 = (bf16[208,1600]{1,0:T(8,128)(2,1)}, bf16[208,1600]{1,0:T(8,128)(2,1)S(1)}, u32[]{:S(2)}, u32[]{:S(2)}) collective-permute-start(bf16[208,1600]{1,0:T(8,128)(2,1)} %bitcast.156), channel_id=1, source_target_pairs={{0,1},{1,0},{2,3},{3,2},{4,5},{5,4},{6,7},{7,6},{8,9},{9,8},{10,11... | collective-permute-start | bytes 1996808 | tf_op jit(solution)/shard_map/ppermute | solution.py:94
  (294 other events, 4877.5 us)
Sparse Core Ops, SparseCore 0:
  62.6 66.8 all-gather.7
  131.6 69.9 all-gather.17
  203.7 57.4 all-gather.9
  262.6 50.6 all-gather.11
  314.7 69.8 all-gather.13
  386.0 57.4 all-gather.15
  570.6 53.9 reduce-scatter.22
  626.9 54.4 reduce-scatter.16
  714.9 21.7 reduce-scatter.18
  738.8 48.8 reduce-scatter.10
  790.0 55.6 reduce-scatter.20
  848.6 48.7 reduce-scatter.8
  900.3 54.1 reduce-scatter.12
  969.4 21.7 reduce-scatter.14

commit v3 on v2

--- a/solution.py
+++ b/solution.py
@@ -557,6 +557,71 @@
     lax.fori_loop(0, half // block, second, 0)
 
 
+def lift_kernel(count, *refs):
+    pieces = refs[:count]
+    up, bias, full, slope, activated = refs[count:]
+    rows = pieces[0].shape[0]
+    for i, piece in enumerate(pieces):
+        full[i * rows : (i + 1) * rows, :] = piece[:, : full.shape[1]]
+    block = 2 * rows
+
+    def lift(i, carry):
+        at = pl.ds(pl.multiple_of(i * block, block), block)
+        value, pull = gelu_both(dot(full[at, :], up[...]) + bias[...])
+        activated[at, :] = value.astype(BF)
+        slope[at, :] = pull.astype(BF)
+        return carry
+
+    lax.fori_loop(0, count // 2, lift, 0)
+
+
+def lift_units(plan, pieces, up, bias):
+    rows, width = pieces[0].shape[0], up.shape[0]
+    if not plan.cube:
+        full = jnp.concatenate(pieces)[:, :width]
+        value, pull = gelu_both(dot(full, up) + bias)
+        return full, pull.astype(BF), value.astype(BF)
+    tall, units = plan.group * rows, up.shape[1]
+    return call(
+        functools.partial(lift_kernel, plan.group),
+        [sds((tall, width), BF), sds((tall, units), BF), sds((tall, units), BF)],
+        [],
+        2 * tall * width * units,
+        [*pieces, up, bias[None]],
+    )
+
+
+def lower_kernel(block, left, right, near, far):
+    half, width = near.shape
+
+    def first(i, carry):
+        at = pl.ds(pl.multiple_of(i * block, block), block)
+        near[at, :] = dot(left[at, :], right[...])
+        return carry
+
+    def second(i, carry):
+        at = pl.ds(pl.multiple_of(i * block, block), block)
+        rows = left[pl.ds(pl.multiple_of(half + i * block, block), block), :]
+        far[at, :width] = dot(rows, right[...]).astype(BF)
+        return carry
+
+    lax.fori_loop(0, half // block, first, 0)
+    lax.fori_loop(0, half // block, second, 0)
+
+
+def lower_units(plan, activated, down):
+    tall, width = activated.shape[0], down.shape[1]
+    if not plan.cube:
+        return halves(dot(activated, down))
+    return call(
+        functools.partial(lower_kernel, 2 * (tall // plan.group)),
+        [sds((tall // 2, width), F32), sds((tall // 2, lanes(width)), BF)],
+        [],
+        2 * activated.size * width,
+        [activated, down],
+    )
+
+
 def hidden_units(plan, pieces, up, bias, down):
     rows, width = pieces[0].shape[0], up.shape[0]
     if not plan.cube:
@@ -793,20 +858,19 @@
     )(*operands)
 
 
-def rows_back_kernel(kept, x_ref, own, other, own_out, other_out, *refs):
-    down, out = refs[-2:]
-    units = down.shape[1] // 2
+def rows_back_kernel(kept, x_ref, own, other, *refs):
+    out = refs[-1]
     for x in range(2):
 
         @pl.when(x_ref[0] == x)
         def _():
             first, second = (own, other) if x == 0 else (other, own)
-            down[0, :units, :] = first[:units, :].astype(F32)
-            down[0, units:, :] = second[:units, :].astype(F32)
-            first, second = (own_out, other_out) if x == 0 else (other_out, own_out)
-            out[0] = jnp.concatenate(
-                [first[...].astype(F32)[:kept], second[...].astype(F32)[:kept]]
-            )
+            first, second = (v[...].astype(F32)[:kept] for v in (first, second))
+            if kept % 8:
+                out[0] = jnp.concatenate([first, second])
+            else:
+                out[0, :kept, :] = first
+                out[0, kept:, :] = second
 
 
 def shards(
@@ -845,14 +909,16 @@
     seq = lax.axis_index("seq")
     rank = plan.rank()
 
-    def rest_of(down, out):
+    def down_of(down):
         down = lax.dynamic_slice_in_dim(down, replica * piece, piece, 0)
-        down = jnp.pad(down, ((0, piece_rows - piece), (0, 0)))
+        return jnp.pad(down, ((0, piece_rows - piece), (0, 0)))
+
+    def out_of(out):
         out = jnp.pad(out, ((0, nr * part + part_rows - own_rows), (0, 0)))
         out = lax.dynamic_slice_in_dim(out, replica * part, part_rows, 0)
         valid = lax.broadcasted_iota(jnp.int32, out.shape, 0)
         valid = (valid < part) & (valid + replica * part < own_rows)
-        return jnp.concatenate([down, jnp.where(valid, out, jnp.zeros_like(out))])
+        return jnp.where(valid, out, jnp.zeros_like(out))
 
     qkv_send = head_columns(plan, w_qkv)
     first = plan.exchange_fsdp(qkv_send[0]).reshape(nf * own_rows, 3 * span)
@@ -872,8 +938,9 @@
     codes = segments[0] * CODE + seq * length + jnp.arange(length, dtype=jnp.int32)
     codes = plan.gather_doubling(plan.regroup(codes[None]))
 
-    first, both, qkv_send, w_up, w_down, w_out, small, codes = lax.optimization_barrier(
-        (first, both, qkv_send, w_up, w_down, w_out, small, codes)
+    outs = jnp.concatenate([out_of(w_out[layer]) for layer in range(layers)])
+    first, both, qkv_send, w_up, w_down, outs, small, codes = lax.optimization_barrier(
+        (first, both, qkv_send, w_up, w_down, outs, small, codes)
     )
     hidden = both[:length].astype(F32)
     grad = both[length:].astype(F32)
@@ -884,23 +951,19 @@
         if layer:
             qkv = plan.exchange_fsdp(qkv_send[layer]).reshape(nf * own_rows, 3 * span)
         up = plan.exchange_fsdp(up_send[layer]).reshape(nf * own_rows, units)
-        prepared.append((qkv, up, rest_of(w_down[layer], w_out[layer])))
+        prepared.append((qkv, up, down_of(w_down[layer])))
     early = [prepared[0][1:], prepared[1:]]
     codes, early = lax.optimization_barrier((codes, early))
     prepared = [(first, *early[0])] + early[1]
 
-    def fetch(layer):
-        qkv, up, rest = prepared[layer]
+    weights = []
+    for layer, (qkv, up, down) in enumerate(prepared):
         qkv = gather_seq(qkv)
-        rest = gather_seq(rest, lead=layer % 2 == 0)
+        if layer == 0:
+            outs = gather_seq(outs).reshape(nz, layers, part_rows, width)
         up = gather_seq(up)
-        return qkv, rest, up
-
-    def unpack(rest):
-        rest = rest.reshape(nz, piece_rows + part_rows, width)
-        down = rest[:, :piece_rows].reshape(units, width)
-        out = rest[:, piece_rows:].reshape(nz * part_rows, width)
-        return jnp.concatenate(plan.gather_pieces(out)), down
+        down = gather_seq(down, lead=layer % 2 == 0)
+        weights.append((qkv, up, down))
 
     source = plan.source()
     feature_heads = (source[:, None] * span + jnp.arange(span, dtype=jnp.int32)).reshape(-1)
@@ -935,11 +998,12 @@
 
     vecs = [vectors(layer) for layer in range(layers)]
 
-    weights = [fetch(layer) for layer in range(layers)]
+    def out_block(layer):
+        return outs[:, layer].reshape(nz * part_rows, width)
 
     kept = []
     for layer in range(layers):
-        qkv_w, rest, up_w = weights[layer]
+        qkv_w, up_w, down_w = weights[layer]
         (gain1, shift1, _, _, bias_out, gain2, shift2, bias_down), bias_qkv, bias_up = vecs[layer]
         unit1, inv1 = norm_parts(hidden)
         pieces = plan.gather_pieces(widen((unit1 * gain1 + shift1).astype(BF)))
@@ -949,8 +1013,11 @@
         normed, packed, lse, mixed = attend(
             plan, pieces, qkv_w, bias_qkv, codes, total, scale
         )
-        out_w, down_w = unpack(after(rest, packed))
+        if layer == 0:
+            out_w = jnp.concatenate(plan.gather_pieces(out_block(0)))
         weights[layer] = qkv_w, out_w, up_w, down_w
+        if layer < layers - 1:
+            next_out = plan.gather_pieces(after(out_block(layer + 1), packed))
         mixed = jnp.concatenate(plan.exchange(mixed), axis=1)
         mixed = dot(mixed, select).astype(BF)
         block = nz * part_rows
@@ -960,7 +1027,12 @@
         middle = hidden + (dot(mixed, out_w) + bias_out)
         unit2, inv2 = norm_parts(middle)
         pieces = plan.gather_pieces(widen((unit2 * gain2 + shift2).astype(BF)))
-        normed_two, slope, activated, near, far = hidden_units(plan, pieces, up_w, bias_up, down_w)
+        if layer == layers - 1:
+            normed_two, slope, activated = lift_units(plan, pieces, up_w, bias_up)
+        else:
+            normed_two, slope, activated, near, far = hidden_units(
+                plan, pieces, up_w, bias_up, down_w
+            )
         kept.append(
             (
                 unit1,
@@ -978,10 +1050,9 @@
         )
         if layer < layers - 1:
             hidden = middle + (plan.scatter_parts(near, far) + bias_down)
-    hidden = middle + (plan.scatter_parts(near, far) + bias_down)
-    output = plan.regroup(hidden.astype(BF), back=True)
-
-    def late_up(layer, up, rest, qkv):
+            out_w = jnp.concatenate(next_out)
+
+    def late_up(up, layer):
         up = plan.to_owners(up)
         if plan.cube:
             ranks = [[plan.rank_of(f, r) for r in range(nr)] for f in range(nf)]
@@ -999,7 +1070,7 @@
         up = up.reshape(1, own_rows, -1).astype(F32)
         return up if into_up is None else jnp.concatenate([up, into_up])
 
-    def late_qkv(layer, up, rest, qkv):
+    def late_qkv(qkv, layer):
         qkv = plan.to_owners(qkv)
         if plan.cube:
             return into_layer(
@@ -1016,45 +1087,40 @@
         qkv = qkv.reshape(1, own_rows, triple).astype(F32)
         return qkv if into_qkv is None else jnp.concatenate([qkv, into_qkv])
 
-    def late_rest(layer, up, rest, qkv):
-        down, out = rest
+    def late_rows(v, rows, kept, layer, previous):
         if not plan.cube:
-            down = lax.all_gather(down, "replica", axis=0, tiled=False)
-            out = lax.all_gather(out, "replica", axis=0, tiled=False)
-            down = down[:, :piece].reshape(1, own_hidden, width).astype(F32)
-            out = out[:, :part].reshape(nr * part, width)[None, :own_rows].astype(F32)
-            if into_down is None:
-                return down, out
-            return jnp.concatenate([down, into_down]), jnp.concatenate([out, into_out])
-        operands = [down, plan.swap_x(down), out, plan.swap_x(out)]
-        in_specs = [pl.BlockSpec(v.shape, lambda i, s: (0, 0)) for v in operands]
+            v = lax.all_gather(v, "replica", axis=0, tiled=False)
+            v = v[:, :kept].reshape(nr * kept, width)[None, :rows].astype(F32)
+            return v if previous is None else jnp.concatenate([v, previous])
+        operands = [v, plan.swap_x(v)]
+        in_specs = [pl.BlockSpec(v.shape, lambda i, s: (0, 0))] * 2
         operands = [replica.astype(jnp.int32).reshape(1)] + operands
         aliases = {}
-        if into_down is not None:
-            operands += [into_down, into_out]
-            in_specs += [pl.BlockSpec(memory_space=pl.ANY)] * 2
-            aliases = {5: 0, 6: 1}
+        if previous is not None:
+            operands.append(previous)
+            in_specs.append(pl.BlockSpec(memory_space=pl.ANY))
+            aliases = {3: 0}
         return pl.pallas_call(
-            functools.partial(rows_back_kernel, part),
+            functools.partial(rows_back_kernel, kept),
             grid_spec=pltpu.PrefetchScalarGridSpec(
                 num_scalar_prefetch=1,
                 grid=(1,),
                 in_specs=in_specs,
-                out_specs=[
-                    pl.BlockSpec((1, own_hidden, width), lambda i, s: (layer, 0, 0)),
-                    pl.BlockSpec((1, own_rows, width), lambda i, s: (layer, 0, 0)),
-                ],
+                out_specs=pl.BlockSpec((1, rows, width), lambda i, s: (layer, 0, 0)),
             ),
-            out_shape=[
-                sds((layers, own_hidden, width), F32),
-                sds((layers, own_rows, width), F32),
-            ],
+            out_shape=sds((layers, rows, width), F32),
             input_output_aliases=aliases,
             compiler_params=pltpu.CompilerParams(vmem_limit_bytes=44 * 1024 * 1024),
             cost_estimate=pl.CostEstimate(
-                flops=0, bytes_accessed=12 * down.size, transcendentals=0
+                flops=0, bytes_accessed=12 * v.size, transcendentals=0
             ),
         )(*operands)
+
+    def late_down(down, layer):
+        return late_rows(down, own_hidden, piece, layer, into_down)
+
+    def late_out(out, layer):
+        return late_rows(out, own_rows, part, layer, into_out)
 
     into_qkv = into_up = into_down = into_out = None
     smalls = [None] * layers
@@ -1068,10 +1134,11 @@
         g_low = grad.astype(BF)
         grad_down = down_grad(plan, activated, grad_pieces, width)
         if late is not None:
-            out = scatter_seq(down_grad(plan, *late[2][1], width))
-            late = (late[0], late[1], (late[2][0], out), late[3])
-            into_up = late_up(*late)
-            into_down, into_out = late_rest(*late)
+            above = layer + 1
+            out = scatter_seq(down_grad(plan, *late[2], width))
+            into_up = late_up(late[0], above)
+            into_down = late_down(late[1], above)
+            into_out = late_out(out, above)
         if late is None:
             grad_pieces, grad_down = lax.optimization_barrier((grad_pieces, grad_down))
         down = scatter_seq(grad_down, lead=True)
@@ -1090,6 +1157,10 @@
         )
         g_mixed = plan.exchange(g_mixed)
         att_pieces = plan.gather_pieces(widen(g_att))
+        if late is None:
+            near, far = lower_units(plan, after(activated, g_mixed), down_w)
+            hidden = middle + (plan.scatter_parts(near, far) + bias_down)
+            output = plan.regroup(hidden.astype(BF), back=True)
         g_packed, g_b, near, far = attend_back(
             plan, g_mixed, packed, lse, codes, qkv_w, total, scale
         )
@@ -1098,8 +1169,11 @@
         qkv = scatter_seq(grad_qkv)
         qkv = qkv.reshape(nf, own_rows, 3 * span)
         if late is not None:
-            into_qkv = late_qkv(*late[:3], after(late[3], g_n1))
-        late = (layer, up, (down, (after(mixed, g_n1), att_pieces)), qkv)
+            into_qkv = late_qkv(after(late[3], g_n1), above)
+        if layer == 0:
+            into_up = late_up(up, layer)
+            into_down = late_down(down, layer)
+        late = (up, down, (after(mixed, g_n1), att_pieces), qkv)
         smalls[layer] = (
             jnp.sum(g_n1 * unit1, axis=0),
             jnp.sum(g_n1, axis=0),
@@ -1113,13 +1187,11 @@
         grad = g_mid + norm_pull(g_n1, unit1, inv1, gain1)
         if layer:
             grad_pieces = plan.gather_pieces(widen(grad.astype(BF)))
-    out = scatter_seq(down_grad(plan, *late[2][1], width))
-    late = (late[0], late[1], (late[2][0], out), late[3])
+    out = scatter_seq(down_grad(plan, *late[2], width))
     grad_tokens = plan.regroup(grad.astype(BF), back=True).astype(F32)
     output = after(output, grad).astype(F32)
-    into_up = late_up(*late)
-    into_down, into_out = late_rest(*late)
-    into_qkv = late_qkv(*late)
+    into_qkv = late_qkv(after(late[3], (into_up, into_down)), 0)
+    into_out = late_out(out, 0)
 
     def scattered(layer):
         n1g, n1s, g_b, b_o, n2g, n2s, b_d, b_u = smalls[layer]

time: 1090 us -> 1070 us (0.982)
  waiting for transfers between devices: 403 us -> 390 us
  local copies, waits for them, and re-layouts: 192 us -> 181 us
    ppermute x33, waiting for transfers between devices: 134 us -> 102 us  [swap_y(): return lax.ppermute(v, 'fsdp', [(f, f ^ 2) for f in range(self.nf)])]
    ppermute x27, starting transfers between devices: 61 us -> 33.4 us  [swap_xy(): return lax.ppermute(v, GROUP, pairs)]
    ppermute x33, starting transfers between devices: 39.4 us -> 55.5 us  [swap_y(): return lax.ppermute(v, 'fsdp', [(f, f ^ 2) for f in range(self.nf)])]
    all_gather x5 -> x6, waiting for transfers between devices: 0.03 us -> 14 us  [gather_seq(): return lax.all_gather(v, 'seq', axis=0, tiled=True)]
    ppermute x32, starting transfers between devices: 30.6 us -> 42.1 us  [swap_x(): return lax.ppermute(v, 'replica', [(r, r ^ 1) for r in range(self.nr)])]
    ppermute x32, waiting for transfers between devices: 128 us -> 139 us  [swap_x(): return lax.ppermute(v, 'replica', [(r, r ^ 1) for r in range(self.nr)])]
    unnamed x324 -> x352, local copies, waits for them, and re-layouts: 106 us -> 99.3 us
    pallas_call x26 -> x27, Pallas kernels: 184 us -> 187 us  [call(): pl.pallas_call(kernel, out_shape=tuple(outs), scratch_shapes=scratch, com...]
  transfers between devices with their start and end apart: 179 -> 180, of which waited for: 65 -> 69; matrix products, arithmetic and copies ran while one was open for 20% -> 19% of each run, Pallas kernels for 15% -> 18%
where the time goes in v3:
time: 1070 us; the launch traced here: 1050 us
  waiting for transfers between devices  390 us (36%)
  Pallas kernels  209 us (20%)
  local copies, waits for them, and re-layouts  181 us (17%)
  starting transfers between devices  177 us (17%)
  other arithmetic  46.4 us (4%)
  matrix products  33 us (3%)
  between operations  16.9 us (2%)
    pallas_call x27, Pallas kernels, call(): pl.pallas_call(kernel, out_shape=tuple(outs), scratch_shapes=scratch, com...  187 us
    ppermute x32, waiting for transfers between devices, swap_x(): return lax.ppermute(v, 'replica', [(r, r ^ 1) for r in range(self.nr)])  139 us
    ppermute x33, waiting for transfers between devices, swap_y(): return lax.ppermute(v, 'fsdp', [(f, f ^ 2) for f in range(self.nf)])  102 us
    unnamed x352, local copies, waits for them, and re-layouts  99.3 us
    ppermute x27, waiting for transfers between devices, swap_xy(): return lax.ppermute(v, GROUP, pairs)  97.5 us
    ppermute x33, starting transfers between devices, swap_y(): return lax.ppermute(v, 'fsdp', [(f, f ^ 2) for f in range(self.nf)])  55.5 us
    ppermute x32, starting transfers between devices, swap_x(): return lax.ppermute(v, 'replica', [(r, r ^ 1) for r in range(self.nr)])  42.1 us
    ppermute x27, starting transfers between devices, swap_xy(): return lax.ppermute(v, GROUP, pairs)  33.4 us
  transfers between devices with their start and end apart: 180, of which 69 were waited for; matrix products, arithmetic and copies ran while one was open for 19% of the time, Pallas kernels for 18%

profile of v3, /device:TPU:0, one launch (start us, length us, event | category | flops | bytes accessed | tf_op | source)
XLA Modules:
  0.0 1053.3 jit_solution(12968573224249191761)
XLA Ops:
  63.6 19.1 %collective-permute-start.22 = (bf16[2,100,768]{2,1,0:T(8,128)(2,1)}, bf16[2,100,768]{2,1,0:T(8,128)(2,1)}, u32[]{:S(2)}, u32[]{:S(2)}) collective-permute-start(bf16[2,100,768]{2,1,0:T(8,128)(2,1)} %get-tuple-element.392), channel_id=1, source_target_pairs={{0,4},{2,6},{4,0},{6,2},{1,5},{3,7},{5,1},{7,3},{8,12},{10,14},{12... | collective-permute-start | bytes 921608 | tf_op jit(solution)/shard_map/ppermute | solution.py:91
  113.1 14.0 %all-gather.11.cloned.1.call-done = bf16[512,1600]{1,0:T(8,128)(2,1)} async-done(((bf16[128,1600]{1,0:T(8,128)(2,1)}), bf16[512,1600]{1,0:T(8,128)(2,1)}) %all-gather.11.cloned.1.call-update) | async-done | bytes 1638416 | tf_op jit(solution)/shard_map/all_gather | solution.py:247
  140.9 13.8 %collective-permute-done.29 = bf16[256,1600]{0,1:T(8,128)(2,1)} collective-permute-done((bf16[256,1600]{0,1:T(8,128)(2,1)}, bf16[256,1600]{0,1:T(8,128)(2,1)}, u32[]{:S(2)}, u32[]{:S(2)}) %collective-permute-start.29) | collective-permute-done | bytes 819232 | tf_op jit(solution)/shard_map/ppermute | solution.py:94
  155.0 19.2 %collective-permute-done.30 = bf16[256,1600]{0,1:T(8,128)(2,1)} collective-permute-done((bf16[256,1600]{0,1:T(8,128)(2,1)}, bf16[256,1600]{0,1:T(8,128)(2,1)}, u32[]{:S(2)}, u32[]{:S(2)}) %collective-permute-start.30) | collective-permute-done | bytes 819232 | tf_op jit(solution)/shard_map/ppermute | solution.py:91
  181.3 9.6 collective-permute-done.13.refs_2_
  204.1 17.7 %shard_map.282 = (bf16[1024,1600]{1,0:T(8,128)(2,1)}, bf16[1024,768]{1,0:T(8,128)(2,1)S(1)}, f32[8,1024]{1,0:T(8,128)S(1)}, bf16[1024,256]{1,0:T(8,128)(2,1)S(1)}) custom-call(bf16[128,1664]{1,0:T(8,128)(2,1)S(1)} %pad.82.refs_0_, bf16[128,1664]{1,0:T(8,128)(2,1)S(1)} %collective-permute-done.12.refs_1_, ...), custom_call_target="tpu_custom_call" | custom-call | flops 3590324224 | bytes 11283456 | tf_op jit(solution)/shard_map/pallas_call | solution.py:259
  254.3 9.2 collective-permute-done.36.refs_1_
  272.6 23.8 %all-gather.21.cloned.1.call-done.refs_10_.refs_9_ = bf16[832,1600]{1,0:T(8,128)(2,1)} async-done(((bf16[208,1600]{1,0:T(8,128)(2,1)}), bf16[832,1600]{1,0:T(8,128)(2,1)}) %all-gather.21.cloned.1.call-update) | async-done | bytes 2662416 | tf_op jit(solution)/shard_map/all_gather | solution.py:246
  296.4 14.7 %shard_map.283 = (bf16[1024,1600]{1,0:T(8,128)(2,1)}, bf16[1024,832]{1,0:T(8,128)(2,1)S(1)}, bf16[1024,832]{1,0:T(8,128)(2,1)S(1)}, f32[512,1600]{1,0:T(8,128)}, bf16[512,1664]{1,0:T(8,128)(2,1)}) custom-call(bf16[128,1664]{1,0:T(8,128)(2,1)S(1)} %pad.89.refs_0_, bf16[128,1664]{1,0:T(8,128)(2,1)S(1)} %collective-permute-done.36.refs_1_, ...), custom_call_target="tpu_custom_call" | custom-call | flops 5452595200 | bytes 20401408 | tf_op jit(solution)/shard_map/pallas_call | solution.py:259
  324.0 13.2 %collective-permute-done.65 = bf16[256,1600]{0,1:T(8,128)(2,1)} collective-permute-done((bf16[256,1600]{0,1:T(8,128)(2,1)}, bf16[256,1600]{0,1:T(8,128)(2,1)}, u32[]{:S(2)}, u32[]{:S(2)}) %collective-permute-start.65) | collective-permute-done | bytes 819232 | tf_op jit(solution)/shard_map/ppermute | solution.py:94
  340.8 14.4 %collective-permute-done.66 = bf16[256,1600]{0,1:T(8,128)(2,1)} collective-permute-done((bf16[256,1600]{0,1:T(8,128)(2,1)}, bf16[256,1600]{0,1:T(8,128)(2,1)}, u32[]{:S(2)}, u32[]{:S(2)}) %collective-permute-start.66) | collective-permute-done | bytes 819232 | tf_op jit(solution)/shard_map/ppermute | solution.py:91
  387.9 12.3 %collective-permute-done.56.refs_3_ = bf16[128,1664]{1,0:T(8,128)(2,1)S(1)} collective-permute-done((bf16[128,1664]{1,0:T(8,128)(2,1)S(1)}, bf16[128,1664]{1,0:T(8,128)(2,1)S(1)}, u32[]{:S(2)}, u32[]{:S(2)}) %collective-permute-start.56) | collective-permute-done | bytes 426016 | tf_op jit(solution)/shard_map/ppermute | solution.py:102
  435.7 17.8 %shard_map.285 = (bf16[1024,1600]{1,0:T(8,128)(2,1)}, bf16[1024,768]{1,0:T(8,128)(2,1)S(1)}, f32[8,1024]{1,0:T(8,128)S(1)}, bf16[1024,256]{1,0:T(8,128)(2,1)S(1)}) custom-call(bf16[128,1664]{1,0:T(8,128)(2,1)S(1)} %pad.91.refs_0_, bf16[128,1664]{1,0:T(8,128)(2,1)} %collective-permute-done.47.refs_1_, bf16[128,1664]{1,0:T(8,128)(2,1)} %collective-permute-done.48.refs_2_, ...), custom_call_target="tpu_custom_call" | custom-call | flops 3590324224 | bytes 11283456 | tf_op jit(solution)/shard_map/pallas_call | solution.py:259
  478.1 9.2 collective-permute-done.72.refs_1_
  520.5 14.2 %shard_map.288 = (bf16[1024,832]{1,0:T(8,128)(2,1)S(1)}, f32[1,832]{1,0:T(1,128)S(1)}, f32[512,1600]{1,0:T(8,128)}, bf16[512,1664]{1,0:T(8,128)(2,1)S(1)}) custom-call(bf16[128,1664]{1,0:T(8,128)(2,1)S(1)} %copy-done.29, bf16[128,1664]{1,0:T(8,128)(2,1)} %collective-permute-done.54.refs_1_, bf16[128,1664]{1,0:T(8,128)(2,1)} %collective-permute-done.55.refs_2_, ...), custom_call_target="tpu_custom_call" | custom-call | flops 5452595200 | bytes 17124608 | tf_op jit(solution)/shard_map/pallas_call | solution.py:259
  552.5 10.3 collective-permute-done.80
  595.9 19.8 %shard_map.292 = (bf16[1024,768]{1,0:T(8,128)(2,1)S(1)}, f32[1,768]{1,0:T(1,128)S(1)}, f32[512,1600]{1,0:T(8,128)}, bf16[512,1664]{1,0:T(8,128)(2,1)S(1)}) custom-call(bf16[128,256]{1,0:T(8,128)(2,1)S(1)} %get-tuple-element.430.refs_0_, bf16[128,256]{1,0:T(8,128)(2,1)S(1)} %get-tuple-element.473.refs_1_, bf16[128,256]{1,0:T(8,128)(2,1)S(1)} %get-tuple-element.471.refs_2_, ...), custom_call_target="tpu_custom_call" | custom-call | flops 5200936960 | bytes 11152384 | tf_op jit(solution)/shard_map/pallas_call | solution.py:259
  683.7 9.2 collective-permute-done.96.refs_1_
  713.0 14.7 %shard_map.294 = (bf16[1024,832]{1,0:T(8,128)(2,1)S(1)}, f32[1,832]{1,0:T(1,128)S(1)}, f32[512,1600]{1,0:T(8,128)}, bf16[512,1664]{1,0:T(8,128)(2,1)}) custom-call(bf16[128,1664]{1,0:T(8,128)(2,1)S(1)} %pad.99.refs_0_, bf16[128,1664]{1,0:T(8,128)(2,1)S(1)} %collective-permute-done.96.refs_1_, bf16[128,1664]{1,0:T(8,128)(2,1)S(1)} %collective-permute-done.97.refs_2_, ...), custom_call_target="tpu_custom_call" | custom-call | flops 5452595200 | bytes 17124608 | tf_op jit(solution)/shard_map/pallas_call | solution.py:259
  739.8 10.1 collective-permute-done.104
  761.6 9.4 fusion.27
  786.8 20.1 %shard_map.296 = (bf16[1024,768]{1,0:T(8,128)(2,1)S(1)}, f32[1,768]{1,0:T(1,128)S(1)}, f32[512,1600]{1,0:T(8,128)}, bf16[512,1664]{1,0:T(8,128)(2,1)S(1)}) custom-call(bf16[128,256]{1,0:T(8,128)(2,1)S(1)} %get-tuple-element.422.refs_0_, bf16[128,256]{1,0:T(8,128)(2,1)S(1)} %get-tuple-element.467.refs_1_, bf16[128,256]{1,0:T(8,128)(2,1)S(1)} %get-tuple-element.465.refs_2_, ...), custom_call_target="tpu_custom_call" | custom-call | flops 5200936960 | bytes 11152384 | tf_op jit(solution)/shard_map/pallas_call | solution.py:259
  857.8 13.7 %collective-permute-done.88 = bf16[128,1664]{1,0:T(8,128)(2,1)S(1)} collective-permute-done((bf16[128,1664]{1,0:T(8,128)(2,1)S(1)}, bf16[128,1664]{1,0:T(8,128)(2,1)S(1)}, u32[]{:S(2)}, u32[]{:S(2)}) %collective-permute-start.88) | collective-permute-done | bytes 426016 | tf_op jit(solution)/shard_map/ppermute | solution.py:102
  904.1 9.6 collective-permute-done.164.other
  (1043 shorter events, 697.4 us)
Async XLA Ops:
  7.2 119.8 %all-gather.11.cloned.1.call-start = ((), (), s32[]{:S(2)}) async-start(), calls=%async_computation.9 | async-start | bytes 2129920 | tf_op jit(solution)/shard_map/all_gather | solution.py:247
  55.1 147.3 %all-gather.9.cloned.1.call-start = ((), (), s32[]{:S(2)}) async-start(), calls=%async_computation.8 | async-start | bytes 3072000 | tf_op jit(solution)/shard_map/all_gather | solution.py:247
  59.9 212.7 %all-gather.13.cloned.1.call-start = ((), (), s32[]{:S(2)}) async-start(), calls=%async_computation.10 | async-start | bytes 3584000 | tf_op jit(solution)/shard_map/all_gather | solution.py:247
  108.7 187.7 %all-gather.21.cloned.1.call-start = ((), (), s32[]{:S(2)}) async-start(), calls=%async_computation.22 | async-start | bytes 3461120 | tf_op jit(solution)/shard_map/all_gather | solution.py:246
  109.3 320.7 %all-gather.15.cloned.1.call-start = ((), (), s32[]{:S(2)}) async-start(), calls=%async_computation.11 | async-start | bytes 3072000 | tf_op jit(solution)/shard_map/all_gather | solution.py:247
  110.1 386.2 %all-gather.17.cloned.1.call-start = ((), (), s32[]{:S(2)}) async-start(), calls=%async_computation.12 | async-start | bytes 3584000 | tf_op jit(solution)/shard_map/all_gather | solution.py:247
  136.6 54.9 %collective-permute-start.31 = (bf16[256,1600]{0,1:T(8,128)(2,1)}, bf16[256,1600]{0,1:T(8,128)(2,1)}, u32[]{:S(2)}, u32[]{:S(2)}) collective-permute-start(bf16[256,1600]{0,1:T(8,128)(2,1)} %copy.262), channel_id=1, source_target_pairs={{0,5},{1,4},{2,7},{3,6},{4,1},{5,0},{6,3},{7,2},{8,13},{9,12},{10,... | collective-permute-start | bytes 2457608 | tf_op jit(solution)/shard_map/ppermute | solution.py:102
  138.7 42.6 %collective-permute-start.12 = (bf16[128,1664]{1,0:T(8,128)(2,1)S(1)}, bf16[128,1664]{1,0:T(8,128)(2,1)S(1)}, u32[]{:S(2)}, u32[]{:S(2)}) collective-permute-start(bf16[128,1664]{1,0:T(8,128)(2,1)S(1)} %pad.82.refs_0_), channel_id=1, source_target_pairs={{0,1},{1,0},{2,3},{3,2},{4,5},{5,4},{6,7},{7,6},{8,9},{9,8},{10,11... | collective-permute-start | bytes 1277960 | tf_op jit(solution)/shard_map/ppermute | solution.py:94
  140.8 55.1 %collective-permute-start.32 = (bf16[256,1600]{0,1:T(8,128)(2,1)}, bf16[256,1600]{0,1:T(8,128)(2,1)}, u32[]{:S(2)}, u32[]{:S(2)}) collective-permute-start(bf16[256,1600]{0,1:T(8,128)(2,1)} %copy.262), channel_id=1, source_target_pairs={{0,2},{2,0},{4,6},{6,4},{1,3},{3,1},{5,7},{7,5},{8,10},{10,8},{12,... | collective-permute-start | bytes 2457608 | tf_op jit(solution)/shard_map/ppermute | solution.py:88
  174.8 344.1 %all-gather.19.cloned.1.call-start = ((), (), s32[]{:S(2)}) async-start(), calls=%async_computation.13 | async-start | bytes 3461120 | tf_op jit(solution)/shard_map/all_gather | solution.py:247
  313.6 50.0 %collective-permute-start.43 = (bf16[512,1664]{1,0:T(8,128)(2,1)}, bf16[512,1664]{1,0:T(8,128)(2,1)}, u32[]{:S(2)}, u32[]{:S(2)}) collective-permute-start(bf16[512,1664]{1,0:T(8,128)(2,1)} %get-tuple-element.148), channel_id=1, source_target_pairs={{0,2},{2,0},{4,6},{6,4},{1,3},{3,1},{5,7},{7,5},{8,10},{10,8},{12,... | collective-permute-start | bytes 5111816 | tf_op jit(solution)/shard_map/ppermute | solution.py:88
  318.7 40.5 %collective-permute-start.67 = (bf16[256,1600]{0,1:T(8,128)(2,1)}, bf16[256,1600]{0,1:T(8,128)(2,1)}, u32[]{:S(2)}, u32[]{:S(2)}) collective-permute-start(bf16[256,1600]{0,1:T(8,128)(2,1)} %copy.280), channel_id=1, source_target_pairs={{0,5},{1,4},{2,7},{3,6},{4,1},{5,0},{6,3},{7,2},{8,13},{9,12},{10,... | collective-permute-start | bytes 2457608 | tf_op jit(solution)/shard_map/ppermute | solution.py:102
  319.2 42.2 %collective-permute-start.68 = (bf16[256,1600]{0,1:T(8,128)(2,1)}, bf16[256,1600]{0,1:T(8,128)(2,1)}, u32[]{:S(2)}, u32[]{:S(2)}) collective-permute-start(bf16[256,1600]{0,1:T(8,128)(2,1)} %copy.280), channel_id=1, source_target_pairs={{0,2},{2,0},{4,6},{6,4},{1,3},{3,1},{5,7},{7,5},{8,10},{10,8},{12,... | collective-permute-start | bytes 2457608 | tf_op jit(solution)/shard_map/ppermute | solution.py:88
  321.6 514.1 %reduce-scatter.13.cloned.1.call-start = ((), (), s32[]{:S(2)}) async-start(), calls=%async_computation.16 | async-start | bytes 3584000 | tf_op jit(solution)/shard_map/reduce_scatter | solution.py:253
  337.2 49.9 %collective-permute-start.54 = (bf16[128,1664]{1,0:T(8,128)(2,1)}, bf16[128,1664]{1,0:T(8,128)(2,1)}, u32[]{:S(2)}, u32[]{:S(2)}) collective-permute-start(bf16[128,1664]{1,0:T(8,128)(2,1)} %pad.92.refs_0_), channel_id=1, source_target_pairs={{0,1},{1,0},{2,3},{3,2},{4,5},{5,4},{6,7},{7,6},{8,9},{9,8},{10,11... | collective-permute-start | bytes 1277960 | tf_op jit(solution)/shard_map/ppermute | solution.py:94
  542.9 300.5 %reduce-scatter.17.cloned.1.call-start = ((), (), s32[]{:S(2)}) async-start(), calls=%async_computation.18 | async-start | bytes 3461120 | tf_op jit(solution)/shard_map/reduce_scatter | solution.py:252
  552.5 334.5 %reduce-scatter.23.cloned.1.call-start = ((), (), s32[]{:S(2)}) async-start(), calls=%async_computation.21 | async-start | bytes 1064960 | tf_op jit(solution)/shard_map/reduce_scatter | solution.py:253
  669.4 261.4 %reduce-scatter.19.cloned.1.call-start = ((), (), s32[]{:S(2)}) async-start(), calls=%async_computation.19 | async-start | bytes 3072000 | tf_op jit(solution)/shard_map/reduce_scatter | solution.py:253
  676.5 291.6 %reduce-scatter.15.cloned.1.call-start = ((), (), s32[]{:S(2)}) async-start(), calls=%async_computation.17 | async-start | bytes 3461120 | tf_op jit(solution)/shard_map/reduce_scatter | solution.py:252
  711.4 256.7 %reduce-scatter.11.cloned.1.call-start = ((), (), s32[]{:S(2)}) async-start(), calls=%async_computation.15 | async-start | bytes 3584000 | tf_op jit(solution)/shard_map/reduce_scatter | solution.py:253
  734.3 275.1 %reduce-scatter.9.cloned.1.call-start = ((), (), s32[]{:S(2)}) async-start(), calls=%async_computation.14 | async-start | bytes 3072000 | tf_op jit(solution)/shard_map/reduce_scatter | solution.py:253
  813.7 199.9 %reduce-scatter.21.cloned.1.call-start = ((), (), s32[]{:S(2)}) async-start(), calls=%async_computation.20 | async-start | bytes 1064960 | tf_op jit(solution)/shard_map/reduce_scatter | solution.py:253
  831.5 55.5 %collective-permute-start.111 = (bf16[512,1664]{1,0:T(8,128)(2,1)}, bf16[512,1664]{1,0:T(8,128)(2,1)}, u32[]{:S(2)}, u32[]{:S(2)}) collective-permute-start(bf16[512,1664]{1,0:T(8,128)(2,1)} %copy-done.42), channel_id=1, source_target_pairs={{0,2},{2,0},{4,6},{6,4},{1,3},{3,1},{5,7},{7,5},{8,10},{10,8},{12,... | collective-permute-start | bytes 5111816 | tf_op jit(solution)/shard_map/ppermute | solution.py:88
  901.2 38.9 %collective-permute-start.143 = (bf16[128,1664]{1,0:T(8,128)(2,1)}, bf16[128,1664]{1,0:T(8,128)(2,1)}, u32[]{:S(2)}, u32[]{:S(2)}) collective-permute-start(bf16[128,1664]{1,0:T(8,128)(2,1)} %pad.101.refs_0_), channel_id=1, source_target_pairs={{0,5},{1,4},{2,7},{3,6},{4,1},{5,0},{6,3},{7,2},{8,13},{9,12},{10,... | collective-permute-start | bytes 1277960 | tf_op jit(solution)/shard_map/ppermute | solution.py:102
  (307 other events, 4902.0 us)
Sparse Core Ops, SparseCore 0:
  55.2 71.7 all-gather.10
  128.6 50.7 all-gather.8
  181.5 57.4 all-gather.12
  240.5 55.8 all-gather.20
  297.8 50.6 all-gather.14
  349.9 57.4 all-gather.16
  409.0 55.8 all-gather.18
  543.0 53.9 reduce-scatter.12
  599.3 54.4 reduce-scatter.16
  669.5 22.7 reduce-scatter.22
  694.6 48.9 reduce-scatter.18
  745.7 54.1 reduce-scatter.14
  802.2 55.9 reduce-scatter.10
  860.3 49.3 reduce-scatter.8
  961.8 23.1 reduce-scatter.20

commit v4 on v3

--- a/solution.py
+++ b/solution.py
@@ -1007,17 +1007,12 @@
         (gain1, shift1, _, _, bias_out, gain2, shift2, bias_down), bias_qkv, bias_up = vecs[layer]
         unit1, inv1 = norm_parts(hidden)
         pieces = plan.gather_pieces(widen((unit1 * gain1 + shift1).astype(BF)))
-        if layer == layers - 1:
-            grad_pieces = plan.gather_pieces(widen(grad.astype(BF)))
-            pieces, grad_pieces = lax.optimization_barrier((pieces, grad_pieces))
-        normed, packed, lse, mixed = attend(
-            plan, pieces, qkv_w, bias_qkv, codes, total, scale
-        )
         if layer == 0:
-            out_w = jnp.concatenate(plan.gather_pieces(out_block(0)))
+            grad_pieces = plan.gather_pieces(widen(after(grad.astype(BF), pieces)))
+        normed, packed, lse, mixed = attend(plan, pieces, qkv_w, bias_qkv, codes, total, scale)
+        out_w = out_block(layer)
+        out_w = jnp.concatenate(plan.gather_pieces(after(out_w, pieces) if layer else out_w))
         weights[layer] = qkv_w, out_w, up_w, down_w
-        if layer < layers - 1:
-            next_out = plan.gather_pieces(after(out_block(layer + 1), packed))
         mixed = jnp.concatenate(plan.exchange(mixed), axis=1)
         mixed = dot(mixed, select).astype(BF)
         block = nz * part_rows
@@ -1050,7 +1045,6 @@
         )
         if layer < layers - 1:
             hidden = middle + (plan.scatter_parts(near, far) + bias_down)
-            out_w = jnp.concatenate(next_out)
 
     def late_up(up, layer):
         up = plan.to_owners(up)
@@ -1136,6 +1130,11 @@
         if late is not None:
             above = layer + 1
             out = scatter_seq(down_grad(plan, *late[2], width))
+            if above == layers - 1:
+                last_down = weights[above][3]
+                parts = lower_units(plan, after(kept[above][-1], late[2][0]), last_down)
+                hidden = middle + (plan.scatter_parts(*parts) + bias_down)
+                output = plan.regroup(hidden.astype(BF), back=True)
             into_up = late_up(late[0], above)
             into_down = late_down(late[1], above)
             into_out = late_out(out, above)
@@ -1157,10 +1156,6 @@
         )
         g_mixed = plan.exchange(g_mixed)
         att_pieces = plan.gather_pieces(widen(g_att))
-        if late is None:
-            near, far = lower_units(plan, after(activated, g_mixed), down_w)
-            hidden = middle + (plan.scatter_parts(near, far) + bias_down)
-            output = plan.regroup(hidden.astype(BF), back=True)
         g_packed, g_b, near, far = attend_back(
             plan, g_mixed, packed, lse, codes, qkv_w, total, scale
         )
@@ -1173,7 +1168,7 @@
         if layer == 0:
             into_up = late_up(up, layer)
             into_down = late_down(down, layer)
-        late = (up, down, (after(mixed, g_n1), att_pieces), qkv)
+        late = (up, down, (after(mixed, g_n1 if layer else grad_qkv), att_pieces), qkv)
         smalls[layer] = (
             jnp.sum(g_n1 * unit1, axis=0),
             jnp.sum(g_n1, axis=0),

time: 1070 us -> 1100 us (1.028)
  starting transfers between devices: 177 us -> 196 us
  waiting for transfers between devices: 390 us -> 405 us
    ppermute x33, waiting for transfers between devices: 102 us -> 147 us  [swap_y(): return lax.ppermute(v, 'fsdp', [(f, f ^ 2) for f in range(self.nf)])]
    ppermute x27, waiting for transfers between devices: 97.5 us -> 57.5 us  [swap_xy(): return lax.ppermute(v, GROUP, pairs)]
    ppermute x33, starting transfers between devices: 55.5 us -> 70.5 us  [swap_y(): return lax.ppermute(v, 'fsdp', [(f, f ^ 2) for f in range(self.nf)])]
    unnamed x352 -> x298, local copies, waits for them, and re-layouts: 99.3 us -> 110 us
  transfers between devices with their start and end apart: 180 -> 180, of which waited for: 69 -> 71; matrix products, arithmetic and copies ran while one was open for 19% -> 17% of each run, Pallas kernels for 18% -> 17%
where the time goes in v4:
time: 1100 us; the launch traced here: 1080 us
  waiting for transfers between devices  405 us (37%)
  Pallas kernels  207 us (19%)
  starting transfers between devices  196 us (18%)
  local copies, waits for them, and re-layouts  179 us (16%)
  other arithmetic  42.9 us (4%)
  matrix products  31.7 us (3%)
  between operations  16.8 us (2%)
    pallas_call x27, Pallas kernels, call(): pl.pallas_call(kernel, out_shape=tuple(outs), scratch_shapes=scratch, com...  184 us
    ppermute x33, waiting for transfers between devices, swap_y(): return lax.ppermute(v, 'fsdp', [(f, f ^ 2) for f in range(self.nf)])  147 us
    ppermute x32, waiting for transfers between devices, swap_x(): return lax.ppermute(v, 'replica', [(r, r ^ 1) for r in range(self.nr)])  145 us
    unnamed x298, local copies, waits for them, and re-layouts  110 us
    ppermute x33, starting transfers between devices, swap_y(): return lax.ppermute(v, 'fsdp', [(f, f ^ 2) for f in range(self.nf)])  70.5 us
    ppermute x27, waiting for transfers between devices, swap_xy(): return lax.ppermute(v, GROUP, pairs)  57.5 us
    ppermute x32, starting transfers between devices, swap_x(): return lax.ppermute(v, 'replica', [(r, r ^ 1) for r in range(self.nr)])  41 us
    ppermute x27, starting transfers between devices, swap_xy(): return lax.ppermute(v, GROUP, pairs)  36.5 us
  transfers between devices with their start and end apart: 180, of which 71 were waited for; matrix products, arithmetic and copies ran while one was open for 17% of the time, Pallas kernels for 17%

profile of v4, /device:TPU:0, one launch (start us, length us, event | category | flops | bytes accessed | tf_op | source)
XLA Modules:
  0.0 1078.0 jit_solution(10348115455389560887)
XLA Ops:
  63.6 19.1 %collective-permute-start.22 = (bf16[2,100,768]{2,1,0:T(8,128)(2,1)}, bf16[2,100,768]{2,1,0:T(8,128)(2,1)}, u32[]{:S(2)}, u32[]{:S(2)}) collective-permute-start(bf16[2,100,768]{2,1,0:T(8,128)(2,1)} %get-tuple-element.362), channel_id=1, source_target_pairs={{0,4},{2,6},{4,0},{6,2},{1,5},{3,7},{5,1},{7,3},{8,12},{10,14},{12... | collective-permute-start | bytes 921608 | tf_op jit(solution)/shard_map/ppermute | solution.py:91
  113.7 13.4 %all-gather.11.cloned.1.call-done = bf16[512,1600]{1,0:T(8,128)(2,1)} async-done(((bf16[128,1600]{1,0:T(8,128)(2,1)}), bf16[512,1600]{1,0:T(8,128)(2,1)}) %all-gather.11.cloned.1.call-update) | async-done | bytes 1638416 | tf_op jit(solution)/shard_map/all_gather | solution.py:247
  141.5 13.7 %collective-permute-done.29 = bf16[256,1600]{0,1:T(8,128)(2,1)S(1)} collective-permute-done((bf16[256,1600]{0,1:T(8,128)(2,1)}, bf16[256,1600]{0,1:T(8,128)(2,1)S(1)}, u32[]{:S(2)}, u32[]{:S(2)}) %collective-permute-start.29) | collective-permute-done | bytes 819232 | tf_op jit(solution)/shard_map/ppermute | solution.py:94
  155.5 19.3 %collective-permute-done.30 = bf16[256,1600]{0,1:T(8,128)(2,1)} collective-permute-done((bf16[256,1600]{0,1:T(8,128)(2,1)}, bf16[256,1600]{0,1:T(8,128)(2,1)}, u32[]{:S(2)}, u32[]{:S(2)}) %collective-permute-start.30) | collective-permute-done | bytes 819232 | tf_op jit(solution)/shard_map/ppermute | solution.py:91
  181.9 9.6 collective-permute-done.13.refs_2_
  204.8 17.7 %shard_map.282 = (bf16[1024,1600]{1,0:T(8,128)(2,1)}, bf16[1024,768]{1,0:T(8,128)(2,1)S(1)}, f32[8,1024]{1,0:T(8,128)S(1)}, bf16[1024,256]{1,0:T(8,128)(2,1)S(1)}) custom-call(bf16[128,1664]{1,0:T(8,128)(2,1)S(1)} %pad.82.refs_0_, bf16[128,1664]{1,0:T(8,128)(2,1)S(1)} %collective-permute-done.12.refs_1_, ...), custom_call_target="tpu_custom_call" | custom-call | flops 3590324224 | bytes 11283456 | tf_op jit(solution)/shard_map/pallas_call | solution.py:259
  275.6 20.2 %all-gather.21.cloned.1.call-done.refs_10_.refs_9_ = bf16[832,1600]{1,0:T(8,128)(2,1)} async-done(((bf16[208,1600]{1,0:T(8,128)(2,1)}), bf16[832,1600]{1,0:T(8,128)(2,1)}) %all-gather.21.cloned.1.call-update) | async-done | bytes 2662416 | tf_op jit(solution)/shard_map/all_gather | solution.py:246
  295.8 13.7 %shard_map.283 = (bf16[1024,1600]{1,0:T(8,128)(2,1)}, bf16[1024,832]{1,0:T(8,128)(2,1)S(1)}, bf16[1024,832]{1,0:T(8,128)(2,1)S(1)}, f32[512,1600]{1,0:T(8,128)}, bf16[512,1664]{1,0:T(8,128)(2,1)}) custom-call(bf16[128,1664]{1,0:T(8,128)(2,1)S(1)} %pad.89.refs_0_, bf16[128,1664]{1,0:T(8,128)(2,1)S(1)} %collective-permute-done.36.refs_1_, ...), custom_call_target="tpu_custom_call" | custom-call | flops 5452595200 | bytes 20401408 | tf_op jit(solution)/shard_map/pallas_call | solution.py:259
  322.8 10.1 collective-permute-done.44
  346.8 9.2 collective-permute-done.47.refs_1_
  356.0 9.4 collective-permute-done.48.refs_2_
  375.5 18.0 %shard_map.285 = (bf16[1024,1600]{1,0:T(8,128)(2,1)}, bf16[1024,768]{1,0:T(8,128)(2,1)S(1)}, f32[8,1024]{1,0:T(8,128)S(1)}, bf16[1024,256]{1,0:T(8,128)(2,1)S(1)}) custom-call(bf16[128,1664]{1,0:T(8,128)(2,1)S(1)} %pad.91.refs_0_, bf16[128,1664]{1,0:T(8,128)(2,1)S(1)} %collective-permute-done.47.refs_1_, ...), custom_call_target="tpu_custom_call" | custom-call | flops 3590324224 | bytes 11283456 | tf_op jit(solution)/shard_map/pallas_call | solution.py:259
  397.2 18.9 %collective-permute-done.55 = bf16[256,256]{1,0:T(8,128)(2,1)S(1)} collective-permute-done((bf16[256,256]{1,0:T(8,128)(2,1)S(1)}, bf16[256,256]{1,0:T(8,128)(2,1)S(1)}, u32[]{:S(2)}, u32[]{:S(2)}) %collective-permute-start.55) | collective-permute-done | bytes 131104 | tf_op jit(solution)/shard_map/ppermute | solution.py:94
  476.0 17.4 %collective-permute-done.66.refs_2_ = bf16[128,1664]{1,0:T(8,128)(2,1)S(1)} collective-permute-done((bf16[128,1664]{1,0:T(8,128)(2,1)S(1)}, bf16[128,1664]{1,0:T(8,128)(2,1)S(1)}, u32[]{:S(2)}, u32[]{:S(2)}) %collective-permute-start.66) | collective-permute-done | bytes 426016 | tf_op jit(solution)/shard_map/ppermute | solution.py:91
  521.6 14.4 %shard_map.288 = (bf16[1024,832]{1,0:T(8,128)(2,1)S(1)}, f32[1,832]{1,0:T(1,128)S(1)}, f32[512,1600]{1,0:T(8,128)}, bf16[512,1664]{1,0:T(8,128)(2,1)S(1)}) custom-call(bf16[128,1664]{1,0:T(8,128)(2,1)S(1)} %pad.98.refs_0_, bf16[128,1664]{1,0:T(8,128)(2,1)S(1)} %collective-permute-done.76.refs_1_, bf16[128,1664]{1,0:T(8,128)(2,1)S(1)} %collective-permute-done.77.refs_2_, ...), custom_call_target="tpu_custom_call" | custom-call | flops 5452595200 | bytes 17124608 | tf_op jit(solution)/shard_map/pallas_call | solution.py:259
  553.6 10.3 collective-permute-done.84
  596.6 19.9 %shard_map.290 = (bf16[1024,768]{1,0:T(8,128)(2,1)S(1)}, f32[1,768]{1,0:T(1,128)S(1)}, f32[512,1600]{1,0:T(8,128)}, bf16[512,1664]{1,0:T(8,128)(2,1)S(1)}) custom-call(bf16[128,256]{1,0:T(8,128)(2,1)S(1)} %get-tuple-element.392.refs_0_, bf16[128,256]{1,0:T(8,128)(2,1)S(1)} %get-tuple-element.443.refs_1_, bf16[128,256]{1,0:T(8,128)(2,1)S(1)} %get-tuple-element.441.refs_2_, ...), custom_call_target="tpu_custom_call" | custom-call | flops 5200936960 | bytes 11152384 | tf_op jit(solution)/shard_map/pallas_call | solution.py:259
  642.4 16.4 %collective-permute-done.158.refs_2_ = bf16[128,1664]{1,0:T(8,128)(2,1)S(1)} collective-permute-done((bf16[128,1664]{1,0:T(8,128)(2,1)S(1)}, bf16[128,1664]{1,0:T(8,128)(2,1)S(1)}, u32[]{:S(2)}, u32[]{:S(2)}) %collective-permute-start.158) | collective-permute-done | bytes 426016 | tf_op jit(solution)/shard_map/ppermute | solution.py:91
  714.5 14.2 %shard_map.294 = (bf16[1024,832]{1,0:T(8,128)(2,1)S(1)}, f32[1,832]{1,0:T(1,128)S(1)}, f32[512,1600]{1,0:T(8,128)}, bf16[512,1664]{1,0:T(8,128)(2,1)S(1)}) custom-call(bf16[128,1664]{1,0:T(8,128)(2,1)S(1)} %pad.99.refs_0_, bf16[128,1664]{1,0:T(8,128)(2,1)S(1)} %collective-permute-done.100.refs_1_, bf16[128,1664]{1,0:T(8,128)(2,1)S(1)} %collective-permute-done.101.refs_2_, ...), custom_call_target="tpu_custom_call" | custom-call | flops 5452595200 | bytes 17124608 | tf_op jit(solution)/shard_map/pallas_call | solution.py:259
  794.6 18.8 %collective-permute-done.114 = bf16[256,256]{1,0:T(8,128)(2,1)S(1)} collective-permute-done((bf16[256,256]{1,0:T(8,128)(2,1)S(1)}, bf16[256,256]{1,0:T(8,128)(2,1)S(1)}, u32[]{:S(2)}, u32[]{:S(2)}) %collective-permute-start.114) | collective-permute-done | bytes 131104 | tf_op jit(solution)/shard_map/ppermute | solution.py:102
  823.4 20.4 %shard_map.296 = (bf16[1024,768]{1,0:T(8,128)(2,1)S(1)}, f32[1,768]{1,0:T(1,128)S(1)}, f32[512,1600]{1,0:T(8,128)}, bf16[512,1664]{1,0:T(8,128)(2,1)}) custom-call(bf16[128,256]{1,0:T(8,128)(2,1)S(1)} %get-tuple-element.384.refs_0_, bf16[128,256]{1,0:T(8,128)(2,1)S(1)} %get-tuple-element.437.refs_1_, bf16[128,256]{1,0:T(8,128)(2,1)S(1)} %get-tuple-element.435.refs_2_, ...), custom_call_target="tpu_custom_call" | custom-call | flops 5200936960 | bytes 11152384 | tf_op jit(solution)/shard_map/pallas_call | solution.py:259
  909.9 9.4 collective-permute-done.164.other
  966.5 14.5 %collective-permute-start.125 = (f32[2,2,1280]{2,1,0:T(2,128)S(1)}, f32[2,2,1280]{2,1,0:T(2,128)}, u32[]{:S(2)}, u32[]{:S(2)}) collective-permute-start(f32[2,2,1280]{2,1,0:T(2,128)S(1)} %pad_maximum_fusion.36), channel_id=1, source_target_pairs={{0,4},{2,6},{4,0},{6,2},{1,5},{3,7},{5,1},{7,3},{8,12},{10,14},{12... | collective-permute-start | bytes 61448 | tf_op jit(solution)/shard_map/ppermute | solution.py:91
  1043.6 13.5 %collective-permute-done.143.refs_2_ = bf16[2,100,768]{2,1,0:T(8,128)(2,1)S(1)} collective-permute-done((bf16[2,100,768]{2,1,0:T(8,128)(2,1)S(1)}, bf16[2,100,768]{2,1,0:T(8,128)(2,1)S(1)}, u32[]{:S(2)}, u32[]{:S(2)}) %collective-permute-start.143) | collective-permute-done | bytes 307232 | tf_op jit(solution)/shard_map/ppermute | solution.py:91
  (990 shorter events, 699.9 us)
Async XLA Ops:
  7.2 119.8 %all-gather.11.cloned.1.call-start = ((), (), s32[]{:S(2)}) async-start(), calls=%async_computation.9 | async-start | bytes 2129920 | tf_op jit(solution)/shard_map/all_gather | solution.py:247
  55.1 148.0 %all-gather.9.cloned.1.call-start = ((), (), s32[]{:S(2)}) async-start(), calls=%async_computation.8 | async-start | bytes 3072000 | tf_op jit(solution)/shard_map/all_gather | solution.py:247
  60.0 215.6 %all-gather.13.cloned.1.call-start = ((), (), s32[]{:S(2)}) async-start(), calls=%async_computation.10 | async-start | bytes 3584000 | tf_op jit(solution)/shard_map/all_gather | solution.py:247
  108.7 187.1 %all-gather.21.cloned.1.call-start = ((), (), s32[]{:S(2)}) async-start(), calls=%async_computation.22 | async-start | bytes 3461120 | tf_op jit(solution)/shard_map/all_gather | solution.py:246
  109.5 264.3 %all-gather.15.cloned.1.call-start = ((), (), s32[]{:S(2)}) async-start(), calls=%async_computation.11 | async-start | bytes 3072000 | tf_op jit(solution)/shard_map/all_gather | solution.py:247
  176.1 321.2 %all-gather.17.cloned.1.call-start = ((), (), s32[]{:S(2)}) async-start(), calls=%async_computation.12 | async-start | bytes 3584000 | tf_op jit(solution)/shard_map/all_gather | solution.py:247
  312.0 208.1 %all-gather.19.cloned.1.call-start = ((), (), s32[]{:S(2)}) async-start(), calls=%async_computation.13 | async-start | bytes 3461120 | tf_op jit(solution)/shard_map/all_gather | solution.py:247
  366.2 481.8 %reduce-scatter.13.cloned.1.call-start = ((), (), s32[]{:S(2)}) async-start(), calls=%async_computation.16 | async-start | bytes 3584000 | tf_op jit(solution)/shard_map/reduce_scatter | solution.py:253
  366.3 100.4 %collective-permute-start.76 = (bf16[128,1664]{1,0:T(8,128)(2,1)S(1)}, bf16[128,1664]{1,0:T(8,128)(2,1)S(1)}, u32[]{:S(2)}, u32[]{:S(2)}) collective-permute-start(bf16[128,1664]{1,0:T(8,128)(2,1)S(1)} %pad.98.refs_0_), channel_id=1, source_target_pairs={{0,1},{1,0},{2,3},{3,2},{4,5},{5,4},{6,7},{7,6},{8,9},{9,8},{10,11... | collective-permute-start | bytes 1277960 | tf_op jit(solution)/shard_map/ppermute | solution.py:94
  370.3 59.9 %collective-permute-start.58 = (bf16[256,1600]{0,1:T(8,128)(2,1)}, bf16[256,1600]{0,1:T(8,128)(2,1)}, u32[]{:S(2)}, u32[]{:S(2)}) collective-permute-start(bf16[256,1600]{0,1:T(8,128)(2,1)} %copy.279), channel_id=1, source_target_pairs={{0,1},{1,0},{2,3},{3,2},{4,5},{5,4},{6,7},{7,6},{8,9},{9,8},{10,11... | collective-permute-start | bytes 2457608 | tf_op jit(solution)/shard_map/ppermute | solution.py:94
  371.2 61.3 %collective-permute-start.59 = (bf16[256,1600]{0,1:T(8,128)(2,1)}, bf16[256,1600]{0,1:T(8,128)(2,1)}, u32[]{:S(2)}, u32[]{:S(2)}) collective-permute-start(bf16[256,1600]{0,1:T(8,128)(2,1)} %copy.279), channel_id=1, source_target_pairs={{0,4},{2,6},{4,0},{6,2},{1,5},{3,7},{5,1},{7,3},{8,12},{10,14},{12... | collective-permute-start | bytes 2457608 | tf_op jit(solution)/shard_map/ppermute | solution.py:91
  372.3 60.2 %collective-permute-start.60 = (bf16[256,1600]{0,1:T(8,128)(2,1)}, bf16[256,1600]{0,1:T(8,128)(2,1)}, u32[]{:S(2)}, u32[]{:S(2)}) collective-permute-start(bf16[256,1600]{0,1:T(8,128)(2,1)} %copy.279), channel_id=1, source_target_pairs={{0,5},{1,4},{2,7},{3,6},{4,1},{5,0},{6,3},{7,2},{8,13},{9,12},{10,... | collective-permute-start | bytes 2457608 | tf_op jit(solution)/shard_map/ppermute | solution.py:102
  543.9 318.5 %reduce-scatter.17.cloned.1.call-start = ((), (), s32[]{:S(2)}) async-start(), calls=%async_computation.18 | async-start | bytes 3461120 | tf_op jit(solution)/shard_map/reduce_scatter | solution.py:252
  553.5 344.5 %reduce-scatter.23.cloned.1.call-start = ((), (), s32[]{:S(2)}) async-start(), calls=%async_computation.21 | async-start | bytes 1064960 | tf_op jit(solution)/shard_map/reduce_scatter | solution.py:253
  671.4 261.2 %reduce-scatter.19.cloned.1.call-start = ((), (), s32[]{:S(2)}) async-start(), calls=%async_computation.19 | async-start | bytes 3072000 | tf_op jit(solution)/shard_map/reduce_scatter | solution.py:253
  678.5 305.6 %reduce-scatter.15.cloned.1.call-start = ((), (), s32[]{:S(2)}) async-start(), calls=%async_computation.17 | async-start | bytes 3461120 | tf_op jit(solution)/shard_map/reduce_scatter | solution.py:252
  713.0 272.6 %reduce-scatter.11.cloned.1.call-start = ((), (), s32[]{:S(2)}) async-start(), calls=%async_computation.15 | async-start | bytes 3584000 | tf_op jit(solution)/shard_map/reduce_scatter | solution.py:253
  756.0 247.1 %reduce-scatter.21.cloned.1.call-start = ((), (), s32[]{:S(2)}) async-start(), calls=%async_computation.20 | async-start | bytes 1064960 | tf_op jit(solution)/shard_map/reduce_scatter | solution.py:253
  788.9 85.9 %collective-permute-start.95 = (bf16[512,1664]{1,0:T(8,128)(2,1)}, bf16[512,1664]{1,0:T(8,128)(2,1)}, u32[]{:S(2)}, u32[]{:S(2)}) collective-permute-start(bf16[512,1664]{1,0:T(8,128)(2,1)} %get-tuple-element.171), channel_id=1, source_target_pairs={{0,2},{2,0},{4,6},{6,4},{1,3},{3,1},{5,7},{7,5},{8,10},{10,8},{12,... | collective-permute-start | bytes 5111816 | tf_op jit(solution)/shard_map/ppermute | solution.py:88
  789.5 55.5 %collective-permute-start.145 = (bf16[128,1664]{1,0:T(8,128)(2,1)S(1)}, bf16[128,1664]{1,0:T(8,128)(2,1)}, u32[]{:S(2)}, u32[]{:S(2)}) collective-permute-start(bf16[128,1664]{1,0:T(8,128)(2,1)S(1)} %pad.101.refs_0_), channel_id=1, source_target_pairs={{0,1},{1,0},{2,3},{3,2},{4,5},{5,4},{6,7},{7,6},{8,9},{9,8},{10,11... | collective-permute-start | bytes 1277960 | tf_op jit(solution)/shard_map/ppermute | solution.py:94
  790.1 56.0 %collective-permute-start.146 = (bf16[128,1664]{1,0:T(8,128)(2,1)S(1)}, bf16[128,1664]{1,0:T(8,128)(2,1)}, u32[]{:S(2)}, u32[]{:S(2)}) collective-permute-start(bf16[128,1664]{1,0:T(8,128)(2,1)S(1)} %pad.101.refs_0_), channel_id=1, source_target_pairs={{0,4},{2,6},{4,0},{6,2},{1,5},{3,7},{5,1},{7,3},{8,12},{10,14},{12... | collective-permute-start | bytes 1277960 | tf_op jit(solution)/shard_map/ppermute | solution.py:91
  844.9 74.5 %collective-permute-start.115 = (bf16[512,1664]{1,0:T(8,128)(2,1)}, bf16[512,1664]{1,0:T(8,128)(2,1)}, u32[]{:S(2)}, u32[]{:S(2)}) collective-permute-start(bf16[512,1664]{1,0:T(8,128)(2,1)} %get-tuple-element.186), channel_id=1, source_target_pairs={{0,2},{2,0},{4,6},{6,4},{1,3},{3,1},{5,7},{7,5},{8,10},{10,8},{12,... | collective-permute-start | bytes 5111816 | tf_op jit(solution)/shard_map/ppermute | solution.py:88
  869.9 156.1 %reduce-scatter.9.cloned.1.call-start = ((), (), s32[]{:S(2)}) async-start(), calls=%async_computation.14 | async-start | bytes 3072000 | tf_op jit(solution)/shard_map/reduce_scatter | solution.py:253
  927.7 59.8 %collective-permute-start.99 = (bf16[128,1600]{1,0:T(8,128)(2,1)}, bf16[128,1600]{1,0:T(8,128)(2,1)}, u32[]{:S(2)}, u32[]{:S(2)}) collective-permute-start(bf16[128,1600]{1,0:T(8,128)(2,1)} %add_convert_fusion), channel_id=1, source_target_pairs={{0,0},{9,1},{20,4},{29,5},{2,2},{11,3},{22,6},{31,7},{1,8},{8,9},{... | collective-permute-start | bytes 1228808 | tf_op jit(solution)/shard_map/ppermute | solution.py:85
  (281 other events, 4360.8 us)
Sparse Core Ops, SparseCore 0:
  55.2 71.7 all-gather.10
  128.6 50.7 all-gather.8
  180.9 57.4 all-gather.12
  239.9 55.8 all-gather.20
  297.2 50.6 all-gather.14
  349.3 57.4 all-gather.16
  408.4 55.8 all-gather.18
  544.0 54.0 reduce-scatter.12
  600.5 54.4 reduce-scatter.16
  671.5 22.1 reduce-scatter.22
  696.0 48.8 reduce-scatter.18
  747.1 54.1 reduce-scatter.14
  803.6 55.8 reduce-scatter.10
  870.0 22.0 reduce-scatter.20
  934.2 49.5 reduce-scatter.8

commit v5 on v4

--- a/solution.py
+++ b/solution.py
@@ -13,11 +13,13 @@
 HD = 64
 BF = jnp.bfloat16
 F32 = jnp.float32
-ALL = ("seq", "fsdp", "replica")
-GROUP = ("fsdp", "replica")
-OWNERS = ("seq", "fsdp")
 CODE = 65536
 LOW = -1e30
+SEQ, FSDP, REPLICA = "seq", "fsdp", "replica"
+QK, PV, PK = "sqhd,skhd->shqk", "shqk,skhd->sqhd", "shqk,sqhd->skhd"
+ALL = (SEQ, FSDP, REPLICA)
+GROUP = (FSDP, REPLICA)
+OWNERS = (SEQ, FSDP)
 
 
 def dot(a, b, ca=1, cb=0):
@@ -48,9 +50,9 @@
 
 class Plan:
     def __init__(self, mesh):
-        self.nz = mesh.shape["seq"]
-        self.nf = mesh.shape["fsdp"]
-        self.nr = mesh.shape["replica"]
+        self.nz = mesh.shape[SEQ]
+        self.nf = mesh.shape[FSDP]
+        self.nr = mesh.shape[REPLICA]
         self.group = self.nf * self.nr
         self.cube = self.nf == 4 and self.nr == 2
         self.heads = 2 * -(-HEADS // (2 * self.group))
@@ -70,7 +72,7 @@
         return (f % 2) * half + (f // 2) * self.nr + r
 
     def rank(self):
-        return self.rank_of(lax.axis_index("fsdp"), lax.axis_index("replica"))
+        return self.rank_of(lax.axis_index(FSDP), lax.axis_index(REPLICA))
 
     def regroup(self, v, back=False):
         nz = self.nz
@@ -85,13 +87,13 @@
         return lax.ppermute(v, ALL, pairs)
 
     def swap_core(self, v):
-        return lax.ppermute(v, "fsdp", [(f, f ^ 1) for f in range(self.nf)])
+        return lax.ppermute(v, FSDP, [(f, f ^ 1) for f in range(self.nf)])
 
     def swap_y(self, v):
-        return lax.ppermute(v, "fsdp", [(f, f ^ 2) for f in range(self.nf)])
+        return lax.ppermute(v, FSDP, [(f, f ^ 2) for f in range(self.nf)])
 
     def swap_x(self, v):
-        return lax.ppermute(v, "replica", [(r, r ^ 1) for r in range(self.nr)])
+        return lax.ppermute(v, REPLICA, [(r, r ^ 1) for r in range(self.nr)])
 
     def swap_xy(self, v):
         pairs = [
@@ -155,7 +157,7 @@
         return [pair[0] for pair in out] + [pair[1] for pair in out]
 
     def flips(self, v):
-        f = lax.axis_index("fsdp")
+        f = lax.axis_index(FSDP)
         v = v.reshape((2, 2) + v.shape[1:])
         v = jnp.where(f // 2 == 1, jnp.flip(v, 0), v)
         return jnp.where(f % 2 == 1, jnp.flip(v, 1), v)
@@ -163,9 +165,9 @@
     def gather_owners(self, v):
         if not self.cube or self.nz != 4:
             return lax.all_gather(v, OWNERS, axis=0, tiled=False)
-        z, f = lax.axis_index("seq"), lax.axis_index("fsdp")
+        z, f = lax.axis_index(SEQ), lax.axis_index(FSDP)
         far = [
-            lax.ppermute(v, "seq", [(i, i ^ d) for i in range(4)]) if d else v for d in range(4)
+            lax.ppermute(v, SEQ, [(i, i ^ d) for i in range(4)]) if d else v for d in range(4)
         ]
         v = jnp.stack(far).reshape((2, 2) + v.shape)
         v = jnp.where(z // 2 == 1, jnp.flip(v, 0), v)
@@ -178,7 +180,7 @@
 
     def exchange_fsdp(self, v):
         if not self.cube:
-            return lax.all_to_all(v, "fsdp", split_axis=0, concat_axis=0, tiled=True)
+            return lax.all_to_all(v, FSDP, split_axis=0, concat_axis=0, tiled=True)
         shape = v.shape
         v = self.flips(v)
         both = jnp.stack([v[:, 0], self.swap_core(v[:, 1])], axis=1)
@@ -186,18 +188,18 @@
 
     def scatter_small(self, v):
         if not self.cube or self.nz != 4:
-            return lax.psum_scatter(v, "seq", scatter_dimension=0, tiled=False)
-        z = lax.axis_index("seq")
+            return lax.psum_scatter(v, SEQ, scatter_dimension=0, tiled=False)
+        z = lax.axis_index(SEQ)
         total = lax.dynamic_index_in_dim(v, z, 0, keepdims=False)
         for d in range(1, 4):
             other = lax.dynamic_index_in_dim(v, z ^ d, 0, keepdims=False)
-            total = total + lax.ppermute(other, "seq", [(i, i ^ d) for i in range(4)])
+            total = total + lax.ppermute(other, SEQ, [(i, i ^ d) for i in range(4)])
         return total
 
     def to_owners_small(self, v):
         if not self.cube:
-            v = lax.all_to_all(v, "fsdp", split_axis=0, concat_axis=0, tiled=True)
-            v = lax.all_gather(v, "replica", axis=1, tiled=False)
+            v = lax.all_to_all(v, FSDP, split_axis=0, concat_axis=0, tiled=True)
+            v = lax.all_gather(v, REPLICA, axis=1, tiled=False)
             return jnp.stack([v[m // self.nr, m % self.nr] for m in self.place])
         v = self.flips(v)
         far = self.swap_core(v[:, 1])
@@ -211,7 +213,7 @@
         if not self.cube:
             return self.to_owners_small(v)
         nf, rows, columns = v.shape
-        f = lax.axis_index("fsdp")
+        f = lax.axis_index(FSDP)
         pick = (f ^ jnp.arange(nf, dtype=jnp.int32)).astype(jnp.int32)
         pair = sds((2, rows, columns), BF)
         near, far = pl.pallas_call(
@@ -243,14 +245,14 @@
 
 def gather_seq(v, lead=False):
     if lead:
-        return lax.all_gather(v[None], "seq", axis=1, tiled=True)[0]
-    return lax.all_gather(v, "seq", axis=0, tiled=True)
+        return lax.all_gather(v[None], SEQ, axis=1, tiled=True)[0]
+    return lax.all_gather(v, SEQ, axis=0, tiled=True)
 
 
 def scatter_seq(v, lead=False):
     if lead:
-        return lax.psum_scatter(v[None], "seq", scatter_dimension=1, tiled=True)[0]
-    return lax.psum_scatter(v, "seq", scatter_dimension=0, tiled=True)
+        return lax.psum_scatter(v[None], SEQ, scatter_dimension=1, tiled=True)[0]
+    return lax.psum_scatter(v, SEQ, scatter_dimension=0, tiled=True)
 
 
 def call(kernel, outs, scratch, flops, operands, **more):
@@ -314,6 +316,36 @@
 
 def after(v, other):
     return lax.optimization_barrier((v, other))[0]
+
+
+def project_kernel(count, left, *refs):
+    block = refs[0].shape[0]
+    total = dot(left[:, :block], refs[0][...])
+    for i in range(1, count):
+        total = total + dot(left[:, i * block : (i + 1) * block], refs[i][...])
+    refs[-1][...] = total
+
+
+def project(plan, left, pieces):
+    if not plan.cube:
+        return dot(left, jnp.concatenate(pieces))
+    shape = sds((left.shape[0], pieces[0].shape[1]), F32)
+    kernel = functools.partial(project_kernel, len(pieces))
+    return call(kernel, [shape], [], 2 * left.size * shape.shape[1], [left, *pieces])[0]
+
+
+def project_back_kernel(count, left, *refs):
+    block = refs[0].shape[0]
+    for i in range(count):
+        refs[-1][:, i * block : (i + 1) * block] = dot(left[...], refs[i][...], 1, 1).astype(BF)
+
+
+def project_back(plan, left, pieces):
+    if not plan.cube:
+        return dot(left, jnp.concatenate(pieces), 1, 1).astype(BF)
+    shape = sds((left.shape[0], len(pieces) * pieces[0].shape[0]), BF)
+    kernel = functools.partial(project_back_kernel, len(pieces))
+    return call(kernel, [shape], [], 2 * left.size * shape.shape[1], [left, *pieces])[0]
 
 
 def first_half(shape):
@@ -379,13 +411,13 @@
             for i in range(3)
         )
         allowed = mask_of(codes, total)
-        scores = jnp.einsum("sqhd,skhd->shqk", q, k, preferred_element_type=F32) * scale
+        scores = jnp.einsum(QK, q, k, preferred_element_type=F32) * scale
         scores = jnp.where(allowed[:, None], scores, LOW)
         top = jnp.max(scores, axis=-1, keepdims=True)
         expo = jnp.exp(scores - top)
         denom = jnp.sum(expo, axis=-1, keepdims=True)
         probs = (expo / denom).astype(BF)
-        mixed = jnp.einsum("shqk,skhd->sqhd", probs, v, preferred_element_type=F32)
+        mixed = jnp.einsum(PV, probs, v, preferred_element_type=F32)
         return full, packed, top + jnp.log(denom), mixed.reshape(-1, span).astype(BF)
     tall = count * rows
     return call(
@@ -497,14 +529,14 @@
         )
         gm = jnp.concatenate(pieces).reshape(-1, total, plan.heads, HD)
         allowed = mask_of(codes, total)
-        scores = jnp.einsum("sqhd,skhd->shqk", q, k, preferred_element_type=F32) * scale
+        scores = jnp.einsum(QK, q, k, preferred_element_type=F32) * scale
         probs = jnp.exp(jnp.where(allowed[:, None], scores, LOW) - lse)
-        g_probs = jnp.einsum("sqhd,skhd->shqk", gm, v, preferred_element_type=F32)
-        g_v = jnp.einsum("shqk,sqhd->skhd", probs.astype(BF), gm, preferred_element_type=F32)
+        g_probs = jnp.einsum(QK, gm, v, preferred_element_type=F32)
+        g_v = jnp.einsum(PK, probs.astype(BF), gm, preferred_element_type=F32)
         row = jnp.sum(g_probs * probs, axis=-1, keepdims=True)
         g_s = (probs * (g_probs - row)).astype(BF)
-        g_q = jnp.einsum("shqk,skhd->sqhd", g_s, k, preferred_element_type=F32) * scale
-        g_k = jnp.einsum("shqk,sqhd->skhd", g_s, q, preferred_element_type=F32) * scale
+        g_q = jnp.einsum(PV, g_s, k, preferred_element_type=F32) * scale
+        g_k = jnp.einsum(PK, g_s, q, preferred_element_type=F32) * scale
         g_packed = jnp.concatenate(
             [u.reshape(-1, span).astype(BF) for u in (g_q, g_k, g_v)], axis=1
         )
@@ -765,7 +797,7 @@
     layers, rows, triple = w.shape
     nf, nr, span, group = plan.nf, plan.nr, plan.span, plan.group
     ranks = [[plan.rank_of(f, r) for f in range(nf)] for r in range(nr)]
-    x = lax.axis_index("replica")
+    x = lax.axis_index(REPLICA)
     if not plan.cube:
         width = triple // 3
         v = w.reshape(layers, rows, 3, width)
@@ -785,7 +817,7 @@
 def unit_columns(plan, w, piece, piece_rows):
     layers, rows, _ = w.shape
     nz, nf, nr = plan.nz, plan.nf, plan.nr
-    x = lax.axis_index("replica")
+    x = lax.axis_index(REPLICA)
     if not plan.cube:
         v = w.reshape(layers, rows, nz, nf, nr, piece)
         v = lax.dynamic_index_in_dim(v, x, 4, keepdims=False)
@@ -904,9 +936,9 @@
     length = tokens.shape[1]
     total = length * nz
     scale = 1.0 / math.sqrt(HD)
-    fsdp = lax.axis_index("fsdp")
-    replica = lax.axis_index("replica")
-    seq = lax.axis_index("seq")
+    fsdp = lax.axis_index(FSDP)
+    replica = lax.axis_index(REPLICA)
+    seq = lax.axis_index(SEQ)
     rank = plan.rank()
 
     def down_of(down):
@@ -922,7 +954,7 @@
 
     qkv_send = head_columns(plan, w_qkv)
     first = plan.exchange_fsdp(qkv_send[0]).reshape(nf * own_rows, 3 * span)
-    both = plan.regroup(jnp.concatenate([tokens[0], cotangent[0]]))
+    hidden = plan.regroup(tokens[0]).astype(F32)
     small = jnp.concatenate(
         [norm1_gain, norm1_shift, b_query, b_value, b_out, norm2_gain, norm2_shift, b_down, b_up],
         axis=1,
@@ -939,11 +971,10 @@
     codes = plan.gather_doubling(plan.regroup(codes[None]))
 
     outs = jnp.concatenate([out_of(w_out[layer]) for layer in range(layers)])
-    first, both, qkv_send, w_up, w_down, outs, small, codes = lax.optimization_barrier(
-        (first, both, qkv_send, w_up, w_down, outs, small, codes)
-    )
-    hidden = both[:length].astype(F32)
-    grad = both[length:].astype(F32)
+    first, qkv_send, w_up, w_down, outs, small, codes = lax.optimization_barrier(
+        (first, qkv_send, w_up, w_down, outs, small, codes)
+    )
+    grad = plan.regroup(after(cotangent[0], hidden)).astype(F32)
     up_send = unit_columns(plan, w_up, piece, piece_rows)
     prepared = []
     for layer in range(layers):
@@ -1011,7 +1042,7 @@
             grad_pieces = plan.gather_pieces(widen(after(grad.astype(BF), pieces)))
         normed, packed, lse, mixed = attend(plan, pieces, qkv_w, bias_qkv, codes, total, scale)
         out_w = out_block(layer)
-        out_w = jnp.concatenate(plan.gather_pieces(after(out_w, pieces) if layer else out_w))
+        out_w = plan.gather_pieces(after(out_w, pieces) if layer else out_w)
         weights[layer] = qkv_w, out_w, up_w, down_w
         mixed = jnp.concatenate(plan.exchange(mixed), axis=1)
         mixed = dot(mixed, select).astype(BF)
@@ -1019,7 +1050,7 @@
         mixed_own = plan.exchange(
             jnp.concatenate([mixed[:, i * block : (i + 1) * block] for i in range(group)])
         )
-        middle = hidden + (dot(mixed, out_w) + bias_out)
+        middle = hidden + (project(plan, mixed, out_w) + bias_out)
         unit2, inv2 = norm_parts(middle)
         pieces = plan.gather_pieces(widen((unit2 * gain2 + shift2).astype(BF)))
         if layer == layers - 1:
@@ -1083,7 +1114,7 @@
 
     def late_rows(v, rows, kept, layer, previous):
         if not plan.cube:
-            v = lax.all_gather(v, "replica", axis=0, tiled=False)
+            v = lax.all_gather(v, REPLICA, axis=0, tiled=False)
             v = v[:, :kept].reshape(nr * kept, width)[None, :rows].astype(F32)
             return v if previous is None else jnp.concatenate([v, previous])
         operands = [v, plan.swap_x(v)]
@@ -1131,13 +1162,11 @@
             above = layer + 1
             out = scatter_seq(down_grad(plan, *late[2], width))
             if above == layers - 1:
-                last_down = weights[above][3]
-                parts = lower_units(plan, after(kept[above][-1], late[2][0]), last_down)
-                hidden = middle + (plan.scatter_parts(*parts) + bias_down)
                 output = plan.regroup(hidden.astype(BF), back=True)
             into_up = late_up(late[0], above)
             into_down = late_down(late[1], above)
             into_out = late_out(out, above)
+            into_qkv = late_qkv(late[3], above)
         if late is None:
             grad_pieces, grad_down = lax.optimization_barrier((grad_pieces, grad_down))
         down = scatter_seq(grad_down, lead=True)
@@ -1149,12 +1178,15 @@
         up = scatter_seq(grad_up).reshape(nf, own_rows, units)
         g_mid = grad + norm_pull(g_n2, unit2, inv2, gain2)
         g_att = g_mid.astype(BF)
-        g_mixed = dot(g_att, out_w, 1, 1).astype(BF)
+        g_mixed = project_back(plan, g_att, out_w)
         g_mixed = dot(g_mixed, select, 1, 1).astype(BF)
         g_mixed = jnp.concatenate(
             [g_mixed[:, i * span : (i + 1) * span] for i in range(group)]
         )
         g_mixed = plan.exchange(g_mixed)
+        if late is None:
+            parts = lower_units(plan, after(activated, g_lift), down_w)
+            hidden = middle + (plan.scatter_parts(*parts) + bias_down)
         att_pieces = plan.gather_pieces(widen(g_att))
         g_packed, g_b, near, far = attend_back(
             plan, g_mixed, packed, lse, codes, qkv_w, total, scale
@@ -1163,8 +1195,6 @@
         g_n1 = plan.scatter_parts(near, far)
         qkv = scatter_seq(grad_qkv)
         qkv = qkv.reshape(nf, own_rows, 3 * span)
-        if late is not None:
-            into_qkv = late_qkv(after(late[3], g_n1), above)
         if layer == 0:
             into_up = late_up(up, layer)
             into_down = late_down(down, layer)
@@ -1184,8 +1214,8 @@
             grad_pieces = plan.gather_pieces(widen(grad.astype(BF)))
     out = scatter_seq(down_grad(plan, *late[2], width))
     grad_tokens = plan.regroup(grad.astype(BF), back=True).astype(F32)
+    into_qkv = late_qkv(after(late[3], (into_up, into_down)), 0)
     output = after(output, grad).astype(F32)
-    into_qkv = late_qkv(after(late[3], (into_up, into_down)), 0)
     into_out = late_out(out, 0)
 
     def scattered(layer):
@@ -1236,9 +1266,9 @@
 
 def solution(mesh):
     plan = Plan(mesh)
-    data = P(("fsdp", "replica"), "seq", None)
-    vector = P(None, ("seq", "fsdp"))
-    matrix = P(None, ("seq", "fsdp"), None)
+    data = P((FSDP, REPLICA), SEQ, None)
+    vector = P(None, (SEQ, FSDP))
+    matrix = P(None, (SEQ, FSDP), None)
     weights = (
         vector,
         vector,
@@ -1254,7 +1284,7 @@
         matrix,
         vector,
     )
-    in_specs = (data, data, P(("fsdp", "replica"), "seq")) + weights
+    in_specs = (data, data, P((FSDP, REPLICA), SEQ)) + weights
     out_specs = (data, data) + weights
     return jax.shard_map(
         functools.partial(shards, plan),

time: 1100 us -> 1140 us (1.036)
  starting transfers between devices: 196 us -> 264 us
  waiting for transfers between devices: 405 us -> 375 us
  local copies, waits for them, and re-layouts: 179 us -> 196 us
  matrix products: 31.7 us -> 14.9 us
    ppermute x134, starting transfers between devices: 140 us -> 201 us  [the longest x32 123 us: swap_x(): return lax.ppermute(v, REPLICA, [(r, r ^ 1) for r in range(self.nr)])]
    ppermute x134, waiting for transfers between devices: 313 us -> 274 us  [the longest x32 160 us: swap_x(): return lax.ppermute(v, REPLICA, [(r, r ^ 1) for r in range(self.nr)])]
    ppermute x27, waiting for transfers between devices: 57.5 us -> 89.9 us  [swap_xy(): return lax.ppermute(v, GROUP, pairs)]
    all_gather x7, waiting for transfers between devices: 33.7 us -> 11.2 us  [the longest x1 11.1 us: gather_seq(): return lax.all_gather(v[None], SEQ, axis=1, tiled=True)[0]]
    dot_general x6 -> x4, matrix products: 31.7 us -> 14.9 us  [dot(): lax.dot_general(a, b, (((ca,), (cb,)), ((), ())), preferred_element_type=...]
    unnamed x298 -> x394, local copies, waits for them, and re-layouts: 110 us -> 121 us
    pallas_call x27 -> x31, Pallas kernels: 184 us -> 193 us  [call(): pl.pallas_call(kernel, out_shape=tuple(outs), scratch_shapes=scratch, com...]
  transfers between devices with their start and end apart: 180 -> 181, of which waited for: 71 -> 63; matrix products, arithmetic and copies ran while one was open for 17% -> 13% of each run, Pallas kernels for 17% -> 19%
where the time goes in v5:
time: 1140 us; the launch traced here: 1120 us
  waiting for transfers between devices  375 us (33%)
  starting transfers between devices  264 us (23%)
  Pallas kernels  214 us (19%)
  local copies, waits for them, and re-layouts  196 us (17%)
  other arithmetic  38.1 us (3%)
  between operations  17.3 us (2%)
  matrix products  14.9 us (1%)
    pallas_call x31, Pallas kernels, call(): pl.pallas_call(kernel, out_shape=tuple(outs), scratch_shapes=scratch, com...  193 us
    ppermute x32, waiting for transfers between devices, swap_x(): return lax.ppermute(v, REPLICA, [(r, r ^ 1) for r in range(self.nr)])  160 us
    ppermute x32, starting transfers between devices, swap_x(): return lax.ppermute(v, REPLICA, [(r, r ^ 1) for r in range(self.nr)])  123 us
    unnamed x394, local copies, waits for them, and re-layouts  121 us
    ppermute x33, waiting for transfers between devices, swap_y(): return lax.ppermute(v, FSDP, [(f, f ^ 2) for f in range(self.nf)])  93.9 us
    ppermute x27, waiting for transfers between devices, swap_xy(): return lax.ppermute(v, GROUP, pairs)  89.9 us
    ppermute x33, starting transfers between devices, swap_y(): return lax.ppermute(v, FSDP, [(f, f ^ 2) for f in range(self.nf)])  53 us
    ppermute x27, starting transfers between devices, swap_xy(): return lax.ppermute(v, GROUP, pairs)  44.2 us
  transfers between devices with their start and end apart: 181, of which 63 were waited for; matrix products, arithmetic and copies ran while one was open for 13% of the time, Pallas kernels for 19%

profile of v5, /device:TPU:0, one launch (start us, length us, event | category | flops | bytes accessed | tf_op | source)
XLA Modules:
  0.0 1119.7 jit_solution(13058484716921179328)
XLA Ops:
  88.1 51.5 %collective-permute-start.12 = (bf16[128,1664]{1,0:T(8,128)(2,1)S(1)}, bf16[128,1664]{1,0:T(8,128)(2,1)S(1)}, u32[]{:S(2)}, u32[]{:S(2)}) collective-permute-start(bf16[128,1664]{1,0:T(8,128)(2,1)S(1)} %pad.82.refs_0_), channel_id=1, source_target_pairs={{0,1},{1,0},{2,3},{3,2},{4,5},{5,4},{6,7},{7,6},{8,9},{9,8},{10,11... | collective-permute-start | bytes 1277960 | tf_op jit(solution)/shard_map/ppermute | solution.py:96
  141.6 8.7 collective-permute-done.12.refs_1_
  168.7 18.0 %shard_map.282 = (bf16[1024,1600]{1,0:T(8,128)(2,1)}, bf16[1024,768]{1,0:T(8,128)(2,1)S(1)}, f32[8,1024]{1,0:T(8,128)S(1)}, bf16[1024,256]{1,0:T(8,128)(2,1)S(1)}) custom-call(bf16[128,1664]{1,0:T(8,128)(2,1)S(1)} %pad.82.refs_0_, bf16[128,1664]{1,0:T(8,128)(2,1)S(1)} %collective-permute-done.12.refs_1_, bf16[128,1664]{1,0:T(8,128)(2,1)S(1)} %copy-done.78, ...), custom_call_target="tpu_custom_call" | custom-call | flops 3590324224 | bytes 11283456 | tf_op jit(solution)/shard_map/pallas_call | solution.py:261
  244.0 9.5 collective-permute-done.36.refs_1_
  263.3 11.1 all-gather.21.cloned.1.call-done.refs_10_.refs_9_
  274.3 15.5 %shard_map.284 = (bf16[1024,1600]{1,0:T(8,128)(2,1)}, bf16[1024,832]{1,0:T(8,128)(2,1)S(1)}, bf16[1024,832]{1,0:T(8,128)(2,1)S(1)}, f32[512,1600]{1,0:T(8,128)}, bf16[512,1664]{1,0:T(8,128)(2,1)}) custom-call(bf16[128,1664]{1,0:T(8,128)(2,1)} %pad.89.refs_0_, bf16[128,1664]{1,0:T(8,128)(2,1)} %collective-permute-done.36.refs_1_, ...), custom_call_target="tpu_custom_call" | custom-call | flops 5452595200 | bytes 20401408 | tf_op jit(solution)/shard_map/pallas_call | solution.py:261
  305.4 10.2 collective-permute-done.44
  331.5 9.5 collective-permute-done.47.refs_1_
  341.1 9.3 collective-permute-done.48.refs_2_
  360.7 18.4 %shard_map.286 = (bf16[1024,1600]{1,0:T(8,128)(2,1)}, bf16[1024,768]{1,0:T(8,128)(2,1)S(1)}, f32[8,1024]{1,0:T(8,128)S(1)}, bf16[1024,256]{1,0:T(8,128)(2,1)S(1)}) custom-call(bf16[128,1664]{1,0:T(8,128)(2,1)} %pad.91.refs_0_, bf16[128,1664]{1,0:T(8,128)(2,1)} %collective-permute-done.47.refs_1_, bf16[128,1664]{1,0:T(8,128)(2,1)} %collective-permute-done.48.refs_2_, ...), custom_call_target="tpu_custom_call" | custom-call | flops 3590324224 | bytes 11283456 | tf_op jit(solution)/shard_map/pallas_call | solution.py:261
  383.9 27.5 %collective-permute-start.73 = (bf16[128,1664]{1,0:T(8,128)(2,1)}, bf16[128,1664]{1,0:T(8,128)(2,1)}, u32[]{:S(2)}, u32[]{:S(2)}) collective-permute-start(bf16[128,1664]{1,0:T(8,128)(2,1)} %pad.98.refs_0_), channel_id=1, source_target_pairs={{0,1},{1,0},{2,3},{3,2},{4,5},{5,4},{6,7},{7,6},{8,9},{9,8},{10,11... | collective-permute-start | bytes 1277960 | tf_op jit(solution)/shard_map/ppermute | solution.py:96
  418.2 41.4 %collective-permute-done.55 = bf16[256,256]{1,0:T(8,128)(2,1)S(1)} collective-permute-done((bf16[256,256]{1,0:T(8,128)(2,1)S(1)}, bf16[256,256]{1,0:T(8,128)(2,1)S(1)}, u32[]{:S(2)}, u32[]{:S(2)}) %collective-permute-start.55) | collective-permute-done | bytes 131104 | tf_op jit(solution)/shard_map/ppermute | solution.py:96
  516.5 17.8 %collective-permute-done.66.refs_2_ = bf16[128,1664]{1,0:T(8,128)(2,1)S(1)} collective-permute-done((bf16[128,1664]{1,0:T(8,128)(2,1)S(1)}, bf16[128,1664]{1,0:T(8,128)(2,1)S(1)}, u32[]{:S(2)}, u32[]{:S(2)}) %collective-permute-start.66) | collective-permute-done | bytes 426016 | tf_op jit(solution)/shard_map/ppermute | solution.py:93
  566.4 16.0 %shard_map.290 = (bf16[1024,832]{1,0:T(8,128)(2,1)S(1)}, f32[1,832]{1,0:T(1,128)S(1)}, f32[512,1600]{1,0:T(8,128)}, bf16[512,1664]{1,0:T(8,128)(2,1)}) custom-call(bf16[128,1664]{1,0:T(8,128)(2,1)} %pad.98.refs_0_, bf16[128,1664]{1,0:T(8,128)(2,1)} %collective-permute-done.73.refs_1_, bf16[128,1664]{1,0:T(8,128)(2,1)} %collective-permute-done.74.refs_2_, ...), custom_call_target="tpu_custom_call" | custom-call | flops 5452595200 | bytes 17124608 | tf_op jit(solution)/shard_map/pallas_call | solution.py:261
  667.7 19.7 %shard_map.295 = (bf16[1024,768]{1,0:T(8,128)(2,1)S(1)}, f32[1,768]{1,0:T(1,128)S(1)}, f32[512,1600]{1,0:T(8,128)}, bf16[512,1664]{1,0:T(8,128)(2,1)S(1)}) custom-call(bf16[128,256]{1,0:T(8,128)(2,1)S(1)} %get-tuple-element.386.refs_0_, bf16[128,256]{1,0:T(8,128)(2,1)S(1)} %get-tuple-element.430.refs_1_, bf16[128,256]{1,0:T(8,128)(2,1)S(1)} %get-tuple-element.428.refs_2_, ...), custom_call_target="tpu_custom_call" | custom-call | flops 5200936960 | bytes 11152384 | tf_op jit(solution)/shard_map/pallas_call | solution.py:261
  721.9 8.6 collective-permute-done.156.refs_3_
  730.5 9.1 collective-permute-done.94
  758.2 9.2 collective-permute-done.97.refs_1_
  767.9 8.5 collective-permute-done.99.refs_3_
  794.0 14.6 %shard_map.297 = (bf16[1024,832]{1,0:T(8,128)(2,1)S(1)}, f32[1,832]{1,0:T(1,128)S(1)}, f32[512,1600]{1,0:T(8,128)}, bf16[512,1664]{1,0:T(8,128)(2,1)}) custom-call(bf16[128,1664]{1,0:T(8,128)(2,1)S(1)} %copy-done.65, bf16[128,1664]{1,0:T(8,128)(2,1)S(1)} %copy-done.86, bf16[128,1664]{1,0:T(8,128)(2,1)S(1)} %copy-done.90, bf16[128,1664]{1,0:T(8,128)(2,1)S(1)} %copy-done.92, ...), custom_call_target="tpu_custom_call" | custom-call | flops 5452595200 | bytes 17124608 | tf_op jit(solution)/shard_map/pallas_call | solution.py:261
  865.9 18.8 %collective-permute-done.111 = bf16[256,256]{1,0:T(8,128)(2,1)S(1)} collective-permute-done((bf16[256,256]{1,0:T(8,128)(2,1)S(1)}, bf16[256,256]{1,0:T(8,128)(2,1)S(1)}, u32[]{:S(2)}, u32[]{:S(2)}) %collective-permute-start.111) | collective-permute-done | bytes 131104 | tf_op jit(solution)/shard_map/ppermute | solution.py:104
  894.6 20.3 %shard_map.300 = (bf16[1024,768]{1,0:T(8,128)(2,1)S(1)}, f32[1,768]{1,0:T(1,128)S(1)}, f32[512,1600]{1,0:T(8,128)}, bf16[512,1664]{1,0:T(8,128)(2,1)}) custom-call(bf16[128,256]{1,0:T(8,128)(2,1)S(1)} %get-tuple-element.378.refs_0_, bf16[128,256]{1,0:T(8,128)(2,1)S(1)} %get-tuple-element.424.refs_1_, bf16[128,256]{1,0:T(8,128)(2,1)S(1)} %get-tuple-element.422.refs_2_, ...), custom_call_target="tpu_custom_call" | custom-call | flops 5200936960 | bytes 11152384 | tf_op jit(solution)/shard_map/pallas_call | solution.py:261
  962.9 8.5 collective-permute-done.165.other
  1022.9 20.6 %collective-permute-start.122 = (f32[2,2,1280]{2,1,0:T(2,128)S(1)}, f32[2,2,1280]{2,1,0:T(2,128)S(1)}, u32[]{:S(2)}, u32[]{:S(2)}) collective-permute-start(f32[2,2,1280]{2,1,0:T(2,128)S(1)} %pad_maximum_fusion.35), channel_id=1, source_target_pairs={{0,4},{2,6},{4,0},{6,2},{1,5},{3,7},{5,1},{7,3},{8,12},{10,14},{12... | collective-permute-start | bytes 61448 | tf_op jit(solution)/shard_map/ppermute | solution.py:93
  (1085 shorter events, 700.4 us)
Async XLA Ops:
  7.2 150.9 %all-gather.11.cloned.1.call-start = ((), (), s32[]{:S(2)}) async-start(), calls=%async_computation.9 | async-start | bytes 2129920 | tf_op jit(solution)/shard_map/all_gather | solution.py:249
  47.2 118.4 %all-gather.9.cloned.1.call-start = ((), (), s32[]{:S(2)}) async-start(), calls=%async_computation.8 | async-start | bytes 3072000 | tf_op jit(solution)/shard_map/all_gather | solution.py:249
  52.0 211.2 %all-gather.13.cloned.1.call-start = ((), (), s32[]{:S(2)}) async-start(), calls=%async_computation.10 | async-start | bytes 3584000 | tf_op jit(solution)/shard_map/all_gather | solution.py:249
  83.6 190.7 %all-gather.21.cloned.1.call-start = ((), (), s32[]{:S(2)}) async-start(), calls=%async_computation.22 | async-start | bytes 3461120 | tf_op jit(solution)/shard_map/all_gather | solution.py:248
  85.4 272.5 %all-gather.15.cloned.1.call-start = ((), (), s32[]{:S(2)}) async-start(), calls=%async_computation.11 | async-start | bytes 3072000 | tf_op jit(solution)/shard_map/all_gather | solution.py:249
  88.1 62.2 %collective-permute-start.12 = (bf16[128,1664]{1,0:T(8,128)(2,1)S(1)}, bf16[128,1664]{1,0:T(8,128)(2,1)S(1)}, u32[]{:S(2)}, u32[]{:S(2)}) collective-permute-start(bf16[128,1664]{1,0:T(8,128)(2,1)S(1)} %pad.82.refs_0_), channel_id=1, source_target_pairs={{0,1},{1,0},{2,3},{3,2},{4,5},{5,4},{6,7},{7,6},{8,9},{9,8},{10,11... | collective-permute-start | bytes 1277960 | tf_op jit(solution)/shard_map/ppermute | solution.py:96
  190.2 348.8 %all-gather.17.cloned.1.call-start = ((), (), s32[]{:S(2)}) async-start(), calls=%async_computation.12 | async-start | bytes 3584000 | tf_op jit(solution)/shard_map/all_gather | solution.py:249
  292.3 272.7 %all-gather.19.cloned.1.call-start = ((), (), s32[]{:S(2)}) async-start(), calls=%async_computation.13 | async-start | bytes 3461120 | tf_op jit(solution)/shard_map/all_gather | solution.py:249
  382.0 543.6 %reduce-scatter.17.cloned.1.call-start = ((), (), s32[]{:S(2)}) async-start(), calls=%async_computation.18 | async-start | bytes 3461120 | tf_op jit(solution)/shard_map/reduce_scatter | solution.py:254
  383.9 122.6 %collective-permute-start.73 = (bf16[128,1664]{1,0:T(8,128)(2,1)}, bf16[128,1664]{1,0:T(8,128)(2,1)}, u32[]{:S(2)}, u32[]{:S(2)}) collective-permute-start(bf16[128,1664]{1,0:T(8,128)(2,1)} %pad.98.refs_0_), channel_id=1, source_target_pairs={{0,1},{1,0},{2,3},{3,2},{4,5},{5,4},{6,7},{7,6},{8,9},{9,8},{10,11... | collective-permute-start | bytes 1277960 | tf_op jit(solution)/shard_map/ppermute | solution.py:96
  412.7 58.6 %collective-permute-start.58 = (bf16[256,1600]{0,1:T(8,128)(2,1)}, bf16[256,1600]{0,1:T(8,128)(2,1)}, u32[]{:S(2)}, u32[]{:S(2)}) collective-permute-start(bf16[256,1600]{0,1:T(8,128)(2,1)} %copy.226), channel_id=1, source_target_pairs={{0,1},{1,0},{2,3},{3,2},{4,5},{5,4},{6,7},{7,6},{8,9},{9,8},{10,11... | collective-permute-start | bytes 2457608 | tf_op jit(solution)/shard_map/ppermute | solution.py:96
  412.7 59.1 %collective-permute-start.59 = (bf16[256,1600]{0,1:T(8,128)(2,1)}, bf16[256,1600]{0,1:T(8,128)(2,1)}, u32[]{:S(2)}, u32[]{:S(2)}) collective-permute-start(bf16[256,1600]{0,1:T(8,128)(2,1)} %copy.226), channel_id=1, source_target_pairs={{0,4},{2,6},{4,0},{6,2},{1,5},{3,7},{5,1},{7,3},{8,12},{10,14},{12... | collective-permute-start | bytes 2457608 | tf_op jit(solution)/shard_map/ppermute | solution.py:93
  412.7 59.2 %collective-permute-start.60 = (bf16[256,1600]{0,1:T(8,128)(2,1)}, bf16[256,1600]{0,1:T(8,128)(2,1)}, u32[]{:S(2)}, u32[]{:S(2)}) collective-permute-start(bf16[256,1600]{0,1:T(8,128)(2,1)} %copy.226), channel_id=1, source_target_pairs={{0,5},{1,4},{2,7},{3,6},{4,1},{5,0},{6,3},{7,2},{8,13},{9,12},{10,... | collective-permute-start | bytes 2457608 | tf_op jit(solution)/shard_map/ppermute | solution.py:104
  564.5 362.8 %reduce-scatter.13.cloned.1.call-start = ((), (), s32[]{:S(2)}) async-start(), calls=%async_computation.16 | async-start | bytes 3584000 | tf_op jit(solution)/shard_map/reduce_scatter | solution.py:255
  600.9 331.9 %reduce-scatter.19.cloned.1.call-start = ((), (), s32[]{:S(2)}) async-start(), calls=%async_computation.19 | async-start | bytes 3072000 | tf_op jit(solution)/shard_map/reduce_scatter | solution.py:255
  694.3 251.7 %reduce-scatter.23.cloned.1.call-start = ((), (), s32[]{:S(2)}) async-start(), calls=%async_computation.21 | async-start | bytes 1064960 | tf_op jit(solution)/shard_map/reduce_scatter | solution.py:255
  750.8 292.6 %reduce-scatter.15.cloned.1.call-start = ((), (), s32[]{:S(2)}) async-start(), calls=%async_computation.17 | async-start | bytes 3461120 | tf_op jit(solution)/shard_map/reduce_scatter | solution.py:254
  784.2 261.2 %reduce-scatter.11.cloned.1.call-start = ((), (), s32[]{:S(2)}) async-start(), calls=%async_computation.15 | async-start | bytes 3584000 | tf_op jit(solution)/shard_map/reduce_scatter | solution.py:255
  823.6 235.7 %reduce-scatter.21.cloned.1.call-start = ((), (), s32[]{:S(2)}) async-start(), calls=%async_computation.20 | async-start | bytes 1064960 | tf_op jit(solution)/shard_map/reduce_scatter | solution.py:255
  859.8 55.1 %collective-permute-start.142 = (bf16[128,1664]{1,0:T(8,128)(2,1)S(1)}, bf16[128,1664]{1,0:T(8,128)(2,1)S(1)}, u32[]{:S(2)}, u32[]{:S(2)}) collective-permute-start(bf16[128,1664]{1,0:T(8,128)(2,1)S(1)} %pad.101.refs_0_), channel_id=1, source_target_pairs={{0,1},{1,0},{2,3},{3,2},{4,5},{5,4},{6,7},{7,6},{8,9},{9,8},{10,11... | collective-permute-start | bytes 1277960 | tf_op jit(solution)/shard_map/ppermute | solution.py:96
  861.5 54.0 %collective-permute-start.143 = (bf16[128,1664]{1,0:T(8,128)(2,1)S(1)}, bf16[128,1664]{1,0:T(8,128)(2,1)S(1)}, u32[]{:S(2)}, u32[]{:S(2)}) collective-permute-start(bf16[128,1664]{1,0:T(8,128)(2,1)S(1)} %pad.101.refs_0_), channel_id=1, source_target_pairs={{0,4},{2,6},{4,0},{6,2},{1,5},{3,7},{5,1},{7,3},{8,12},{10,14},{12... | collective-permute-start | bytes 1277960 | tf_op jit(solution)/shard_map/ppermute | solution.py:93
  863.4 59.0 %collective-permute-start.145 = (bf16[128,1664]{1,0:T(8,128)(2,1)S(1)}, bf16[128,1664]{1,0:T(8,128)(2,1)S(1)}, u32[]{:S(2)}, u32[]{:S(2)}) collective-permute-start(bf16[128,1664]{1,0:T(8,128)(2,1)S(1)} %pad.101.refs_0_), channel_id=1, source_target_pairs={{0,2},{2,0},{4,6},{6,4},{1,3},{3,1},{5,7},{7,5},{8,10},{10,8},{12,... | collective-permute-start | bytes 1277960 | tf_op jit(solution)/shard_map/ppermute | solution.py:90
  925.5 159.2 %reduce-scatter.9.cloned.1.call-start = ((), (), s32[]{:S(2)}) async-start(), calls=%async_computation.14 | async-start | bytes 3072000 | tf_op jit(solution)/shard_map/reduce_scatter | solution.py:255
  987.5 62.8 %collective-permute-start.84 = (bf16[128,1600]{1,0:T(8,128)(2,1)}, bf16[128,1600]{1,0:T(8,128)(2,1)}, u32[]{:S(2)}, u32[]{:S(2)}) collective-permute-start(bf16[128,1600]{1,0:T(8,128)(2,1)} %get-tuple-element.336), channel_id=1, source_target_pairs={{0,0},{9,1},{20,4},{29,5},{2,2},{11,3},{22,6},{31,7},{1,8},{8,9},{... | collective-permute-start | bytes 1228808 | tf_op jit(solution)/shard_map/ppermute | solution.py:87
  (335 other events, 4510.8 us)
Sparse Core Ops, SparseCore 0:
  47.3 39.1 all-gather.10
  88.7 68.2 all-gather.8
  159.1 57.2 all-gather.12
  218.4 55.8 all-gather.20
  275.7 50.6 all-gather.14
  327.8 83.0 all-gather.16
  412.5 57.1 all-gather.18
  564.6 53.5 reduce-scatter.16
  620.5 55.9 reduce-scatter.12
  694.4 47.6 reduce-scatter.18
  751.0 23.0 reduce-scatter.22
  784.4 53.8 reduce-scatter.14
  840.6 55.8 reduce-scatter.10
  925.6 22.7 reduce-scatter.20
  986.7 50.4 reduce-scatter.8

commit v6 on v5

--- a/solution.py
+++ b/solution.py
@@ -121,7 +121,7 @@
             v = jnp.concatenate([v, swap(v)])
         return v
 
-    def scatter_parts(self, near, far):
+    def scatter_parts(self, near, far, gate=None):
         if not self.cube:
             blocks = jnp.concatenate([near.astype(BF), far])
             rows = blocks.shape[0] // self.group
@@ -137,6 +137,8 @@
             [near, self.swap_core(far)],
         )
         parts = self.swap_xy(to_xy), self.swap_x(to_x), self.swap_y(to_y)
+        if gate is not None:
+            own = after(own, gate)
         parts = [part[:, :columns].astype(F32) for part in parts]
         return own + parts[0] + parts[1] + parts[2]
 
@@ -319,30 +321,31 @@
 
 
 def project_kernel(count, left, *refs):
-    block = refs[0].shape[0]
-    total = dot(left[:, :block], refs[0][...])
+    block, width = refs[0].shape[0], refs[-1].shape[1]
+    total = dot(left[:, :block], refs[0][:, :width])
     for i in range(1, count):
-        total = total + dot(left[:, i * block : (i + 1) * block], refs[i][...])
+        total = total + dot(left[:, i * block : (i + 1) * block], refs[i][:, :width])
     refs[-1][...] = total
 
 
-def project(plan, left, pieces):
+def project(plan, left, pieces, width):
     if not plan.cube:
-        return dot(left, jnp.concatenate(pieces))
-    shape = sds((left.shape[0], pieces[0].shape[1]), F32)
+        return dot(left, jnp.concatenate(pieces)[:, :width])
+    shape = sds((left.shape[0], width), F32)
     kernel = functools.partial(project_kernel, len(pieces))
     return call(kernel, [shape], [], 2 * left.size * shape.shape[1], [left, *pieces])[0]
 
 
 def project_back_kernel(count, left, *refs):
-    block = refs[0].shape[0]
+    block, width = refs[0].shape[0], left.shape[1]
     for i in range(count):
-        refs[-1][:, i * block : (i + 1) * block] = dot(left[...], refs[i][...], 1, 1).astype(BF)
+        part = dot(left[...], refs[i][:, :width], 1, 1)
+        refs[-1][:, i * block : (i + 1) * block] = part.astype(BF)
 
 
 def project_back(plan, left, pieces):
     if not plan.cube:
-        return dot(left, jnp.concatenate(pieces), 1, 1).astype(BF)
+        return dot(left, jnp.concatenate(pieces)[:, : left.shape[1]], 1, 1).astype(BF)
     shape = sds((left.shape[0], len(pieces) * pieces[0].shape[0]), BF)
     kernel = functools.partial(project_back_kernel, len(pieces))
     return call(kernel, [shape], [], 2 * left.size * shape.shape[1], [left, *pieces])[0]
@@ -1042,7 +1045,7 @@
             grad_pieces = plan.gather_pieces(widen(after(grad.astype(BF), pieces)))
         normed, packed, lse, mixed = attend(plan, pieces, qkv_w, bias_qkv, codes, total, scale)
         out_w = out_block(layer)
-        out_w = plan.gather_pieces(after(out_w, pieces) if layer else out_w)
+        out_w = plan.gather_pieces(widen(after(out_w, pieces) if layer else out_w))
         weights[layer] = qkv_w, out_w, up_w, down_w
         mixed = jnp.concatenate(plan.exchange(mixed), axis=1)
         mixed = dot(mixed, select).astype(BF)
@@ -1050,7 +1053,7 @@
         mixed_own = plan.exchange(
             jnp.concatenate([mixed[:, i * block : (i + 1) * block] for i in range(group)])
         )
-        middle = hidden + (project(plan, mixed, out_w) + bias_out)
+        middle = hidden + (project(plan, mixed, out_w, width) + bias_out)
         unit2, inv2 = norm_parts(middle)
         pieces = plan.gather_pieces(widen((unit2 * gain2 + shift2).astype(BF)))
         if layer == layers - 1:
@@ -1186,7 +1189,7 @@
         g_mixed = plan.exchange(g_mixed)
         if late is None:
             parts = lower_units(plan, after(activated, g_lift), down_w)
-            hidden = middle + (plan.scatter_parts(*parts) + bias_down)
+            hidden = middle + (plan.scatter_parts(*parts, g_mixed) + bias_down)
         att_pieces = plan.gather_pieces(widen(g_att))
         g_packed, g_b, near, far = attend_back(
             plan, g_mixed, packed, lse, codes, qkv_w, total, scale

time: 1140 us -> 1130 us (level)
  local copies, waits for them, and re-layouts: 196 us -> 150 us
  waiting for transfers between devices: 375 us -> 413 us
    ppermute x33, waiting for transfers between devices: 93.9 us -> 127 us  [swap_y(): return lax.ppermute(v, FSDP, [(f, f ^ 2) for f in range(self.nf)])]
    ppermute x14 -> x0, local copies, waits for them, and re-layouts: 29.4 us -> none  [the longest x8 17.6 us: swap_core(): return lax.ppermute(v, FSDP, [(f, f ^ 1) for f in range(self.nf)])]
    unnamed x394 -> x430, local copies, waits for them, and re-layouts: 121 us -> 101 us
    ppermute x27, waiting for transfers between devices: 89.9 us -> 74.6 us  [swap_xy(): return lax.ppermute(v, GROUP, pairs)]
    all_gather x1, waiting for transfers between devices: 11.1 us -> 25.3 us  [gather_seq(): return lax.all_gather(v[None], SEQ, axis=1, tiled=True)[0]]
  transfers between devices with their start and end apart: 181 -> 181, of which waited for: 63 -> 68; matrix products, arithmetic and copies ran while one was open for 13% -> 11% of each run, Pallas kernels for 19% -> 18%
where the time goes in v6:
time: 1130 us; the launch traced here: 1110 us
  waiting for transfers between devices  413 us (37%)
  starting transfers between devices  260 us (23%)
  Pallas kernels  216 us (19%)
  local copies, waits for them, and re-layouts  150 us (13%)
  other arithmetic  43.7 us (4%)
  between operations  17.5 us (2%)
  matrix products  13.9 us (1%)
    pallas_call x31, Pallas kernels, call(): pl.pallas_call(kernel, out_shape=tuple(outs), scratch_shapes=scratch, com...  196 us
    ppermute x32, waiting for transfers between devices, swap_x(): return lax.ppermute(v, REPLICA, [(r, r ^ 1) for r in range(self.nr)])  164 us
    ppermute x33, waiting for transfers between devices, swap_y(): return lax.ppermute(v, FSDP, [(f, f ^ 2) for f in range(self.nf)])  127 us
    ppermute x32, starting transfers between devices, swap_x(): return lax.ppermute(v, REPLICA, [(r, r ^ 1) for r in range(self.nr)])  116 us
    unnamed x430, local copies, waits for them, and re-layouts  101 us
    ppermute x27, waiting for transfers between devices, swap_xy(): return lax.ppermute(v, GROUP, pairs)  74.6 us
    ppermute x33, starting transfers between devices, swap_y(): return lax.ppermute(v, FSDP, [(f, f ^ 2) for f in range(self.nf)])  54.5 us
    ppermute x27, starting transfers between devices, swap_xy(): return lax.ppermute(v, GROUP, pairs)  43.4 us
  transfers between devices with their start and end apart: 181, of which 68 were waited for; matrix products, arithmetic and copies ran while one was open for 11% of the time, Pallas kernels for 18%

profile of v6, /device:TPU:0, one launch (start us, length us, event | category | flops | bytes accessed | tf_op | source)
XLA Modules:
  0.0 1114.0 jit_solution(11046711708514447782)
XLA Ops:
  88.6 51.0 %collective-permute-start.12 = (bf16[128,1664]{1,0:T(8,128)(2,1)S(1)}, bf16[128,1664]{1,0:T(8,128)(2,1)S(1)}, u32[]{:S(2)}, u32[]{:S(2)}) collective-permute-start(bf16[128,1664]{1,0:T(8,128)(2,1)S(1)} %pad.89.refs_0_), channel_id=1, source_target_pairs={{0,1},{1,0},{2,3},{3,2},{4,5},{5,4},{6,7},{7,6},{8,9},{9,8},{10,11... | collective-permute-start | bytes 1277960 | tf_op jit(solution)/shard_map/ppermute | solution.py:96
  170.0 18.0 %shard_map.282 = (bf16[1024,1600]{1,0:T(8,128)(2,1)}, bf16[1024,768]{1,0:T(8,128)(2,1)S(1)}, f32[8,1024]{1,0:T(8,128)S(1)}, bf16[1024,256]{1,0:T(8,128)(2,1)S(1)}) custom-call(bf16[128,1664]{1,0:T(8,128)(2,1)S(1)} %pad.89.refs_0_, bf16[128,1664]{1,0:T(8,128)(2,1)S(1)} %copy-done.82, bf16[128,1664]{1,0:T(8,128)(2,1)} %collective-permute-done.13.refs_2_, ...), custom_call_target="tpu_custom_call" | custom-call | flops 3590324224 | bytes 11283456 | tf_op jit(solution)/shard_map/pallas_call | solution.py:263
  230.4 9.2 collective-permute-done.36.refs_1_
  249.1 25.3 %all-gather.21.cloned.1.call-done.refs_10_.refs_9_ = bf16[832,1600]{1,0:T(8,128)(2,1)} async-done(((bf16[208,1600]{1,0:T(8,128)(2,1)}), bf16[832,1600]{1,0:T(8,128)(2,1)}) %all-gather.21.cloned.1.call-update) | async-done | bytes 2662416 | tf_op jit(solution)/shard_map/all_gather | solution.py:250
  274.3 15.1 %shard_map.284 = (bf16[1024,1600]{1,0:T(8,128)(2,1)}, bf16[1024,832]{1,0:T(8,128)(2,1)S(1)}, bf16[1024,832]{1,0:T(8,128)(2,1)S(1)}, f32[512,1600]{1,0:T(8,128)}, bf16[512,1664]{1,0:T(8,128)(2,1)}) custom-call(bf16[128,1664]{1,0:T(8,128)(2,1)S(1)} %pad.97.refs_0_, bf16[128,1664]{1,0:T(8,128)(2,1)S(1)} %collective-permute-done.36.refs_1_, ...), custom_call_target="tpu_custom_call" | custom-call | flops 5452595200 | bytes 20401408 | tf_op jit(solution)/shard_map/pallas_call | solution.py:263
  328.7 9.3 collective-permute-done.47.refs_1_
  338.0 9.3 collective-permute-done.48.refs_2_
  357.5 18.3 %shard_map.286 = (bf16[1024,1600]{1,0:T(8,128)(2,1)}, bf16[1024,768]{1,0:T(8,128)(2,1)S(1)}, f32[8,1024]{1,0:T(8,128)S(1)}, bf16[1024,256]{1,0:T(8,128)(2,1)S(1)}) custom-call(bf16[128,1664]{1,0:T(8,128)(2,1)S(1)} %copy-done.61, bf16[128,1664]{1,0:T(8,128)(2,1)} %collective-permute-done.47.refs_1_, bf16[128,1664]{1,0:T(8,128)(2,1)} %collective-permute-done.48.refs_2_, ...), custom_call_target="tpu_custom_call" | custom-call | flops 3590324224 | bytes 11283456 | tf_op jit(solution)/shard_map/pallas_call | solution.py:263
  380.0 30.1 %collective-permute-start.73 = (bf16[128,1664]{1,0:T(8,128)(2,1)}, bf16[128,1664]{1,0:T(8,128)(2,1)}, u32[]{:S(2)}, u32[]{:S(2)}) collective-permute-start(bf16[128,1664]{1,0:T(8,128)(2,1)} %pad.107.refs_0_), channel_id=1, source_target_pairs={{0,1},{1,0},{2,3},{3,2},{4,5},{5,4},{6,7},{7,6},{8,9},{9,8},{10,11... | collective-permute-start | bytes 1277960 | tf_op jit(solution)/shard_map/ppermute | solution.py:96
  417.0 42.7 %collective-permute-done.55 = bf16[256,256]{1,0:T(8,128)(2,1)S(1)} collective-permute-done((bf16[256,256]{1,0:T(8,128)(2,1)S(1)}, bf16[256,256]{1,0:T(8,128)(2,1)S(1)}, u32[]{:S(2)}, u32[]{:S(2)}) %collective-permute-start.55) | collective-permute-done | bytes 131104 | tf_op jit(solution)/shard_map/ppermute | solution.py:96
  492.8 22.4 %collective-permute-done.66.refs_2_ = bf16[128,1664]{1,0:T(8,128)(2,1)S(1)} collective-permute-done((bf16[128,1664]{1,0:T(8,128)(2,1)S(1)}, bf16[128,1664]{1,0:T(8,128)(2,1)S(1)}, u32[]{:S(2)}, u32[]{:S(2)}) %collective-permute-start.66) | collective-permute-done | bytes 426016 | tf_op jit(solution)/shard_map/ppermute | solution.py:93
  547.8 15.4 %shard_map.290 = (bf16[1024,832]{1,0:T(8,128)(2,1)S(1)}, f32[1,832]{1,0:T(1,128)S(1)}, f32[512,1600]{1,0:T(8,128)}, bf16[512,1664]{1,0:T(8,128)(2,1)}) custom-call(bf16[128,1664]{1,0:T(8,128)(2,1)} %pad.107.refs_0_, bf16[128,1664]{1,0:T(8,128)(2,1)} %collective-permute-done.73.refs_1_, bf16[128,1664]{1,0:T(8,128)(2,1)} %collective-permute-done.74.refs_2_, ...), custom_call_target="tpu_custom_call" | custom-call | flops 5452595200 | bytes 17124608 | tf_op jit(solution)/shard_map/pallas_call | solution.py:263
  577.2 10.1 collective-permute-done.82
  617.8 19.8 %shard_map.295 = (bf16[1024,768]{1,0:T(8,128)(2,1)S(1)}, f32[1,768]{1,0:T(1,128)S(1)}, f32[512,1600]{1,0:T(8,128)}, bf16[512,1664]{1,0:T(8,128)(2,1)S(1)}) custom-call(bf16[128,256]{1,0:T(8,128)(2,1)S(1)} %get-tuple-element.372.refs_0_, bf16[128,256]{1,0:T(8,128)(2,1)S(1)} %get-tuple-element.416.refs_1_, bf16[128,256]{1,0:T(8,128)(2,1)S(1)} %get-tuple-element.414.refs_2_, ...), custom_call_target="tpu_custom_call" | custom-call | flops 5200936960 | bytes 11152384 | tf_op jit(solution)/shard_map/pallas_call | solution.py:263
  671.5 17.9 %collective-permute-done.155.refs_2_ = bf16[128,1664]{1,0:T(8,128)(2,1)S(1)} collective-permute-done((bf16[128,1664]{1,0:T(8,128)(2,1)S(1)}, bf16[128,1664]{1,0:T(8,128)(2,1)S(1)}, u32[]{:S(2)}, u32[]{:S(2)}) %collective-permute-start.155) | collective-permute-done | bytes 426016 | tf_op jit(solution)/shard_map/ppermute | solution.py:93
  709.8 9.2 collective-permute-done.97.refs_1_
  719.0 8.8 collective-permute-done.98.refs_2_
  743.0 14.6 %shard_map.297 = (bf16[1024,832]{1,0:T(8,128)(2,1)S(1)}, f32[1,832]{1,0:T(1,128)S(1)}, f32[512,1600]{1,0:T(8,128)}, bf16[512,1664]{1,0:T(8,128)(2,1)}) custom-call(bf16[128,1664]{1,0:T(8,128)(2,1)S(1)} %pad.108.refs_0_, bf16[128,1664]{1,0:T(8,128)(2,1)S(1)} %collective-permute-done.97.refs_1_, bf16[128,1664]{1,0:T(8,128)(2,1)S(1)} %collective-permute-done.98.refs_2_, ...), custom_call_target="tpu_custom_call" | custom-call | flops 5452595200 | bytes 17124608 | tf_op jit(solution)/shard_map/pallas_call | solution.py:263
  784.0 8.4 collective-permute-done.105
  821.0 19.7 %collective-permute-done.111 = bf16[256,256]{1,0:T(8,128)(2,1)S(1)} collective-permute-done((bf16[256,256]{1,0:T(8,128)(2,1)S(1)}, bf16[256,256]{1,0:T(8,128)(2,1)S(1)}, u32[]{:S(2)}, u32[]{:S(2)}) %collective-permute-start.111) | collective-permute-done | bytes 131104 | tf_op jit(solution)/shard_map/ppermute | solution.py:104
  850.7 20.3 %shard_map.300 = (bf16[1024,768]{1,0:T(8,128)(2,1)S(1)}, f32[1,768]{1,0:T(1,128)S(1)}, f32[512,1600]{1,0:T(8,128)}, bf16[512,1664]{1,0:T(8,128)(2,1)}) custom-call(bf16[128,256]{1,0:T(8,128)(2,1)S(1)} %get-tuple-element.364.refs_0_, bf16[128,256]{1,0:T(8,128)(2,1)S(1)} %get-tuple-element.410.refs_1_, bf16[128,256]{1,0:T(8,128)(2,1)S(1)} %get-tuple-element.408.refs_2_, ...), custom_call_target="tpu_custom_call" | custom-call | flops 5200936960 | bytes 11152384 | tf_op jit(solution)/shard_map/pallas_call | solution.py:263
  915.7 12.9 %collective-permute-done.89 = bf16[128,1664]{1,0:T(8,128)(2,1)} collective-permute-done((bf16[128,1664]{1,0:T(8,128)(2,1)}, bf16[128,1664]{1,0:T(8,128)(2,1)}, u32[]{:S(2)}, u32[]{:S(2)}) %collective-permute-start.89) | collective-permute-done | bytes 426016 | tf_op jit(solution)/shard_map/ppermute | solution.py:104
  947.5 9.5 collective-permute-done.129.refs_1_
  1016.6 21.2 %collective-permute-start.122 = (f32[2,2,1280]{2,1,0:T(2,128)S(1)}, f32[2,2,1280]{2,1,0:T(2,128)S(1)}, u32[]{:S(2)}, u32[]{:S(2)}) collective-permute-start(f32[2,2,1280]{2,1,0:T(2,128)S(1)} %pad_maximum_fusion.35), channel_id=1, source_target_pairs={{0,4},{2,6},{4,0},{6,2},{1,5},{3,7},{5,1},{7,3},{8,12},{10,14},{12... | collective-permute-start | bytes 61448 | tf_op jit(solution)/shard_map/ppermute | solution.py:93
  (1108 shorter events, 658.1 us)
Async XLA Ops:
  7.2 151.0 %all-gather.11.cloned.1.call-start = ((), (), s32[]{:S(2)}) async-start(), calls=%async_computation.9 | async-start | bytes 2129920 | tf_op jit(solution)/shard_map/all_gather | solution.py:251
  47.2 118.9 %all-gather.9.cloned.1.call-start = ((), (), s32[]{:S(2)}) async-start(), calls=%async_computation.8 | async-start | bytes 3072000 | tf_op jit(solution)/shard_map/all_gather | solution.py:251
  52.0 197.0 %all-gather.13.cloned.1.call-start = ((), (), s32[]{:S(2)}) async-start(), calls=%async_computation.10 | async-start | bytes 3584000 | tf_op jit(solution)/shard_map/all_gather | solution.py:251
  83.6 190.7 %all-gather.21.cloned.1.call-start = ((), (), s32[]{:S(2)}) async-start(), calls=%async_computation.22 | async-start | bytes 3461120 | tf_op jit(solution)/shard_map/all_gather | solution.py:250
  85.4 269.4 %all-gather.15.cloned.1.call-start = ((), (), s32[]{:S(2)}) async-start(), calls=%async_computation.11 | async-start | bytes 3072000 | tf_op jit(solution)/shard_map/all_gather | solution.py:251
  88.6 61.7 %collective-permute-start.12 = (bf16[128,1664]{1,0:T(8,128)(2,1)S(1)}, bf16[128,1664]{1,0:T(8,128)(2,1)S(1)}, u32[]{:S(2)}, u32[]{:S(2)}) collective-permute-start(bf16[128,1664]{1,0:T(8,128)(2,1)S(1)} %pad.89.refs_0_), channel_id=1, source_target_pairs={{0,1},{1,0},{2,3},{3,2},{4,5},{5,4},{6,7},{7,6},{8,9},{9,8},{10,11... | collective-permute-start | bytes 1277960 | tf_op jit(solution)/shard_map/ppermute | solution.py:96
  195.2 326.0 %all-gather.17.cloned.1.call-start = ((), (), s32[]{:S(2)}) async-start(), calls=%async_computation.12 | async-start | bytes 3584000 | tf_op jit(solution)/shard_map/all_gather | solution.py:251
  292.0 254.3 %all-gather.19.cloned.1.call-start = ((), (), s32[]{:S(2)}) async-start(), calls=%async_computation.13 | async-start | bytes 3461120 | tf_op jit(solution)/shard_map/all_gather | solution.py:251
  378.1 510.9 %reduce-scatter.13.cloned.1.call-start = ((), (), s32[]{:S(2)}) async-start(), calls=%async_computation.16 | async-start | bytes 3584000 | tf_op jit(solution)/shard_map/reduce_scatter | solution.py:257
  380.0 102.9 %collective-permute-start.73 = (bf16[128,1664]{1,0:T(8,128)(2,1)}, bf16[128,1664]{1,0:T(8,128)(2,1)}, u32[]{:S(2)}, u32[]{:S(2)}) collective-permute-start(bf16[128,1664]{1,0:T(8,128)(2,1)} %pad.107.refs_0_), channel_id=1, source_target_pairs={{0,1},{1,0},{2,3},{3,2},{4,5},{5,4},{6,7},{7,6},{8,9},{9,8},{10,11... | collective-permute-start | bytes 1277960 | tf_op jit(solution)/shard_map/ppermute | solution.py:96
  411.4 60.0 %collective-permute-start.58 = (bf16[256,1664]{1,0:T(8,128)(2,1)S(1)}, bf16[256,1664]{1,0:T(8,128)(2,1)S(1)}, u32[]{:S(2)}, u32[]{:S(2)}) collective-permute-start(bf16[256,1664]{1,0:T(8,128)(2,1)S(1)} %pad.104.refs_0_), channel_id=1, source_target_pairs={{0,1},{1,0},{2,3},{3,2},{4,5},{5,4},{6,7},{7,6},{8,9},{9,8},{10,11... | collective-permute-start | bytes 2555912 | tf_op jit(solution)/shard_map/ppermute | solution.py:96
  411.5 60.5 %collective-permute-start.59 = (bf16[256,1664]{1,0:T(8,128)(2,1)S(1)}, bf16[256,1664]{1,0:T(8,128)(2,1)S(1)}, u32[]{:S(2)}, u32[]{:S(2)}) collective-permute-start(bf16[256,1664]{1,0:T(8,128)(2,1)S(1)} %pad.104.refs_0_), channel_id=1, source_target_pairs={{0,4},{2,6},{4,0},{6,2},{1,5},{3,7},{5,1},{7,3},{8,12},{10,14},{12... | collective-permute-start | bytes 2555912 | tf_op jit(solution)/shard_map/ppermute | solution.py:93
  411.5 60.5 %collective-permute-start.60 = (bf16[256,1664]{1,0:T(8,128)(2,1)S(1)}, bf16[256,1664]{1,0:T(8,128)(2,1)S(1)}, u32[]{:S(2)}, u32[]{:S(2)}) collective-permute-start(bf16[256,1664]{1,0:T(8,128)(2,1)S(1)} %pad.104.refs_0_), channel_id=1, source_target_pairs={{0,5},{1,4},{2,7},{3,6},{4,1},{5,0},{6,3},{7,2},{8,13},{9,12},{10,... | collective-permute-start | bytes 2555912 | tf_op jit(solution)/shard_map/ppermute | solution.py:104
  569.8 325.0 %reduce-scatter.19.cloned.1.call-start = ((), (), s32[]{:S(2)}) async-start(), calls=%async_computation.19 | async-start | bytes 3072000 | tf_op jit(solution)/shard_map/reduce_scatter | solution.py:257
  644.5 255.6 %reduce-scatter.17.cloned.1.call-start = ((), (), s32[]{:S(2)}) async-start(), calls=%async_computation.18 | async-start | bytes 3461120 | tf_op jit(solution)/shard_map/reduce_scatter | solution.py:256
  645.1 294.1 %reduce-scatter.23.cloned.1.call-start = ((), (), s32[]{:S(2)}) async-start(), calls=%async_computation.21 | async-start | bytes 1064960 | tf_op jit(solution)/shard_map/reduce_scatter | solution.py:257
  702.1 335.8 %reduce-scatter.15.cloned.1.call-start = ((), (), s32[]{:S(2)}) async-start(), calls=%async_computation.17 | async-start | bytes 3461120 | tf_op jit(solution)/shard_map/reduce_scatter | solution.py:256
  736.4 303.5 %reduce-scatter.11.cloned.1.call-start = ((), (), s32[]{:S(2)}) async-start(), calls=%async_computation.15 | async-start | bytes 3584000 | tf_op jit(solution)/shard_map/reduce_scatter | solution.py:257
  774.9 278.8 %reduce-scatter.21.cloned.1.call-start = ((), (), s32[]{:S(2)}) async-start(), calls=%async_computation.20 | async-start | bytes 1064960 | tf_op jit(solution)/shard_map/reduce_scatter | solution.py:257
  816.3 84.3 %collective-permute-start.80 = (bf16[512,1664]{1,0:T(8,128)(2,1)}, bf16[512,1664]{1,0:T(8,128)(2,1)}, u32[]{:S(2)}, u32[]{:S(2)}) collective-permute-start(bf16[512,1664]{1,0:T(8,128)(2,1)} %get-tuple-element.157), channel_id=1, source_target_pairs={{0,2},{2,0},{4,6},{6,4},{1,3},{3,1},{5,7},{7,5},{8,10},{10,8},{12,... | collective-permute-start | bytes 5111816 | tf_op jit(solution)/shard_map/ppermute | solution.py:90
  817.3 56.4 %collective-permute-start.143 = (bf16[128,1664]{1,0:T(8,128)(2,1)S(1)}, bf16[128,1664]{1,0:T(8,128)(2,1)}, u32[]{:S(2)}, u32[]{:S(2)}) collective-permute-start(bf16[128,1664]{1,0:T(8,128)(2,1)S(1)} %pad.110.refs_0_), channel_id=1, source_target_pairs={{0,4},{2,6},{4,0},{6,2},{1,5},{3,7},{5,1},{7,3},{8,12},{10,14},{12... | collective-permute-start | bytes 1277960 | tf_op jit(solution)/shard_map/ppermute | solution.py:93
  871.1 68.9 %collective-permute-start.112 = (bf16[512,1664]{1,0:T(8,128)(2,1)}, bf16[512,1664]{1,0:T(8,128)(2,1)}, u32[]{:S(2)}, u32[]{:S(2)}) collective-permute-start(bf16[512,1664]{1,0:T(8,128)(2,1)} %get-tuple-element.187), channel_id=1, source_target_pairs={{0,2},{2,0},{4,6},{6,4},{1,3},{3,1},{5,7},{7,5},{8,10},{10,8},{12,... | collective-permute-start | bytes 5111816 | tf_op jit(solution)/shard_map/ppermute | solution.py:90
  889.0 190.1 %reduce-scatter.9.cloned.1.call-start = ((), (), s32[]{:S(2)}) async-start(), calls=%async_computation.14 | async-start | bytes 3072000 | tf_op jit(solution)/shard_map/reduce_scatter | solution.py:257
  982.3 62.3 %collective-permute-start.92 = (bf16[128,1600]{1,0:T(8,128)(2,1)}, bf16[128,1600]{1,0:T(8,128)(2,1)}, u32[]{:S(2)}, u32[]{:S(2)}) collective-permute-start(bf16[128,1600]{1,0:T(8,128)(2,1)} %add_convert_fusion), channel_id=1, source_target_pairs={{0,0},{9,1},{20,4},{29,5},{2,2},{11,3},{22,6},{31,7},{1,8},{8,9},{... | collective-permute-start | bytes 1228808 | tf_op jit(solution)/shard_map/ppermute | solution.py:87
  (353 other events, 5030.5 us)
Sparse Core Ops, SparseCore 0:
  47.3 39.1 all-gather.10
  88.6 68.3 all-gather.8
  159.1 57.2 all-gather.12
  218.5 55.8 all-gather.20
  275.7 50.6 all-gather.14
  328.4 83.0 all-gather.16
  413.0 57.1 all-gather.18
  569.9 55.0 reduce-scatter.12
  644.6 48.5 reduce-scatter.18
  695.3 54.1 reduce-scatter.16
  751.8 23.8 reduce-scatter.22
  777.9 53.9 reduce-scatter.14
  834.1 55.8 reduce-scatter.10
  892.2 23.9 reduce-scatter.20
  981.6 50.7 reduce-scatter.8

commit v7 on v6

--- a/solution.py
+++ b/solution.py
@@ -1164,8 +1164,6 @@
         if late is not None:
             above = layer + 1
             out = scatter_seq(down_grad(plan, *late[2], width))
-            if above == layers - 1:
-                output = plan.regroup(hidden.astype(BF), back=True)
             into_up = late_up(late[0], above)
             into_down = late_down(late[1], above)
             into_out = late_out(out, above)
@@ -1187,9 +1185,11 @@
             [g_mixed[:, i * span : (i + 1) * span] for i in range(group)]
         )
         g_mixed = plan.exchange(g_mixed)
-        if late is None:
-            parts = lower_units(plan, after(activated, g_lift), down_w)
+        if layer == 0:
+            high = layers - 1
+            parts = lower_units(plan, after(kept[high][-1], g_lift), weights[high][3])
             hidden = middle + (plan.scatter_parts(*parts, g_mixed) + bias_down)
+            output = plan.regroup(hidden.astype(BF), back=True)
         att_pieces = plan.gather_pieces(widen(g_att))
         g_packed, g_b, near, far = attend_back(
             plan, g_mixed, packed, lse, codes, qkv_w, total, scale
@@ -1217,7 +1217,7 @@
             grad_pieces = plan.gather_pieces(widen(grad.astype(BF)))
     out = scatter_seq(down_grad(plan, *late[2], width))
     grad_tokens = plan.regroup(grad.astype(BF), back=True).astype(F32)
-    into_qkv = late_qkv(after(late[3], (into_up, into_down)), 0)
+    into_qkv = late_qkv(late[3], 0)
     output = after(output, grad).astype(F32)
     into_out = late_out(out, 0)
 

time: 1130 us -> 1150 us (1.018)
    reduce_scatter x2, waiting for transfers between devices: 0.01 us -> 36.3 us  [scatter_seq(): return lax.psum_scatter(v[None], SEQ, scatter_dimension=1, tiled=True)[0]]
    ppermute x32, waiting for transfers between devices: 164 us -> 137 us  [swap_x(): return lax.ppermute(v, REPLICA, [(r, r ^ 1) for r in range(self.nr)])]
    unnamed x430 -> x374, local copies, waits for them, and re-layouts: 101 us -> 99.8 us
  transfers between devices with their start and end apart: 181 -> 181, of which waited for: 68 -> 63; matrix products, arithmetic and copies ran while one was open for 11% -> 11% of each run, Pallas kernels for 18% -> 19%
where the time goes in v7:
time: 1150 us; the launch traced here: 1140 us
  waiting for transfers between devices  424 us (37%)
  starting transfers between devices  267 us (23%)
  Pallas kernels  222 us (19%)
  local copies, waits for them, and re-layouts  156 us (14%)
  other arithmetic  41.6 us (4%)
  between operations  17 us (1%)
  matrix products  14 us (1%)
    pallas_call x31, Pallas kernels, call(): pl.pallas_call(kernel, out_shape=tuple(outs), scratch_shapes=scratch, com...  201 us
    ppermute x33, waiting for transfers between devices, swap_y(): return lax.ppermute(v, FSDP, [(f, f ^ 2) for f in range(self.nf)])  138 us
    ppermute x32, waiting for transfers between devices, swap_x(): return lax.ppermute(v, REPLICA, [(r, r ^ 1) for r in range(self.nr)])  137 us
    ppermute x32, starting transfers between devices, swap_x(): return lax.ppermute(v, REPLICA, [(r, r ^ 1) for r in range(self.nr)])  123 us
    unnamed x374, local copies, waits for them, and re-layouts  99.8 us
    ppermute x27, waiting for transfers between devices, swap_xy(): return lax.ppermute(v, GROUP, pairs)  71.5 us
    ppermute x27, starting transfers between devices, swap_xy(): return lax.ppermute(v, GROUP, pairs)  49.9 us
    ppermute x33, starting transfers between devices, swap_y(): return lax.ppermute(v, FSDP, [(f, f ^ 2) for f in range(self.nf)])  48.5 us
  transfers between devices with their start and end apart: 181, of which 63 were waited for; matrix products, arithmetic and copies ran while one was open for 11% of the time, Pallas kernels for 19%

profile of v7, /device:TPU:0, one launch (start us, length us, event | category | flops | bytes accessed | tf_op | source)
XLA Modules:
  0.0 1141.6 jit_solution(14430978699628657913)
XLA Ops:
  88.6 51.0 %collective-permute-start.12 = (bf16[128,1664]{1,0:T(8,128)(2,1)S(1)}, bf16[128,1664]{1,0:T(8,128)(2,1)S(1)}, u32[]{:S(2)}, u32[]{:S(2)}) collective-permute-start(bf16[128,1664]{1,0:T(8,128)(2,1)S(1)} %pad.89.refs_0_), channel_id=1, source_target_pairs={{0,1},{1,0},{2,3},{3,2},{4,5},{5,4},{6,7},{7,6},{8,9},{9,8},{10,11... | collective-permute-start | bytes 1277960 | tf_op jit(solution)/shard_map/ppermute | solution.py:96
  169.6 18.0 %shard_map.282 = (bf16[1024,1600]{1,0:T(8,128)(2,1)}, bf16[1024,768]{1,0:T(8,128)(2,1)S(1)}, f32[8,1024]{1,0:T(8,128)S(1)}, bf16[1024,256]{1,0:T(8,128)(2,1)S(1)}) custom-call(bf16[128,1664]{1,0:T(8,128)(2,1)S(1)} %pad.89.refs_0_, bf16[128,1664]{1,0:T(8,128)(2,1)S(1)} %copy-done.74, bf16[128,1664]{1,0:T(8,128)(2,1)} %collective-permute-done.13.refs_2_, ...), custom_call_target="tpu_custom_call" | custom-call | flops 3590324224 | bytes 11283456 | tf_op jit(solution)/shard_map/pallas_call | solution.py:263
  230.9 9.2 collective-permute-done.36.refs_1_
  248.9 25.5 %all-gather.21.cloned.1.call-done.refs_10_.refs_9_ = bf16[832,1600]{1,0:T(8,128)(2,1)} async-done(((bf16[208,1600]{1,0:T(8,128)(2,1)}), bf16[832,1600]{1,0:T(8,128)(2,1)}) %all-gather.21.cloned.1.call-update) | async-done | bytes 2662416 | tf_op jit(solution)/shard_map/all_gather | solution.py:250
  274.4 15.2 %shard_map.284 = (bf16[1024,1600]{1,0:T(8,128)(2,1)}, bf16[1024,832]{1,0:T(8,128)(2,1)S(1)}, bf16[1024,832]{1,0:T(8,128)(2,1)S(1)}, f32[512,1600]{1,0:T(8,128)}, bf16[512,1664]{1,0:T(8,128)(2,1)}) custom-call(bf16[128,1664]{1,0:T(8,128)(2,1)S(1)} %pad.97.refs_0_, bf16[128,1664]{1,0:T(8,128)(2,1)S(1)} %collective-permute-done.36.refs_1_, ...), custom_call_target="tpu_custom_call" | custom-call | flops 5452595200 | bytes 20401408 | tf_op jit(solution)/shard_map/pallas_call | solution.py:263
  329.7 9.3 collective-permute-done.47.refs_1_
  339.0 9.3 collective-permute-done.48.refs_2_
  358.6 18.2 %shard_map.286 = (bf16[1024,1600]{1,0:T(8,128)(2,1)}, bf16[1024,768]{1,0:T(8,128)(2,1)S(1)}, f32[8,1024]{1,0:T(8,128)S(1)}, bf16[1024,256]{1,0:T(8,128)(2,1)S(1)}) custom-call(bf16[128,1664]{1,0:T(8,128)(2,1)S(1)} %copy-done.57, bf16[128,1664]{1,0:T(8,128)(2,1)} %collective-permute-done.47.refs_1_, bf16[128,1664]{1,0:T(8,128)(2,1)} %collective-permute-done.48.refs_2_, ...), custom_call_target="tpu_custom_call" | custom-call | flops 3590324224 | bytes 11283456 | tf_op jit(solution)/shard_map/pallas_call | solution.py:263
  381.0 30.1 %collective-permute-start.73 = (bf16[128,1664]{1,0:T(8,128)(2,1)}, bf16[128,1664]{1,0:T(8,128)(2,1)}, u32[]{:S(2)}, u32[]{:S(2)}) collective-permute-start(bf16[128,1664]{1,0:T(8,128)(2,1)} %pad.107.refs_0_), channel_id=1, source_target_pairs={{0,1},{1,0},{2,3},{3,2},{4,5},{5,4},{6,7},{7,6},{8,9},{9,8},{10,11... | collective-permute-start | bytes 1277960 | tf_op jit(solution)/shard_map/ppermute | solution.py:96
  417.1 43.3 %collective-permute-done.55 = bf16[256,256]{1,0:T(8,128)(2,1)S(1)} collective-permute-done((bf16[256,256]{1,0:T(8,128)(2,1)S(1)}, bf16[256,256]{1,0:T(8,128)(2,1)S(1)}, u32[]{:S(2)}, u32[]{:S(2)}) %collective-permute-start.55) | collective-permute-done | bytes 131104 | tf_op jit(solution)/shard_map/ppermute | solution.py:96
  492.7 22.3 %collective-permute-done.66.refs_2_ = bf16[128,1664]{1,0:T(8,128)(2,1)S(1)} collective-permute-done((bf16[128,1664]{1,0:T(8,128)(2,1)S(1)}, bf16[128,1664]{1,0:T(8,128)(2,1)S(1)}, u32[]{:S(2)}, u32[]{:S(2)}) %collective-permute-start.66) | collective-permute-done | bytes 426016 | tf_op jit(solution)/shard_map/ppermute | solution.py:93
  546.0 15.4 %shard_map.290 = (bf16[1024,832]{1,0:T(8,128)(2,1)S(1)}, f32[1,832]{1,0:T(1,128)S(1)}, f32[512,1600]{1,0:T(8,128)}, bf16[512,1664]{1,0:T(8,128)(2,1)S(1)}) custom-call(bf16[128,1664]{1,0:T(8,128)(2,1)} %pad.107.refs_0_, bf16[128,1664]{1,0:T(8,128)(2,1)} %collective-permute-done.73.refs_1_, bf16[128,1664]{1,0:T(8,128)(2,1)} %collective-permute-done.74.refs_2_, ...), custom_call_target="tpu_custom_call" | custom-call | flops 5452595200 | bytes 17124608 | tf_op jit(solution)/shard_map/pallas_call | solution.py:263
  570.9 10.1 collective-permute-done.81
  621.2 19.7 %shard_map.293 = (bf16[1024,768]{1,0:T(8,128)(2,1)S(1)}, f32[1,768]{1,0:T(1,128)S(1)}, f32[512,1600]{1,0:T(8,128)}, bf16[512,1664]{1,0:T(8,128)(2,1)S(1)}) custom-call(bf16[128,256]{1,0:T(8,128)(2,1)S(1)} %get-tuple-element.370.refs_0_, bf16[128,256]{1,0:T(8,128)(2,1)S(1)} %get-tuple-element.414.refs_1_, bf16[128,256]{1,0:T(8,128)(2,1)S(1)} %get-tuple-element.412.refs_2_, ...), custom_call_target="tpu_custom_call" | custom-call | flops 5200936960 | bytes 11152384 | tf_op jit(solution)/shard_map/pallas_call | solution.py:263
  660.9 10.1 collective-permute-done.89
  694.2 9.7 collective-permute-done.93.refs_2_
  715.9 14.6 %shard_map.295 = (bf16[1024,832]{1,0:T(8,128)(2,1)S(1)}, f32[1,832]{1,0:T(1,128)S(1)}, f32[512,1600]{1,0:T(8,128)}, bf16[512,1664]{1,0:T(8,128)(2,1)S(1)}) custom-call(bf16[128,1664]{1,0:T(8,128)(2,1)S(1)} %copy-done.54, bf16[128,1664]{1,0:T(8,128)(2,1)S(1)} %copy-done.71, bf16[128,1664]{1,0:T(8,128)(2,1)} %collective-permute-done.93.refs_2_, ...), custom_call_target="tpu_custom_call" | custom-call | flops 5452595200 | bytes 17124608 | tf_op jit(solution)/shard_map/pallas_call | solution.py:263
  755.3 15.3 %collective-permute-done.145.refs_2_ = bf16[128,1664]{1,0:T(8,128)(2,1)S(1)} collective-permute-done((bf16[128,1664]{1,0:T(8,128)(2,1)S(1)}, bf16[128,1664]{1,0:T(8,128)(2,1)S(1)}, u32[]{:S(2)}, u32[]{:S(2)}) %collective-permute-start.145) | collective-permute-done | bytes 426016 | tf_op jit(solution)/shard_map/ppermute | solution.py:93
  801.5 17.1 %collective-permute-done.107 = bf16[256,256]{1,0:T(8,128)(2,1)S(1)} collective-permute-done((bf16[256,256]{1,0:T(8,128)(2,1)S(1)}, bf16[256,256]{1,0:T(8,128)(2,1)S(1)}, u32[]{:S(2)}, u32[]{:S(2)}) %collective-permute-start.107) | collective-permute-done | bytes 131104 | tf_op jit(solution)/shard_map/ppermute | solution.py:104
  830.7 20.2 %shard_map.300 = (bf16[1024,768]{1,0:T(8,128)(2,1)S(1)}, f32[1,768]{1,0:T(1,128)S(1)}, f32[512,1600]{1,0:T(8,128)}, bf16[512,1664]{1,0:T(8,128)(2,1)}) custom-call(bf16[128,256]{1,0:T(8,128)(2,1)S(1)} %get-tuple-element.362.refs_0_, bf16[128,256]{1,0:T(8,128)(2,1)S(1)} %get-tuple-element.408.refs_1_, bf16[128,256]{1,0:T(8,128)(2,1)S(1)} %get-tuple-element.406.refs_2_, ...), custom_call_target="tpu_custom_call" | custom-call | flops 5200936960 | bytes 11152384 | tf_op jit(solution)/shard_map/pallas_call | solution.py:263
  999.8 14.5 %collective-permute-start.122 = (f32[2,2,1280]{2,1,0:T(2,128)S(1)}, f32[2,2,1280]{2,1,0:T(2,128)S(1)}, u32[]{:S(2)}, u32[]{:S(2)}) collective-permute-start(f32[2,2,1280]{2,1,0:T(2,128)S(1)} %pad_maximum_fusion.35), channel_id=1, source_target_pairs={{0,4},{2,6},{4,0},{6,2},{1,5},{3,7},{5,1},{7,3},{8,12},{10,14},{12... | collective-permute-start | bytes 61448 | tf_op jit(solution)/shard_map/ppermute | solution.py:93
  1033.8 36.3 %reduce-scatter.21.cloned.1.call-done = bf16[1,208,1600]{2,1,0:T(8,128)(2,1)} async-done(((bf16[1,832,1600]{2,1,0:T(8,128)(2,1)}), bf16[1,208,1600]{2,1,0:T(8,128)(2,1)}) %reduce-scatter.21.cloned.1.call-update) | async-done | bytes 665616 | tf_op jit(solution)/shard_map/reduce_scatter | solution.py:256
  1070.1 10.2 collective-permute-start.164
  1101.6 10.6 collective-permute-done.159.refs_3_
  (1051 shorter events, 669.1 us)
Async XLA Ops:
  7.2 151.0 %all-gather.11.cloned.1.call-start = ((), (), s32[]{:S(2)}) async-start(), calls=%async_computation.9 | async-start | bytes 2129920 | tf_op jit(solution)/shard_map/all_gather | solution.py:251
  47.2 118.4 %all-gather.9.cloned.1.call-start = ((), (), s32[]{:S(2)}) async-start(), calls=%async_computation.8 | async-start | bytes 3072000 | tf_op jit(solution)/shard_map/all_gather | solution.py:251
  52.0 196.9 %all-gather.13.cloned.1.call-start = ((), (), s32[]{:S(2)}) async-start(), calls=%async_computation.10 | async-start | bytes 3584000 | tf_op jit(solution)/shard_map/all_gather | solution.py:251
  83.6 190.8 %all-gather.21.cloned.1.call-start = ((), (), s32[]{:S(2)}) async-start(), calls=%async_computation.22 | async-start | bytes 3461120 | tf_op jit(solution)/shard_map/all_gather | solution.py:250
  85.4 270.4 %all-gather.15.cloned.1.call-start = ((), (), s32[]{:S(2)}) async-start(), calls=%async_computation.11 | async-start | bytes 3072000 | tf_op jit(solution)/shard_map/all_gather | solution.py:251
  88.6 61.7 %collective-permute-start.12 = (bf16[128,1664]{1,0:T(8,128)(2,1)S(1)}, bf16[128,1664]{1,0:T(8,128)(2,1)S(1)}, u32[]{:S(2)}, u32[]{:S(2)}) collective-permute-start(bf16[128,1664]{1,0:T(8,128)(2,1)S(1)} %pad.89.refs_0_), channel_id=1, source_target_pairs={{0,1},{1,0},{2,3},{3,2},{4,5},{5,4},{6,7},{7,6},{8,9},{9,8},{10,11... | collective-permute-start | bytes 1277960 | tf_op jit(solution)/shard_map/ppermute | solution.py:96
  193.3 326.5 %all-gather.17.cloned.1.call-start = ((), (), s32[]{:S(2)}) async-start(), calls=%async_computation.12 | async-start | bytes 3584000 | tf_op jit(solution)/shard_map/all_gather | solution.py:251
  292.1 252.4 %all-gather.19.cloned.1.call-start = ((), (), s32[]{:S(2)}) async-start(), calls=%async_computation.13 | async-start | bytes 3461120 | tf_op jit(solution)/shard_map/all_gather | solution.py:251
  379.1 500.9 %reduce-scatter.23.cloned.1.call-start = ((), (), s32[]{:S(2)}) async-start(), calls=%async_computation.21 | async-start | bytes 3461120 | tf_op jit(solution)/shard_map/reduce_scatter | solution.py:256
  381.0 101.8 %collective-permute-start.73 = (bf16[128,1664]{1,0:T(8,128)(2,1)}, bf16[128,1664]{1,0:T(8,128)(2,1)}, u32[]{:S(2)}, u32[]{:S(2)}) collective-permute-start(bf16[128,1664]{1,0:T(8,128)(2,1)} %pad.107.refs_0_), channel_id=1, source_target_pairs={{0,1},{1,0},{2,3},{3,2},{4,5},{5,4},{6,7},{7,6},{8,9},{9,8},{10,11... | collective-permute-start | bytes 1277960 | tf_op jit(solution)/shard_map/ppermute | solution.py:96
  412.3 58.9 %collective-permute-start.58 = (bf16[256,1664]{1,0:T(8,128)(2,1)S(1)}, bf16[256,1664]{1,0:T(8,128)(2,1)S(1)}, u32[]{:S(2)}, u32[]{:S(2)}) collective-permute-start(bf16[256,1664]{1,0:T(8,128)(2,1)S(1)} %pad.104.refs_0_), channel_id=1, source_target_pairs={{0,1},{1,0},{2,3},{3,2},{4,5},{5,4},{6,7},{7,6},{8,9},{9,8},{10,11... | collective-permute-start | bytes 2555912 | tf_op jit(solution)/shard_map/ppermute | solution.py:96
  412.4 59.4 %collective-permute-start.59 = (bf16[256,1664]{1,0:T(8,128)(2,1)S(1)}, bf16[256,1664]{1,0:T(8,128)(2,1)S(1)}, u32[]{:S(2)}, u32[]{:S(2)}) collective-permute-start(bf16[256,1664]{1,0:T(8,128)(2,1)S(1)} %pad.104.refs_0_), channel_id=1, source_target_pairs={{0,4},{2,6},{4,0},{6,2},{1,5},{3,7},{5,1},{7,3},{8,12},{10,14},{12... | collective-permute-start | bytes 2555912 | tf_op jit(solution)/shard_map/ppermute | solution.py:93
  412.5 59.4 %collective-permute-start.60 = (bf16[256,1664]{1,0:T(8,128)(2,1)S(1)}, bf16[256,1664]{1,0:T(8,128)(2,1)S(1)}, u32[]{:S(2)}, u32[]{:S(2)}) collective-permute-start(bf16[256,1664]{1,0:T(8,128)(2,1)S(1)} %pad.104.refs_0_), channel_id=1, source_target_pairs={{0,5},{1,4},{2,7},{3,6},{4,1},{5,0},{6,3},{7,2},{8,13},{9,12},{10,... | collective-permute-start | bytes 2555912 | tf_op jit(solution)/shard_map/ppermute | solution.py:104
  544.2 337.4 %reduce-scatter.19.cloned.1.call-start = ((), (), s32[]{:S(2)}) async-start(), calls=%async_computation.19 | async-start | bytes 3584000 | tf_op jit(solution)/shard_map/reduce_scatter | solution.py:257
  607.0 280.2 %reduce-scatter.11.cloned.1.call-start = ((), (), s32[]{:S(2)}) async-start(), calls=%async_computation.15 | async-start | bytes 3072000 | tf_op jit(solution)/shard_map/reduce_scatter | solution.py:257
  710.9 194.8 %reduce-scatter.15.cloned.1.call-start = ((), (), s32[]{:S(2)}) async-start(), calls=%async_computation.17 | async-start | bytes 1064960 | tf_op jit(solution)/shard_map/reduce_scatter | solution.py:257
  793.9 183.5 %reduce-scatter.13.cloned.1.call-start = ((), (), s32[]{:S(2)}) async-start(), calls=%async_computation.16 | async-start | bytes 1064960 | tf_op jit(solution)/shard_map/reduce_scatter | solution.py:257
  859.9 156.0 %reduce-scatter.17.cloned.1.call-start = ((), (), s32[]{:S(2)}) async-start(), calls=%async_computation.18 | async-start | bytes 3584000 | tf_op jit(solution)/shard_map/reduce_scatter | solution.py:257
  869.9 160.6 %reduce-scatter.9.cloned.1.call-start = ((), (), s32[]{:S(2)}) async-start(), calls=%async_computation.14 | async-start | bytes 3072000 | tf_op jit(solution)/shard_map/reduce_scatter | solution.py:257
  870.5 199.6 %reduce-scatter.21.cloned.1.call-start = ((), (), s32[]{:S(2)}) async-start(), calls=%async_computation.20 | async-start | bytes 3461120 | tf_op jit(solution)/shard_map/reduce_scatter | solution.py:256
  879.9 67.2 %collective-permute-start.112 = (bf16[512,1664]{1,0:T(8,128)(2,1)}, bf16[512,1664]{1,0:T(8,128)(2,1)}, u32[]{:S(2)}, u32[]{:S(2)}) collective-permute-start(bf16[512,1664]{1,0:T(8,128)(2,1)} %get-tuple-element.186), channel_id=1, source_target_pairs={{0,2},{2,0},{4,6},{6,4},{1,3},{3,1},{5,7},{7,5},{8,10},{10,8},{12,... | collective-permute-start | bytes 5111816 | tf_op jit(solution)/shard_map/ppermute | solution.py:90
  1022.2 71.6 %collective-permute-start.116 = (bf16[128,1600]{1,0:T(8,128)(2,1)}, bf16[128,1600]{1,0:T(8,128)(2,1)}, u32[]{:S(2)}, u32[]{:S(2)}) collective-permute-start(bf16[128,1600]{1,0:T(8,128)(2,1)} %multiply_add_fusion), channel_id=1, source_target_pairs={{0,0},{9,1},{20,4},{29,5},{2,2},{11,3},{22,6},{31,7},{1,8},{8,9},{... | collective-permute-start | bytes 1228808 | tf_op jit(solution)/shard_map/ppermute | solution.py:87
  1028.2 65.7 %collective-permute-start.157 = (bf16[2,100,832]{2,1,0:T(8,128)(2,1)S(1)}, bf16[2,100,832]{2,1,0:T(8,128)(2,1)S(1)}, u32[]{:S(2)}, u32[]{:S(2)}) collective-permute-start(bf16[2,100,832]{2,1,0:T(8,128)(2,1)S(1)} %get-tuple-element.213.refs_0_), channel_id=1, source_target_pairs={{0,1},{1,0},{2,3},{3,2},{4,5},{5,4},{6,7},{7,6},{8,9},{9,8},{10,11... | collective-permute-start | bytes 998408 | tf_op jit(solution)/shard_map/ppermute | solution.py:96
  1028.4 68.4 %collective-permute-start.158 = (bf16[2,100,832]{2,1,0:T(8,128)(2,1)}, bf16[2,100,832]{2,1,0:T(8,128)(2,1)S(1)}, u32[]{:S(2)}, u32[]{:S(2)}) collective-permute-start(bf16[2,100,832]{2,1,0:T(8,128)(2,1)} %get-tuple-element.214), channel_id=1, source_target_pairs={{0,4},{2,6},{4,0},{6,2},{1,5},{3,7},{5,1},{7,3},{8,12},{10,14},{12... | collective-permute-start | bytes 998408 | tf_op jit(solution)/shard_map/ppermute | solution.py:93
  (325 other events, 4977.3 us)
Sparse Core Ops, SparseCore 0:
  47.3 39.1 all-gather.10
  88.6 68.3 all-gather.8
  159.1 57.2 all-gather.12
  218.4 55.9 all-gather.20
  275.8 50.6 all-gather.14
  328.5 83.0 all-gather.16
  413.1 57.1 all-gather.18
  544.4 53.2 reduce-scatter.22
  607.1 54.4 reduce-scatter.18
  711.0 46.8 reduce-scatter.10
  794.0 22.8 reduce-scatter.14
  860.0 22.7 reduce-scatter.12
  885.8 55.4 reduce-scatter.16
  943.4 49.4 reduce-scatter.8
  995.6 74.4 reduce-scatter.20
